TPU v7x, 256 devices: a whole 4x4x8 slice. The times are simulated.
256 devices in a mesh: buoy: 4 (over x), dom: 64 (over z, y, core).
Axes of the slice: x: 4, y: 4, z: 8, core: 2. Of those that a mesh axis runs over, the one named last changes fastest.
Arguments:
- ambient: float32 [32, 36, 448], P('buoy', None, 'dom'), may hold values from -6 to 6
- initial_out: float32 [32, 36, 448], P('buoy', None, 'dom'), may hold values from -6 to 6
- translation: bfloat16 [512, 448, 448], P(('buoy', 'dom')), may hold values from -0.0625 to 0.0625
- pair_source: int32 [512], P(('buoy', 'dom')), may hold values from 0 to 31, as said below
- pair_target: int32 [512], P(('buoy', 'dom')), may hold values from 0 to 31, as said below
- pair_live: int32 [512], P(('buoy', 'dom')), may hold values from 0 to 1, as said below
- diffract: bfloat16 [448, 448], P('dom'), may hold values from -0.25 to 0.25
- panel_rows: bfloat16 [8192, 448], P('dom'), may hold values from -0.25 to 0.25
Outputs:
- outgoing: float32 [32, 36, 448], P('buoy', None, 'dom')
- sources: bfloat16 [32, 36, 8192], P('buoy', None, 'dom')
Inputs may be any that keep to these rules, and one draw needn't show every extreme that they name: `pair_target`: the slots of one device name target buoys among the 8 buoys of its index of buoy. `pair_source`: A source buoy differs from its target by 1 to 8 places in the farm's order; the live slots of one target name distinct sources. `pair_live`: A slot is live exactly where its source lies inside the farm; some device has all 2 live.
All inputs are finite; a program needn't handle non-finite values.
Results may differ from a plain program's by a relative error of at most 0.015.
Values may be sent and summed in bfloat16 or wider, within the bound.
No kernel may reach another device: no remote copies, remote signals or barrier semaphores. Data moves between devices by JAX's collectives and lax.ppermute only.
A program may use at most 64 MiB of HBM per device.

v0:
```python
import jax
import jax.numpy as jnp
from jax import lax
from jax.sharding import PartitionSpec as P

ITERS = 2


def extended_2(block, sides, width):
    for axis, dim in sides:
        count = lax.axis_size(axis)
        forward = [(i, i + 1) for i in range(count - 1)]
        backward = [(target, source) for source, target in forward]
        low = lax.ppermute(
            lax.slice_in_dim(block, block.shape[dim] - width, None, axis=dim), axis, forward
        )
        high = lax.ppermute(lax.slice_in_dim(block, 0, width, axis=dim), axis, backward)
        block = jnp.concatenate([low, block, high], axis=dim)
    return block


def rows_product(left, right):
    return lax.dot_general(
        left, right, (((1,), (1,)), ((), ())), preferred_element_type=jnp.float32
    )


def shards(
    ambient, initial_out, translation, pair_source, pair_target, pair_live, diffract, panel_rows
):
    per_dev, headings, share_width = initial_out.shape
    full_width = translation.shape[1]
    first_buoy = lax.axis_index("buoy") * per_dev
    column_start = lax.axis_index("dom") * share_width
    rows_source = pair_source - (first_buoy - per_dev)
    rows_target = pair_target - first_buoy
    place_table = (
        (rows_target[None, :] == jnp.arange(per_dev, dtype=jnp.int32)[:, None])
        & (pair_live[None, :] == 1)
    ).astype(jnp.float32)
    matrices = translation.astype(jnp.float32)
    coeffs = initial_out
    incident_bf = None
    for step in range(ITERS):
        whole = lax.all_gather(coeffs, "dom", axis=2, tiled=True)
        extended = extended_2(whole.astype(jnp.bfloat16), (("buoy", 0),), per_dev).astype(
            whole.dtype
        )
        picked = jnp.take(extended, rows_source, axis=0)
        terms = jnp.einsum("phn,pmn->phm", picked, matrices, precision=lax.Precision.HIGHEST)
        partial_value = jnp.einsum(
            "kp,phm->khm", place_table, terms, precision=lax.Precision.HIGHEST
        )
        own_columns = (
            lax.dynamic_slice_in_dim(partial_value, column_start, share_width, 2) + ambient
        )
        partial_value = lax.dynamic_update_slice_in_dim(partial_value, own_columns, column_start, 2)
        incident = lax.psum(partial_value, "dom")
        incident_bf = incident.astype(jnp.bfloat16)
        flat = incident_bf.reshape(per_dev * headings, full_width)
        coeffs = rows_product(flat, diffract).reshape(per_dev, headings, share_width)
    flat = incident_bf.reshape(per_dev * headings, full_width)
    sources = (
        rows_product(flat, panel_rows)
        .astype(jnp.bfloat16)
        .reshape(per_dev, headings, panel_rows.shape[0])
    )
    return (coeffs, sources)


def solution(mesh):
    in_specs = (
        P("buoy", None, "dom"),
        P("buoy", None, "dom"),
        P(("buoy", "dom"), None, None),
        P(("buoy", "dom")),
        P(("buoy", "dom")),
        P(("buoy", "dom")),
        P("dom", None),
        P("dom", None),
    )
    out_specs = (P("buoy", None, "dom"), P("buoy", None, "dom"))
    return jax.shard_map(shards, mesh=mesh, in_specs=in_specs, out_specs=out_specs, check_vma=False)
```

profile of v0, /device:TPU:1, one launch (start us, length us, event | category | flops | bytes accessed | tf_op | source)
XLA Modules:
  0.0 653.7 jit_solution(17983448239093237719)
XLA Ops:
  0.7 0.8 convert.2
  1.5 55.3 %all_gather.6 = bf16[8,36,448]{1,0,2:T(8,128)(2,1)S(1)} all-gather(bf16[8,36,7]{1,0,2:T(8,128)(2,1)S(1)} %convert.2), channel_id=1, replica_groups=mesh['buoy'=4,'dom'=64] {'dom'}, dimensions={2}, use_global_device_ids=true | all-gather | bytes 262080 | tf_op jit(solution)/shard_map/all_gather | solution.py:45
  56.8 0.7 copy.70
  57.5 1.3 collective-permute-start.1
  58.8 4.7 collective-permute-start
  63.5 0.2 copy.72
  63.7 4.8 collective-permute-done.1
  68.5 0.7 copy-done.1
  69.4 1.3 maximum_convert_fusion
  70.7 0.6 gather_fusion
  71.2 0.9 fusion.4
  72.2 0.6 fusion.8
  72.9 5.4 dynamic_update_slice.6
  78.3 249.0 %all-reduce.2 = bf16[8,36,448]{2,0,1:T(8,128)(2,1)S(1)} all-reduce(f32[8,36,448]{2,0,1:T(8,128)S(1)} %dynamic_update_slice.6), channel_id=1, replica_groups=mesh['buoy'=4,'dom'=64] {'dom'}, use_global_device_ids=true, to_apply=%region_0.0 | all-reduce | flops 129024 | bytes 774144 | tf_op jit(solution)/shard_map/psum | solution.py:58
  327.3 0.3 fusion
  327.6 52.8 %all_gather.7 = bf16[8,36,448]{1,0,2:T(8,128)(2,1)S(1)} all-gather(bf16[8,36,7]{1,0,2:T(8,128)(2,1)S(1)} %copy.74), channel_id=1, replica_groups=mesh['buoy'=4,'dom'=64] {'dom'}, dimensions={2}, use_global_device_ids=true | all-gather | bytes 262080 | tf_op jit(solution)/shard_map/all_gather | solution.py:45
  380.4 0.9 copy.75
  381.4 1.3 collective-permute-start.3
  382.7 5.0 collective-permute-start.2
  387.7 5.1 collective-permute-done.3
  392.8 1.0 collective-permute-done.2
  393.7 0.2 maximum_convert_fusion.1
  394.0 1.0 copy.76
  395.0 0.6 gather_fusion.1
  395.6 0.9 fusion.2
  396.5 0.6 fusion.6
  397.2 5.4 dynamic_update_slice.7
  402.7 249.0 %all-reduce.3 = bf16[8,36,448]{2,0,1:T(8,128)(2,1)S(1)} all-reduce(f32[8,36,448]{2,0,1:T(8,128)S(1)} %dynamic_update_slice.7), channel_id=1, replica_groups=mesh['buoy'=4,'dom'=64] {'dom'}, use_global_device_ids=true, to_apply=%region_1.3 | all-reduce | flops 129024 | bytes 774144 | tf_op jit(solution)/shard_map/psum | solution.py:58
  651.7 0.3 fusion.14
  652.1 0.6 copy.81
  652.8 0.2 convolution_convert_fusion
  653.1 0.6 copy.82
  (26 shorter events, 0.6 us)
Async XLA Ops:
  0.6 70.6 %copy-start = (bf16[2,448,448]{2,1,0:T(8,128)(2,1)S(1)}, bf16[2,448,448]{2,1,0:T(8,128)(2,1)}, u32[]{:S(2)}) copy-start(bf16[2,448,448]{2,1,0:T(8,128)(2,1)} %param.12) | copy-start | bytes 2408452
  0.6 62.8 %copy-start.6 = (s32[2]{0:T(128)S(1)}, s32[2]{0:T(128)}, u32[]{:S(2)}) copy-start(s32[2]{0:T(128)} %param.14) | copy-start | bytes 28
  0.7 62.8 %copy-start.4 = (s32[2]{0:T(128)S(1)}, s32[2]{0:T(128)}, u32[]{:S(2)}) copy-start(s32[2]{0:T(128)} %param.13) | copy-start | bytes 28
  0.7 62.9 %copy-start.3 = (f32[8,36,7]{1,0,2:T(8,128)S(1)}, f32[8,36,7]{1,0,2:T(8,128)}, u32[]{:S(2)}) copy-start(f32[8,36,7]{1,0,2:T(8,128)} %param.10) | copy-start | bytes 24196
  0.7 63.0 %copy-start.7 = (s32[2]{0:T(128)S(1)}, s32[2]{0:T(128)}, u32[]{:S(2)}) copy-start(s32[2]{0:T(128)} %param.15) | copy-start | bytes 28
  57.5 11.0 %collective-permute-start.1 = (bf16[8,36,448]{2,1,0:T(8,128)(2,1)S(1)}, bf16[8,36,448]{2,1,0:T(8,128)(2,1)S(1)}, u32[]{:S(2)}, u32[]{:S(2)}) collective-permute-start(bf16[8,36,448]{2,1,0:T(8,128)(2,1)S(1)} %copy.70), channel_id=1, source_target_pairs={{64,0},{128,64},{192,128},{65,1},{129,65},{193,129},{66,2},{130,66... | collective-permute-start | bytes 774152 | tf_op jit(solution)/shard_map/ppermute | solution.py:17
  58.8 10.6 %collective-permute-start = (bf16[8,36,448]{2,1,0:T(8,128)(2,1)S(1)}, bf16[8,36,448]{2,1,0:T(8,128)(2,1)}, u32[]{:S(2)}, u32[]{:S(2)}) collective-permute-start(bf16[8,36,448]{2,1,0:T(8,128)(2,1)S(1)} %copy.70), channel_id=1, source_target_pairs={{0,64},{64,128},{128,192},{1,65},{65,129},{129,193},{2,66},{66,130... | collective-permute-start | bytes 774152 | tf_op jit(solution)/shard_map/ppermute | solution.py:14
  68.5 0.7 copy-start.1
  71.2 256.1 %copy-start.5 = (bf16[7,448]{1,0:T(8,128)(2,1)S(1)}, bf16[7,448]{1,0:T(8,128)(2,1)}, u32[]{:S(2)}) copy-start(bf16[7,448]{1,0:T(8,128)(2,1)} %param.16) | copy-start | bytes 18820
  381.4 11.4 %collective-permute-start.3 = (bf16[8,36,448]{2,0,1:T(8,128)(2,1)S(1)}, bf16[8,36,448]{2,0,1:T(8,128)(2,1)S(1)}, u32[]{:S(2)}, u32[]{:S(2)}) collective-permute-start(bf16[8,36,448]{2,0,1:T(8,128)(2,1)S(1)} %copy.75), channel_id=1, source_target_pairs={{64,0},{128,64},{192,128},{65,1},{129,65},{193,129},{66,2},{130,66... | collective-permute-start | bytes 774152 | tf_op jit(solution)/shard_map/ppermute | solution.py:17
  382.7 11.1 %collective-permute-start.2 = (bf16[8,36,448]{2,0,1:T(8,128)(2,1)S(1)}, bf16[8,36,448]{2,0,1:T(8,128)(2,1)S(1)}, u32[]{:S(2)}, u32[]{:S(2)}) collective-permute-start(bf16[8,36,448]{2,0,1:T(8,128)(2,1)S(1)} %copy.75), channel_id=1, source_target_pairs={{0,64},{64,128},{128,192},{1,65},{65,129},{129,193},{2,66},{66,130... | collective-permute-start | bytes 774152 | tf_op jit(solution)/shard_map/ppermute | solution.py:14
  397.1 255.7 %copy-start.2 = (bf16[128,448]{0,1:T(8,128)(2,1)S(1)}, bf16[128,448]{0,1:T(8,128)(2,1)}, u32[]{:S(2)}) copy-start(bf16[128,448]{0,1:T(8,128)(2,1)} %param.17) | copy-start | bytes 344068
where the time goes:
time: 659 us; the launch traced here: 654 us
  blocking collectives  606 us (92%)
  local copies, waits for them, and re-layouts  17 us (3%)
  starting transfers between devices  12.3 us (2%)
  waiting for transfers between devices  11 us (2%)
    psum x2, blocking collectives, shards(): incident = lax.psum(partial_value, 'dom')  498 us
    all_gather x2, blocking collectives, shards(): whole = lax.all_gather(coeffs, 'dom', axis=2, tiled=True)  108 us
  transfers between devices with their start and end apart: 4, of which 4 were waited for; matrix products, arithmetic and copies ran while one was open for 0% of the time, Pallas kernels for 0%

commit v1 on v0

v1 whole, which is shorter than its diff:
```python
import jax
import jax.numpy as jnp
from jax import lax
from jax.sharding import Mesh, PartitionSpec as P

ITERS = 2
Z, Y, C = 8, 4, 2
PLANE = ("z", "y")
F32, BF16 = jnp.float32, jnp.bfloat16


def dot(left, right, left_dim=1, right_dim=0):
    return lax.dot_general(
        left, right, (((left_dim,), (right_dim,)), ((), ())), preferred_element_type=F32
    )


def to_all(block):
    return lax.all_to_all(
        jnp.broadcast_to(block, (Z * Y,) + block.shape), PLANE, 0, 0, tiled=True
    )


def swapped(value):
    return lax.ppermute(value, "c", [(0, 1), (1, 0)])


def with_neighbours(field):
    count = lax.axis_size("x")
    up = [(i, (i + 1) % count) for i in range(count)]
    down = [(b, a) for a, b in up]
    return jnp.concatenate(
        [lax.ppermute(field, "x", up), field, lax.ppermute(field, "x", down)], axis=1
    )


def shards(
    ambient, initial_out, translation, pair_source, pair_target, pair_live, diffract, panel_rows
):
    per_dev, headings, share = initial_out.shape
    full = translation.shape[1]
    half = headings // C
    lanes = half * per_dev
    rows = share * C
    first_buoy = lax.axis_index("x") * per_dev
    core = lax.axis_index("c")

    tables = jnp.stack([pair_source - (first_buoy - per_dev), pair_target - first_buoy, pair_live])
    tables = jnp.concatenate([tables, swapped(tables)], axis=1)
    blocks = (translation, swapped(translation))
    slots = tables.shape[1]

    packed = jnp.concatenate(
        [
            initial_out.transpose(2, 1, 0).reshape(share, headings * per_dev),
            ambient.transpose(2, 1, 0).reshape(share, headings * per_dev),
            diffract.astype(F32),
        ],
        axis=1,
    )
    packed = lax.all_gather(packed, "c", axis=0, tiled=True)
    first = lax.dynamic_slice_in_dim(packed, core * lanes, lanes, 1).astype(BF16)
    own_ambient = lax.dynamic_slice_in_dim(packed, C * lanes + core * lanes, lanes, 1)
    message = jnp.concatenate([first, packed[:, 2 * C * lanes :].astype(BF16)], axis=1)
    everything = to_all(message).reshape(full, -1)
    coeffs = everything[:, :lanes]
    matrix = everything[:, lanes:]

    src = lax.broadcasted_iota(jnp.int32, (3, half, per_dev, slots, half, per_dev), 0) * per_dev
    src = src + lax.broadcasted_iota(jnp.int32, src.shape, 2)
    same = lax.broadcasted_iota(jnp.int32, src.shape, 1) == lax.broadcasted_iota(
        jnp.int32, src.shape, 4
    )
    tgt = lax.broadcasted_iota(jnp.int32, src.shape, 5)
    table = lambda i: tables[i][None, None, None, :, None, None]
    select = (same & (src == table(0)) & (tgt == table(1)) & (table(2) == 1)).astype(BF16)
    select = select.reshape(3 * lanes, slots * lanes)

    incident = None
    for step in range(ITERS):
        if step:
            coeffs = dot(matrix, incident).astype(BF16)
        picked = dot(with_neighbours(coeffs), select).astype(BF16)
        total = 0
        for i in range(slots):
            block = blocks[i // 2][i % 2]
            total = total + dot(block, picked[:, i * lanes : (i + 1) * lanes])
        parts = lax.all_to_all(
            total.astype(BF16).reshape(Z * Y, rows, lanes), PLANE, 0, 0, tiled=True
        )
        own = own_ambient + jnp.sum(parts.astype(F32), axis=0)
        incident = to_all(own.astype(BF16)).reshape(full, lanes)

    whole = lax.all_gather(incident, "c", axis=0, tiled=False)
    sources = lax.dot_general(
        whole, panel_rows, (((1,), (1,)), ((), ())), preferred_element_type=F32
    ).astype(BF16)
    sources = sources.reshape(headings, per_dev, panel_rows.shape[0]).transpose(1, 0, 2)
    outgoing = lax.dot_general(
        diffract, whole, (((1,), (1,)), ((), ())), preferred_element_type=F32
    )
    outgoing = outgoing.reshape(share, headings, per_dev).transpose(2, 1, 0)
    return outgoing, sources


def solution(mesh):
    fine = Mesh(mesh.devices.reshape(mesh.shape["buoy"], Z, Y, C), ("x", "z", "y", "c"))
    dom = ("z", "y", "c")
    in_specs = (
        P("x", None, dom),
        P("x", None, dom),
        P(("x",) + dom, None, None),
        P(("x",) + dom),
        P(("x",) + dom),
        P(("x",) + dom),
        P(dom, None),
        P(dom, None),
    )
    out_specs = (P("x", None, dom), P("x", None, dom))
    return jax.shard_map(shards, mesh=fine, in_specs=in_specs, out_specs=out_specs, check_vma=False)
```

time: 659 us -> 128 us (0.19)
  blocking collectives: 606 us -> 52.7 us
  waiting for transfers between devices: 11 us -> 36.4 us
  starting transfers between devices: 12.3 us -> 20.7 us
  local copies, waits for them, and re-layouts: 17 us -> 8.96 us
    psum x2 -> x0, blocking collectives: 498 us -> none  [shards(): incident = lax.psum(partial_value, 'dom')]
    all_gather x2, blocking collectives: 108 us -> 15.2 us  [the longest x1 10.4 us: shards(): whole = lax.all_gather(incident, 'c', axis=0, tiled=False)]
    all_to_all x0 -> x3, blocking collectives: none -> 37.6 us  [the longest x2 25 us: to_all(): lax.all_to_all(jnp.broadcast_to(block, (Z * Y,) + block.shape), PLANE, 0,...]
    all_to_all x0 -> x2, waiting for transfers between devices: none -> 26.4 us  [the longest x1 17 us: to_all(): lax.all_to_all(jnp.broadcast_to(block, (Z * Y,) + block.shape), PLANE, 0,...]
    all_to_all x0 -> x2, starting transfers between devices: none -> 15.8 us  [the longest x1 9.47 us: to_all(): lax.all_to_all(jnp.broadcast_to(block, (Z * Y,) + block.shape), PLANE, 0,...]
    dynamic_update_slice x2 -> x0, local copies, waits for them, and re-layouts: 10.9 us -> none  [shards(): lax.dynamic_update_slice_in_dim(partial_value, own_columns, column_start, 2)]
    ppermute x4 -> x6, starting transfers between devices: 12.3 us -> 4.92 us  [the longest x2 2.93 us: with_neighbours(): lax.ppermute(field, 'x', down)]
  transfers between devices with their start and end apart: 4 -> 8, of which waited for: 4 -> 7; matrix products, arithmetic and copies ran while one was open for 0% -> 2% of each run, Pallas kernels for 0% -> 0%
where the time goes in v1:
time: 128 us
  blocking collectives  52.7 us (41%)
  waiting for transfers between devices  36.4 us (28%)
  starting transfers between devices  20.7 us (16%)
  local copies, waits for them, and re-layouts  8.96 us (7%)
  matrix products  6.76 us (5%)
  other arithmetic  1.45 us (1%)
    all_to_all x2, blocking collectives, to_all(): lax.all_to_all(jnp.broadcast_to(block, (Z * Y,) + block.shape), PLANE, 0,...  25 us
    all_to_all x1, waiting for transfers between devices, to_all(): lax.all_to_all(jnp.broadcast_to(block, (Z * Y,) + block.shape), PLANE, 0,...  17 us
    all_to_all x1, blocking collectives, shards(): lax.all_to_all(total.astype(BF16).reshape(Z * Y, rows, lanes), PLANE, 0,...  12.6 us
    all_gather x1, blocking collectives, shards(): whole = lax.all_gather(incident, 'c', axis=0, tiled=False)  10.4 us
    all_to_all x1, starting transfers between devices, to_all(): lax.all_to_all(jnp.broadcast_to(block, (Z * Y,) + block.shape), PLANE, 0,...  9.47 us
    all_to_all x1, waiting for transfers between devices, shards(): lax.all_to_all(total.astype(BF16).reshape(Z * Y, rows, lanes), PLANE, 0,...  9.35 us
    all_to_all x1, starting transfers between devices, shards(): lax.all_to_all(total.astype(BF16).reshape(Z * Y, rows, lanes), PLANE, 0,...  6.3 us
    dot_general x11, matrix products, dot(): lax.dot_general(left, right, (((left_dim,), (right_dim,)), ((), ())), pre...  5.69 us
  transfers between devices with their start and end apart: 8, of which 7 were waited for; matrix products, arithmetic and copies ran while one was open for 2% of the time, Pallas kernels for 0%

profile of v1, /device:TPU:1, one launch (start us, length us, event | category | flops | bytes accessed | tf_op | source)
XLA Modules:
  0.0 128.0 jit_solution(13952701440856783112)
XLA Ops:
  0.7 0.7 convert_element_type.44
  1.4 0.9 copy.21
  2.4 0.9 copy.20
  3.4 4.7 %all-gather = f32[2,7,1024]{2,1,0:T(8,128)S(1)} all-gather(f32[1,7,1024]{2,1,0:T(8,128)S(1)} %maximum_bitcast_fusion), channel_id=1, replica_groups=mesh['x'=4,'z'=8,'y'=4,'c'=2] {'c'}, dimensions={0}, use_global_device_ids=true | all-gather | bytes 86016 | tf_op jit(solution)/shard_map/all_gather | solution.py:61
  8.5 0.9 broadcast_in_dim.9
  9.3 9.5 %all-to-all-start = ((bf16[32,14,592]{2,1,0:T(8,128)(2,1)}), bf16[32,14,592]{2,1,0:T(8,128)(2,1)S(1)}, u32[]{:S(2)}, u32[]{:S(2)}) async-start(bf16[32,14,592]{2,1,0:T(8,128)(2,1)} %broadcast_in_dim.9), calls=%async_computation | async-start | bytes 1310720 | tf_op jit(solution)/shard_map/all_to_all | solution.py:19
  18.9 0.7 collective-permute-start.2
  20.6 17.0 %all-to-all-done = bf16[32,14,592]{2,1,0:T(8,128)(2,1)S(1)} async-done(((bf16[32,14,592]{2,1,0:T(8,128)(2,1)}), bf16[32,14,592]{2,1,0:T(8,128)(2,1)S(1)}, u32[]{:S(2)}, u32[]{:S(2)}) %all-to-all-start) | async-done | bytes 530464 | tf_op jit(solution)/shard_map/all_to_all | solution.py:19
  37.9 2.6 %collective-permute-start.1 = (bf16[448,144]{1,0:T(8,128)(2,1)S(1)}, bf16[448,144]{1,0:T(8,128)(2,1)S(1)}, u32[]{:S(2)}, u32[]{:S(2)}) collective-permute-start(bf16[448,144]{1,0:T(8,128)(2,1)S(1)} %slice.79), channel_id=1, source_target_pairs={{64,0},{128,64},{192,128},{0,192},{65,1},{129,65},{193,129},{1,193... | collective-permute-start | bytes 387080 | tf_op jit(solution)/shard_map/ppermute | solution.py:33
  40.9 2.5 %collective-permute-done.1 = bf16[448,144]{1,0:T(8,128)(2,1)S(1)} collective-permute-done((bf16[448,144]{1,0:T(8,128)(2,1)S(1)}, bf16[448,144]{1,0:T(8,128)(2,1)S(1)}, u32[]{:S(2)}, u32[]{:S(2)}) %collective-permute-start.1) | collective-permute-done | bytes 129056 | tf_op jit(solution)/shard_map/ppermute | solution.py:33
  43.5 3.1 %collective-permute-done = bf16[448,144]{1,0:T(8,128)(2,1)S(1)} collective-permute-done((bf16[448,144]{1,0:T(8,128)(2,1)S(1)}, bf16[448,144]{1,0:T(8,128)(2,1)S(1)}, u32[]{:S(2)}, u32[]{:S(2)}) %collective-permute-start) | collective-permute-done | bytes 129056 | tf_op jit(solution)/shard_map/ppermute | solution.py:33
  46.6 0.9 convolution_convert_fusion.1
  47.8 0.5 convolution_add_fusion.3
  48.3 0.5 fusion.24
  48.8 0.5 fusion.4
  49.5 1.0 reshape.62
  50.5 6.3 %all-to-all-start.1 = ((bf16[32,2,1008]{2,1,0:T(2,128)(2,1)}), bf16[32,2,1008]{2,1,0:T(2,128)(2,1)S(1)}, u32[]{:S(2)}, u32[]{:S(2)}) async-start(bf16[32,2,1008]{2,1,0:T(2,128)(2,1)} %reshape.62), calls=%async_computation.1 | async-start | bytes 262144 | tf_op jit(solution)/shard_map/all_to_all | solution.py:88
  56.8 9.3 %all-to-all-done.1 = bf16[32,2,1008]{2,1,0:T(2,128)(2,1)S(1)} async-done(((bf16[32,2,1008]{2,1,0:T(2,128)(2,1)}), bf16[32,2,1008]{2,1,0:T(2,128)(2,1)S(1)}, u32[]{:S(2)}, u32[]{:S(2)}) %all-to-all-start.1) | async-done | bytes 129056 | tf_op jit(solution)/shard_map/all_to_all | solution.py:88
  67.0 12.6 %all_to_all.25 = bf16[32,2,1008]{2,1,0:T(2,128)(2,1)S(1)} all-to-all(bf16[32,2,1008]{2,1,0:T(2,128)(2,1)S(1)} %reshape.64), channel_id=1, replica_groups=mesh['x'=4,'z'=8,'y'=4,'c'=2] {'z','y'}, dimensions={0} | all-to-all | bytes 258048 | tf_op jit(solution)/shard_map/all_to_all | solution.py:19
  80.1 0.4 convolution_convert_fusion.2
  80.9 1.2 collective-permute-start.4
  82.1 2.5 %collective-permute-done.5 = bf16[448,144]{0,1:T(8,128)(2,1)S(1)} collective-permute-done((bf16[448,144]{0,1:T(8,128)(2,1)S(1)}, bf16[448,144]{0,1:T(8,128)(2,1)S(1)}, u32[]{:S(2)}, u32[]{:S(2)}) %collective-permute-start.5) | collective-permute-done | bytes 129056 | tf_op jit(solution)/shard_map/ppermute | solution.py:33
  84.6 1.5 %collective-permute-done.4 = bf16[448,144]{0,1:T(8,128)(2,1)S(1)} collective-permute-done((bf16[448,144]{0,1:T(8,128)(2,1)S(1)}, bf16[448,144]{0,1:T(8,128)(2,1)S(1)}, u32[]{:S(2)}, u32[]{:S(2)}) %collective-permute-start.4) | collective-permute-done | bytes 129056 | tf_op jit(solution)/shard_map/ppermute | solution.py:33
  86.2 0.7 convolution_convert_fusion
  87.2 0.5 convolution_add_fusion.1
  87.7 0.5 fusion.23
  88.2 0.5 fusion.5
  89.3 12.6 %all_to_all.26 = bf16[32,2,1008]{2,1,0:T(2,128)(2,1)S(1)} all-to-all(bf16[32,2,1008]{2,1,0:T(2,128)(2,1)S(1)} %reshape.66), channel_id=1, replica_groups=mesh['x'=4,'z'=8,'y'=4,'c'=2] {'z','y'}, dimensions={0} | all-to-all | bytes 258048 | tf_op jit(solution)/shard_map/all_to_all | solution.py:88
  102.7 12.4 %all_to_all.27 = bf16[32,2,1008]{2,1,0:T(2,128)(2,1)S(1)} all-to-all(bf16[32,2,1008]{2,1,0:T(2,128)(2,1)S(1)} %reshape.68), channel_id=1, replica_groups=mesh['x'=4,'z'=8,'y'=4,'c'=2] {'z','y'}, dimensions={0} | all-to-all | bytes 258048 | tf_op jit(solution)/shard_map/all_to_all | solution.py:19
  115.6 10.4 %all_gather.7 = bf16[2,448,144]{1,2,0:T(8,128)(2,1)S(1)} all-gather(bf16[1,448,144]{1,2,0:T(8,128)(2,1)S(1)} %copy.24), channel_id=1, replica_groups=mesh['x'=4,'z'=8,'y'=4,'c'=2] {'c'}, dimensions={0}, use_global_device_ids=true | all-gather | bytes 387072 | tf_op jit(solution)/shard_map/all_gather | solution.py:94
  126.2 0.9 convolution_convert_fusion.3
  127.2 0.7 copy.26
  (69 shorter events, 7.0 us)
Async XLA Ops:
  0.6 125.6 %copy-start = (bf16[128,448]{0,1:T(8,128)(2,1)S(1)}, bf16[128,448]{0,1:T(8,128)(2,1)}, u32[]{:S(2)}) copy-start(bf16[128,448]{0,1:T(8,128)(2,1)} %param.15) | copy-start | bytes 344068
  8.4 10.4 %copy-start.4 = (s32[2]{0:T(128)S(1)}, s32[2]{0:T(128)}, u32[]{:S(2)}) copy-start(s32[2]{0:T(128)} %param.12) | copy-start | bytes 28
  8.4 10.4 %copy-start.5 = (s32[2]{0:T(128)S(1)}, s32[2]{0:T(128)}, u32[]{:S(2)}) copy-start(s32[2]{0:T(128)} %param.11) | copy-start | bytes 28
  8.4 10.4 %copy-start.3 = (s32[2]{0:T(128)S(1)}, s32[2]{0:T(128)}, u32[]{:S(2)}) copy-start(s32[2]{0:T(128)} %param.13) | copy-start | bytes 28
  8.4 11.2 %copy-start.1 = (bf16[2,448,448]{2,1,0:T(8,128)(2,1)S(1)}, bf16[2,448,448]{2,1,0:T(8,128)(2,1)}, u32[]{:S(2)}) copy-start(bf16[2,448,448]{2,1,0:T(8,128)(2,1)} %param.10) | copy-start | bytes 2408452
  9.3 28.3 %all-to-all-start = ((bf16[32,14,592]{2,1,0:T(8,128)(2,1)}), bf16[32,14,592]{2,1,0:T(8,128)(2,1)S(1)}, u32[]{:S(2)}, u32[]{:S(2)}) async-start(bf16[32,14,592]{2,1,0:T(8,128)(2,1)} %broadcast_in_dim.9), calls=%async_computation | async-start | bytes 1310720 | tf_op jit(solution)/shard_map/all_to_all | solution.py:19
  18.9 1.5 %collective-permute-start.2 = (s32[3,2]{1,0:T(4,128)S(1)}, s32[3,2]{1,0:T(4,128)S(1)}, u32[]{:S(2)}, u32[]{:S(2)}) collective-permute-start(s32[3,2]{1,0:T(4,128)S(1)} %pad_add_fusion), channel_id=1, source_target_pairs={{0,1},{1,0},{2,3},{3,2},{4,5},{5,4},{6,7},{7,6},{8,9},{9,8},{10,11... | collective-permute-start | bytes 80 | tf_op jit(solution)/shard_map/ppermute | solution.py:25
  19.6 28.7 %collective-permute-start.3 = (bf16[2,448,448]{2,1,0:T(8,128)(2,1)S(1)}, bf16[2,448,448]{2,1,0:T(8,128)(2,1)S(1)}, u32[]{:S(2)}, u32[]{:S(2)}) collective-permute-start(bf16[2,448,448]{2,1,0:T(8,128)(2,1)S(1)} %copy-done.1), channel_id=1, source_target_pairs={{0,1},{1,0},{2,3},{3,2},{4,5},{5,4},{6,7},{7,6},{8,9},{9,8},{10,11... | collective-permute-start | bytes 2408456 | tf_op jit(solution)/shard_map/ppermute | solution.py:25
  37.9 5.5 %collective-permute-start.1 = (bf16[448,144]{1,0:T(8,128)(2,1)S(1)}, bf16[448,144]{1,0:T(8,128)(2,1)S(1)}, u32[]{:S(2)}, u32[]{:S(2)}) collective-permute-start(bf16[448,144]{1,0:T(8,128)(2,1)S(1)} %slice.79), channel_id=1, source_target_pairs={{64,0},{128,64},{192,128},{0,192},{65,1},{129,65},{193,129},{1,193... | collective-permute-start | bytes 387080 | tf_op jit(solution)/shard_map/ppermute | solution.py:33
  40.5 6.1 %collective-permute-start = (bf16[448,144]{1,0:T(8,128)(2,1)S(1)}, bf16[448,144]{1,0:T(8,128)(2,1)S(1)}, u32[]{:S(2)}, u32[]{:S(2)}) collective-permute-start(bf16[448,144]{1,0:T(8,128)(2,1)S(1)} %slice.79), channel_id=1, source_target_pairs={{0,64},{64,128},{128,192},{192,0},{1,65},{65,129},{129,193},{193,1... | collective-permute-start | bytes 387080 | tf_op jit(solution)/shard_map/ppermute | solution.py:33
  50.5 15.7 %all-to-all-start.1 = ((bf16[32,2,1008]{2,1,0:T(2,128)(2,1)}), bf16[32,2,1008]{2,1,0:T(2,128)(2,1)S(1)}, u32[]{:S(2)}, u32[]{:S(2)}) async-start(bf16[32,2,1008]{2,1,0:T(2,128)(2,1)} %reshape.62), calls=%async_computation.1 | async-start | bytes 262144 | tf_op jit(solution)/shard_map/all_to_all | solution.py:88
  80.6 4.1 %collective-permute-start.5 = (bf16[448,144]{0,1:T(8,128)(2,1)S(1)}, bf16[448,144]{0,1:T(8,128)(2,1)S(1)}, u32[]{:S(2)}, u32[]{:S(2)}) collective-permute-start(bf16[448,144]{0,1:T(8,128)(2,1)S(1)} %convolution_convert_fusion.2), channel_id=1, source_target_pairs={{64,0},{128,64},{192,128},{0,192},{65,1},{129,65},{193,129},{1,193... | collective-permute-start | bytes 387080 | tf_op jit(solution)/shard_map/ppermute | solution.py:33
  80.9 5.2 %collective-permute-start.4 = (bf16[448,144]{0,1:T(8,128)(2,1)S(1)}, bf16[448,144]{0,1:T(8,128)(2,1)S(1)}, u32[]{:S(2)}, u32[]{:S(2)}) collective-permute-start(bf16[448,144]{0,1:T(8,128)(2,1)S(1)} %convolution_convert_fusion.2), channel_id=1, source_target_pairs={{0,64},{64,128},{128,192},{192,0},{1,65},{65,129},{129,193},{193,1... | collective-permute-start | bytes 387080 | tf_op jit(solution)/shard_map/ppermute | solution.py:33
  115.0 11.0 %copy-start.2 = (bf16[7,448]{1,0:T(8,128)(2,1)S(1)}, bf16[7,448]{1,0:T(8,128)(2,1)}, u32[]{:S(2)}) copy-start(bf16[7,448]{1,0:T(8,128)(2,1)} %param.14) | copy-start | bytes 18820

commit v2 on v1

v2 whole, which is shorter than its diff:
```python
import functools

import jax
import jax.numpy as jnp
from jax import lax
from jax.experimental import pallas as pl
from jax.experimental.pallas import tpu as pltpu
from jax.sharding import Mesh, PartitionSpec as P

ITERS = 2
Z, Y, C = 8, 4, 2
PLANE = ("z", "y")
CHIPS = Z * Y
F32, BF16, I32 = jnp.float32, jnp.bfloat16, jnp.int32

BD, H, S, M = 8, 36, 7, 448
HC, R, BLK, L = H // C, S * C, 16, 256
LAN = HC * BD
ROWS = CHIPS * BLK
HALF = M // C
SOURCES = 3 * BD
EMPTY = SOURCES * BD


def iota(shape, dim):
    return lax.broadcasted_iota(I32, shape, dim)


def ones(cond):
    return jnp.where(cond, 1.0, 0.0).astype(BF16)


def dot(left, right, dims=(1, 0), exact=False):
    return lax.dot_general(
        left,
        right,
        (((dims[0],), (dims[1],)), ((), ())),
        preferred_element_type=F32,
        precision=lax.Precision.HIGHEST if exact else None,
    )


def shift(rows, cols, start, to, width):
    row, col = iota((rows, cols), 0), iota((rows, cols), 1)
    return ones((row - start == col - to) & (col >= to) & (col < to + width))


def padding():
    row, col = iota((ROWS, M), 0), iota((ROWS, M), 1)
    return ones((col == row - 2 * (row >> 4)) & ((row & 15) < R))


def packing():
    row, col = iota((M, ROWS), 0), iota((M, ROWS), 1)
    return ones((row == col - 2 * (col >> 4)) & ((col & 15) < R))


def chip_field(own, other, core, exact):
    kind = F32 if exact else BF16
    head, lane = iota((H, L), 0), iota((H, L), 1)
    spread = ones((head == core * HC + (lane >> 3)) & (lane < LAN)).astype(kind)
    row, lane = iota((S * BD, L), 0), iota((S * BD, L), 1)
    total = 0.0
    for value, place in ((own, core), (other, 1 - core)):
        wide = dot(value.reshape(S * BD, H).astype(kind), spread, exact=exact)
        wide = jnp.where((row & 7) == (lane & 7), wide, 0.0)
        to, col = iota((BLK, S * BD), 0), iota((BLK, S * BD), 1)
        gather = ones((col >> 3) == to - S * place).astype(kind)
        total = total + dot(gather, wide.astype(kind), exact=exact)
    return total


def send_kernel(scalars, own_ref, other_ref, t_ref, out_ref):
    field = chip_field(own_ref[...], other_ref[...], scalars[0], False)
    row, lane = iota((BLK, 128), 0), iota((BLK, 128), 1)
    frow, fcol = iota((L, 128), 0), iota((L, 128), 1)
    tail = dot(field.astype(BF16), ones(frow == 128 + (fcol & 15)))
    tail = jnp.where((lane >> 4) == (row & 7), tail, 0.0)
    to, col = iota((BLK, BLK), 0), iota((BLK, BLK), 1)
    tail = dot(ones((to == R + (col >> 3)) & (col < R)), tail.astype(BF16))
    block = jnp.where(row < R, field[:, :128], tail)
    corner = (
        dot(block.astype(BF16), shift(128, 128, 0, 64, 64)),
        jnp.where(lane >= 64, block, 0.0),
    )
    pad = padding()
    widen = shift(64, 128, 0, 0, 64)
    for p in range(2):
        number = jnp.where((row == BLK - 1) & (lane == 0), scalars[1 + p].astype(F32), 0.0)
        for q in range(3):
            part = dot(pad, t_ref[p, :, 128 * q : 128 * (q + 1)]).reshape(CHIPS, BLK, 128)
            if q == 0:
                part = part + number[None]
            at = 512 * p + 128 * q
            out_ref[:, :, at : at + 128] = part.astype(BF16)
        last = dot(t_ref[p, :, 384:M], widen).astype(BF16)
        part = dot(pad, last).reshape(CHIPS, BLK, 128) + corner[p][None]
        out_ref[:, :, 512 * p + 384 : 512 * p + 512] = part.astype(BF16)


def first_kernel(in_ref, out_ref):
    third = in_ref[:, :, 384:512].reshape(ROWS, 128)
    last = in_ref[:, :, 896:1024].reshape(ROWS, 128)
    row, lane = iota((ROWS, 128), 0), iota((ROWS, 128), 1)
    block = dot(third, shift(128, 128, 64, 0, 64)) + jnp.where(lane >= 64, last.astype(F32), 0.0)
    block = block.astype(BF16)
    to, col = iota((ROWS, ROWS), 0), iota((ROWS, ROWS), 1)
    tail = dot(ones(col == (to - (to & 15)) + R + ((to & 15) >> 3)), block)
    tail = jnp.where((lane >> 4) == (row & 7), tail, 0.0).astype(BF16)
    frow, fcol = iota((128, 128), 0), iota((128, 128), 1)
    tail = dot(tail, ones((fcol == (frow & 15)) & (fcol < 16))).astype(BF16)
    pack = packing()
    out_ref[:, :128] = dot(pack, block).astype(BF16)
    out_ref[:, 128:] = dot(pack, tail).astype(BF16)


def place_kernel(
    scalars, own_at, other_at, in_ref, other_ref, amb_ref, amb_other_ref, d_ref, w_ref, a_ref, dm_ref
):
    w_ref[...] = jnp.zeros_like(w_ref)
    for j in range(CHIPS):
        for p in range(2):
            w_ref[own_at[j, p]] = in_ref[j, :, 512 * p : 512 * (p + 1)]
            w_ref[other_at[j, p]] = other_ref[j, :, 512 * p : 512 * (p + 1)]
    a_ref[...] = chip_field(amb_ref[...], amb_other_ref[...], scalars[0], True)
    to, col = iota((BLK, S), 0), iota((BLK, S), 1)
    matrix = d_ref[...].astype(F32)
    halves = 0.0
    for k in range(2):
        half = dot(ones(to == col + S * k).astype(F32), matrix, exact=True)
        halves = halves + dot(half.astype(BF16), shift(M, L, HALF * k, 0, HALF))
    halves = halves.astype(BF16)
    dm_ref[:, :128] = dot(halves, shift(L, 128, 128, 32, HALF - 128)).astype(BF16)
    dm_ref[:, 128:] = halves[:, :128]


def incident_kernel(w_ref, low_ref, own_ref, high_ref, a_ref, *rest):
    out_ref = rest[-1]
    lane = iota((BD * BLK, L), 1)
    total = jnp.zeros((BD * BLK, L), F32)
    for g, field in enumerate((low_ref, own_ref, high_ref)):
        for b in range(BD):
            part = dot(w_ref[BD * g + b, :, :M], field[...])
            total = total + jnp.where((lane & 7) == b, part, 0.0)
    row, col = iota((L, L), 0), iota((L, L), 1)
    same = ones(((row >> 3) == (col >> 3)) & (row < LAN)).astype(F32)
    total = dot(total, same, exact=True)
    row, lane = iota((BLK, L), 0), iota((BLK, L), 1)
    mine = a_ref[...]
    for t in range(BD):
        mine = mine + jnp.where((lane & 7) == t, total[BLK * t : BLK * (t + 1)], 0.0)
    mine = jnp.where((row < R) & (lane < LAN), mine, 0.0)
    first, second = mine[:, :128], mine[:, 128:]
    if len(rest) == 2:
        second = second + rest[0][:, :128].astype(F32)
        third = rest[0][:, 128:]
        out_ref[:, :, 256:] = jnp.broadcast_to(third[None], (CHIPS, BLK, 128))
    out_ref[:, :, :128] = jnp.broadcast_to(first.astype(BF16)[None], (CHIPS, BLK, 128))
    out_ref[:, :, 128:256] = jnp.broadcast_to(second.astype(BF16)[None], (CHIPS, BLK, 128))


def coeffs_kernel(scalars, in_ref, other_ref, out_ref):
    core = scalars[0]
    lane = iota((ROWS, L), 1)
    field = jnp.where(lane < LAN, in_ref[:, :, :L].reshape(ROWS, L).astype(F32), 0.0).astype(BF16)
    field = dot(packing(), field).astype(BF16)
    back = shift(128, 128, 32, 0, HALF - 128)
    row, col = iota((M, ROWS), 0), iota((M, ROWS), 1)
    first = 14 * (col >> 4) + (col & 15)
    left, right = [0.0, 0.0], [0.0, 0.0]
    for ref, place in ((in_ref, core), (other_ref, 1 - core)):
        low = ref[:, :, 256:384].reshape(ROWS, 128)
        high = dot(ref[:, :, 128:256].reshape(ROWS, 128), back).astype(BF16)
        above = ones((row == first + S * place) & ((col & 15) < S))
        below = ones((row == first - S + S * place) & ((col & 15) >= S) & ((col & 15) < R))
        for i, part in enumerate((low, high)):
            left[i] = left[i] + dot(above, part)
            right[i] = right[i] + dot(below, part)
    rest = HALF - 128
    total = dot(left[0].astype(BF16), field[:128])
    total = total + dot(left[1].astype(BF16)[:, :rest], field[128:HALF])
    total = total + dot(right[0].astype(BF16), field[HALF : HALF + 128])
    total = total + dot(right[1].astype(BF16)[:, :rest], field[HALF + 128 :])
    out_ref[...] = total.astype(BF16)


def last_kernel(in_ref, p_ref, d_ref, src_ref, out_ref):
    panels = dot(padding(), p_ref[...]).astype(BF16)
    matrix = dot(d_ref[...], packing()).astype(BF16)
    out = 0.0
    for c in range(C):
        field = in_ref[c].reshape(ROWS, L)
        part = dot(field, panels, dims=(0, 0))
        src_ref[LAN * c : LAN * (c + 1), :] = part[:LAN].astype(BF16)
        row, col = iota((L, BD * 128), 0), iota((L, BD * 128), 1)
        to = (row & 7) * 128 + (row >> 3) + HC * c
        wide = dot(field, ones((col == to) & (row < LAN))).astype(BF16)
        out = out + dot(matrix, wide)
    for b in range(BD):
        out_ref[:, b, :] = out[:, 128 * b : 128 * b + H]


VM = pl.BlockSpec(memory_space=pltpu.VMEM)
SM = pl.BlockSpec(memory_space=pltpu.SMEM)


def call(kernel, scalars, arrays, shapes, name):
    return pl.pallas_call(
        kernel,
        out_shape=shapes,
        in_specs=[SM] * len(scalars) + [VM] * len(arrays),
        out_specs=[VM] * len(shapes) if isinstance(shapes, tuple) else VM,
        compiler_params=pltpu.CompilerParams(vmem_limit_bytes=40 << 20),
        name=name,
    )(*scalars, *arrays)


def shape(*dims, dtype=BF16):
    return jax.ShapeDtypeStruct(dims, dtype)


def exchange(blocks):
    return lax.all_to_all(blocks, PLANE, 0, 0, tiled=True)


def swapped(value):
    return lax.ppermute(value, "c", [(0, 1), (1, 0)])


def with_neighbours(field):
    count = lax.axis_size("x")
    up = [(i, (i + 1) % count) for i in range(count)]
    down = [(b, a) for a, b in up]
    return lax.ppermute(field, "x", up), field, lax.ppermute(field, "x", down)


def slot_numbers(blocks):
    return jnp.stack([blocks[:, BLK - 1, 0], blocks[:, BLK - 1, 512]], axis=1).astype(I32)


def shards(
    ambient, initial_out, translation, pair_source, pair_target, pair_live, diffract, panel_rows
):
    first_buoy = lax.axis_index("x") * BD
    core = lax.axis_index("c")
    at = (pair_source - first_buoy + BD) * BD + pair_target - first_buoy
    at = jnp.where(pair_live == 1, jnp.clip(at, 0, EMPTY), EMPTY)
    scalars = jnp.concatenate([core[None], at]).astype(I32)

    begin = initial_out.transpose(2, 0, 1)
    waves = ambient.transpose(2, 0, 1)
    message = call(
        send_kernel,
        (scalars,),
        (begin, swapped(begin), translation),
        shape(CHIPS, BLK, 1024),
        "send",
    )
    got = exchange(message)
    got, waves, diffract, panel_rows = lax.optimization_barrier((got, waves, diffract, panel_rows))
    coeffs = call(first_kernel, (), (got,), shape(M, L), "first")
    around = with_neighbours(coeffs)
    got_other = swapped(got)
    matrices, own_waves, rows = call(
        place_kernel,
        (scalars, slot_numbers(got), slot_numbers(got_other)),
        (got, got_other, waves, swapped(waves), diffract),
        (shape(EMPTY + BD, BLK, 512), shape(BLK, L, dtype=F32), shape(BLK, L)),
        "place",
    )
    matrices = matrices.reshape(SOURCES + 1, BD * BLK, 512)

    message = call(
        incident_kernel,
        (),
        (matrices, *around, own_waves, rows),
        shape(CHIPS, BLK, 384),
        "incident_first",
    )
    got = exchange(message)
    coeffs = call(coeffs_kernel, (scalars,), (got, swapped(got)), shape(M, L), "coeffs")
    message = call(
        incident_kernel,
        (),
        (matrices, *with_neighbours(coeffs), own_waves),
        shape(CHIPS, BLK, L),
        "incident_last",
    )
    whole = lax.all_gather(exchange(message), "c", axis=0, tiled=False)
    sources, outgoing = call(
        last_kernel,
        (),
        (whole, panel_rows.T, diffract),
        (shape(H * BD, panel_rows.shape[0]), shape(S, BD, H, dtype=F32)),
        "last",
    )
    sources = sources.reshape(H, BD, panel_rows.shape[0]).transpose(1, 0, 2)
    return outgoing.transpose(1, 2, 0), sources


def solution(mesh):
    fine = Mesh(mesh.devices.reshape(mesh.shape["buoy"], Z, Y, C), ("x", "z", "y", "c"))
    dom = ("z", "y", "c")
    in_specs = (
        P("x", None, dom),
        P("x", None, dom),
        P(("x",) + dom, None, None),
        P(("x",) + dom),
        P(("x",) + dom),
        P(("x",) + dom),
        P(dom, None),
        P(dom, None),
    )
    out_specs = (P("x", None, dom), P("x", None, dom))
    return jax.shard_map(shards, mesh=fine, in_specs=in_specs, out_specs=out_specs, check_vma=False)
```

time: 128 us -> 115 us (0.90)
  waiting for transfers between devices: 36.4 us -> 9.32 us
  blocking collectives: 52.7 us -> 74 us
  Pallas kernels: 0 us -> 12.7 us
  matrix products: 6.76 us -> 0 us
  starting transfers between devices: 20.7 us -> 14.5 us
  local copies, waits for them, and re-layouts: 8.96 us -> 2.77 us
    all_to_all x3, blocking collectives: 37.6 us -> 68.9 us  [exchange(): return lax.all_to_all(blocks, PLANE, 0, 0, tiled=True)]
    all_to_all x2 -> x0, waiting for transfers between devices: 26.4 us -> none  [the longest x1 17 us: to_all(): lax.all_to_all(jnp.broadcast_to(block, (Z * Y,) + block.shape), PLANE, 0,...]
    all_to_all x2 -> x0, starting transfers between devices: 15.8 us -> none  [the longest x1 9.47 us: to_all(): lax.all_to_all(jnp.broadcast_to(block, (Z * Y,) + block.shape), PLANE, 0,...]
    pallas_call x0 -> x7, Pallas kernels: none -> 12.7 us  [call(): pl.pallas_call(kernel, out_shape=shapes, in_specs=[SM] * len(scalars) + [...]
    all_gather x2 -> x1, blocking collectives: 15.2 us -> 5.13 us  [shards(): whole = lax.all_gather(exchange(message), 'c', axis=0, tiled=False)]
    ppermute x2 -> x4, starting transfers between devices: 0.82 us -> 8.98 us  [swapped(): return lax.ppermute(value, 'c', [(0, 1), (1, 0)])]
    dot_general x13 -> x0, matrix products: 6.76 us -> none  [the longest x11 5.69 us: dot(): lax.dot_general(left, right, (((left_dim,), (right_dim,)), ((), ())), pre...]
    ppermute x4, waiting for transfers between devices: 9.66 us -> 7.26 us  [with_neighbours(): return (lax.ppermute(field, 'x', up), field, lax.ppermute(field, 'x', down))]
  transfers between devices with their start and end apart: 8 -> 8, of which waited for: 7 -> 5; matrix products, arithmetic and copies ran while one was open for 2% -> 1% of each run, Pallas kernels for 0% -> 2%
where the time goes in v2:
time: 115 us
  blocking collectives  74 us (64%)
  starting transfers between devices  14.5 us (13%)
  Pallas kernels  12.7 us (11%)
  waiting for transfers between devices  9.32 us (8%)
  local copies, waits for them, and re-layouts  2.77 us (2%)
    all_to_all x3, blocking collectives, exchange(): return lax.all_to_all(blocks, PLANE, 0, 0, tiled=True)  68.9 us
    pallas_call x7, Pallas kernels, call(): pl.pallas_call(kernel, out_shape=shapes, in_specs=[SM] * len(scalars) + [...  12.7 us
    ppermute x4, starting transfers between devices, swapped(): return lax.ppermute(value, 'c', [(0, 1), (1, 0)])  8.98 us
    ppermute x4, waiting for transfers between devices, with_neighbours(): return (lax.ppermute(field, 'x', up), field, lax.ppermute(field, 'x', down))  7.26 us
    ppermute x4, starting transfers between devices, with_neighbours(): return (lax.ppermute(field, 'x', up), field, lax.ppermute(field, 'x', down))  5.54 us
    all_gather x1, blocking collectives, shards(): whole = lax.all_gather(exchange(message), 'c', axis=0, tiled=False)  5.13 us
  transfers between devices with their start and end apart: 8, of which 5 were waited for; matrix products, arithmetic and copies ran while one was open for 1% of the time, Pallas kernels for 2%

profile of v2, /device:TPU:1, one launch (start us, length us, event | category | flops | bytes accessed | tf_op | source)
XLA Modules:
  0.0 114.8 jit_solution(13757303815223988420)
XLA Ops:
  0.6 3.3 %collective-permute-start = (f32[7,8,36]{2,1,0:T(8,128)}, f32[7,8,36]{2,1,0:T(8,128)S(1)}, u32[]{:S(2)}, u32[]{:S(2)}) collective-permute-start(f32[7,8,36]{2,1,0:T(8,128)} %bitcast.18), channel_id=1, source_target_pairs={{0,1},{1,0},{2,3},{3,2},{4,5},{5,4},{6,7},{7,6},{8,9},{9,8},{10,11... | collective-permute-start | bytes 24200 | tf_op jit(solution)/shard_map/ppermute | solution.py:227
  4.0 0.7 compare_select_fusion
  4.7 0.1 pad_add_fusion.scalars
  4.7 0.3 collective-permute-done.other_ref
  5.0 1.2 %copy-done = bf16[2,448,448]{2,1,0:T(8,128)(2,1)S(1)} copy-done((bf16[2,448,448]{2,1,0:T(8,128)(2,1)S(1)}, bf16[2,448,448]{2,1,0:T(8,128)(2,1)}, u32[]{:S(2)}) %copy-start) | copy-done | bytes 802840
  6.2 0.7 copy-done.3
  7.0 2.7 %send.1 = bf16[32,16,1024]{2,1,0:T(8,128)(2,1)S(1)} custom-call(s32[3]{0:T(128)S(1)} %pad_add_fusion.scalars, f32[7,8,36]{2,1,0:T(8,128)S(1)} %bitcast.19, f32[7,8,36]{2,1,0:T(8,128)S(1)} %collective-permute-done.other_ref, bf16[2,448,448]{2,1,0:T(8,128)(2,1)S(1)} %copy-done), custom_call_target="tpu_custom_call" | custom-call | tf_op jit(solution)/shard_map/send/pallas_call | solution.py:208
  9.6 35.7 %all_to_all.15.in_ref = bf16[32,16,1024]{2,1,0:T(8,128)(2,1)S(1)} all-to-all(bf16[32,16,1024]{2,1,0:T(8,128)(2,1)S(1)} %send.1), channel_id=1, replica_groups=mesh['x'=4,'z'=8,'y'=4,'c'=2] {'z','y'}, dimensions={0} | all-to-all | bytes 2097152 | tf_op jit(solution)/shard_map/all_to_all | solution.py:223
  45.3 2.6 %collective-permute-start.1 = (bf16[32,16,1024]{2,1,0:T(8,128)(2,1)S(1)}, bf16[32,16,1024]{2,1,0:T(8,128)(2,1)S(1)}, u32[]{:S(2)}, u32[]{:S(2)}) collective-permute-start(bf16[32,16,1024]{2,1,0:T(8,128)(2,1)S(1)} %all_to_all.15.in_ref), channel_id=1, source_target_pairs={{0,1},{1,0},{2,3},{3,2},{4,5},{5,4},{6,7},{7,6},{8,9},{9,8},{10,11... | collective-permute-start | bytes 3145736 | tf_op jit(solution)/shard_map/ppermute | solution.py:227
  47.9 0.9 first.1.own_ref
  48.8 1.3 %collective-permute-start.3 = (bf16[448,256]{1,0:T(8,128)(2,1)S(1)}, bf16[448,256]{1,0:T(8,128)(2,1)S(1)}, u32[]{:S(2)}, u32[]{:S(2)}) collective-permute-start(bf16[448,256]{1,0:T(8,128)(2,1)S(1)} %first.1.own_ref), channel_id=1, source_target_pairs={{0,64},{64,128},{128,192},{192,0},{1,65},{65,129},{129,193},{193,1... | collective-permute-start | bytes 688136 | tf_op jit(solution)/shard_map/ppermute | solution.py:234
  50.1 1.5 %collective-permute-start.4 = (bf16[448,256]{1,0:T(8,128)(2,1)S(1)}, bf16[448,256]{1,0:T(8,128)(2,1)S(1)}, u32[]{:S(2)}, u32[]{:S(2)}) collective-permute-start(bf16[448,256]{1,0:T(8,128)(2,1)S(1)} %first.1.own_ref), channel_id=1, source_target_pairs={{64,0},{128,64},{192,128},{0,192},{65,1},{129,65},{193,129},{1,193... | collective-permute-start | bytes 688136 | tf_op jit(solution)/shard_map/ppermute | solution.py:234
  51.6 0.3 slice_reduce_fusion.3
  51.9 0.1 copy.20.own_at
  52.0 0.6 collective-permute-start.2
  52.6 0.3 slice_reduce_fusion.1
  52.9 0.1 copy.21.other_at
  53.0 0.4 collective-permute-done.2.amb_other_ref
  53.5 1.9 %place.1 = (bf16[200,16,512]{2,1,0:T(8,128)(2,1)S(1)}, f32[16,256]{1,0:T(8,128)S(1)}, bf16[16,256]{1,0:T(8,128)(2,1)S(1)}) custom-call(s32[3]{0:T(128)S(1)} %pad_add_fusion.scalars, s32[32,2]{1,0:T(8,128)S(1)} %copy.20.own_at, s32[32,2]{1,0:T(8,128)S(1)} %copy.21.other_at, bf16[32,16,1024]{2,1,0:T(8,128)(2,1)S(1)} %all_to_all.15.in_ref, ...), custom_call_target="tpu_custom_call" | custom-call | tf_op jit(solution)/shard_map/place/pallas_call | solution.py:208
  55.4 1.9 %collective-permute-done.3.low_ref = bf16[448,256]{1,0:T(8,128)(2,1)S(1)} collective-permute-done((bf16[448,256]{1,0:T(8,128)(2,1)S(1)}, bf16[448,256]{1,0:T(8,128)(2,1)S(1)}, u32[]{:S(2)}, u32[]{:S(2)}) %collective-permute-start.3) | collective-permute-done | bytes 229408 | tf_op jit(solution)/shard_map/ppermute | solution.py:234
  57.3 1.4 %incident_first.1 = bf16[32,16,384]{2,1,0:T(8,128)(2,1)S(1)} custom-call(bf16[25,128,512]{2,1,0:T(8,128)(2,1)S(1)} %bitcast.14, bf16[448,256]{1,0:T(8,128)(2,1)S(1)} %collective-permute-done.3.low_ref, bf16[448,256]{1,0:T(8,128)(2,1)S(1)} %first.1.own_ref, bf16[448,256]{1,0:T(8,128)(2,1)S(1)} %collective-permute-done.4.high_ref, ...), custom_call_target="tpu_custom_call" | custom-call | tf_op jit(solution)/shard_map/incident_first/pallas_call | solution.py:208
  58.8 19.0 %all_to_all.16.in_ref = bf16[32,16,384]{2,1,0:T(8,128)(2,1)S(1)} all-to-all(bf16[32,16,384]{2,1,0:T(8,128)(2,1)S(1)} %incident_first.1), channel_id=1, replica_groups=mesh['x'=4,'z'=8,'y'=4,'c'=2] {'z','y'}, dimensions={0} | all-to-all | bytes 786432 | tf_op jit(solution)/shard_map/all_to_all | solution.py:223
  77.8 2.5 %collective-permute-start.5 = (bf16[32,16,384]{2,1,0:T(8,128)(2,1)S(1)}, bf16[32,16,384]{2,1,0:T(8,128)(2,1)S(1)}, u32[]{:S(2)}, u32[]{:S(2)}) collective-permute-start(bf16[32,16,384]{2,1,0:T(8,128)(2,1)S(1)} %all_to_all.16.in_ref), channel_id=1, source_target_pairs={{0,1},{1,0},{2,3},{3,2},{4,5},{5,4},{6,7},{7,6},{8,9},{9,8},{10,11... | collective-permute-start | bytes 1179656 | tf_op jit(solution)/shard_map/ppermute | solution.py:227
  80.2 1.3 %collective-permute-done.5.other_ref = bf16[32,16,384]{2,1,0:T(8,128)(2,1)S(1)} collective-permute-done((bf16[32,16,384]{2,1,0:T(8,128)(2,1)S(1)}, bf16[32,16,384]{2,1,0:T(8,128)(2,1)S(1)}, u32[]{:S(2)}, u32[]{:S(2)}) %collective-permute-start.5) | collective-permute-done | bytes 393248 | tf_op jit(solution)/shard_map/ppermute | solution.py:227
  81.6 2.2 %coeffs.1.own_ref = bf16[448,256]{1,0:T(8,128)(2,1)S(1)} custom-call(s32[3]{0:T(128)S(1)} %pad_add_fusion.scalars, bf16[32,16,384]{2,1,0:T(8,128)(2,1)S(1)} %all_to_all.16.in_ref, bf16[32,16,384]{2,1,0:T(8,128)(2,1)S(1)} %collective-permute-done.5.other_ref), custom_call_target="tpu_custom_call" | custom-call | tf_op jit(solution)/shard_map/coeffs/pallas_call | solution.py:208
  83.8 1.0 collective-permute-start.6
  84.8 1.7 %collective-permute-start.7 = (bf16[448,256]{1,0:T(8,128)(2,1)S(1)}, bf16[448,256]{1,0:T(8,128)(2,1)S(1)}, u32[]{:S(2)}, u32[]{:S(2)}) collective-permute-start(bf16[448,256]{1,0:T(8,128)(2,1)S(1)} %coeffs.1.own_ref), channel_id=1, source_target_pairs={{64,0},{128,64},{192,128},{0,192},{65,1},{129,65},{193,129},{1,193... | collective-permute-start | bytes 688136 | tf_op jit(solution)/shard_map/ppermute | solution.py:234
  86.6 5.3 %collective-permute-done.6.low_ref = bf16[448,256]{1,0:T(8,128)(2,1)S(1)} collective-permute-done((bf16[448,256]{1,0:T(8,128)(2,1)S(1)}, bf16[448,256]{1,0:T(8,128)(2,1)S(1)}, u32[]{:S(2)}, u32[]{:S(2)}) %collective-permute-start.6) | collective-permute-done | bytes 229408 | tf_op jit(solution)/shard_map/ppermute | solution.py:234
  91.9 1.4 %incident_last.1 = bf16[32,16,256]{2,1,0:T(8,128)(2,1)S(1)} custom-call(bf16[25,128,512]{2,1,0:T(8,128)(2,1)S(1)} %bitcast.15, bf16[448,256]{1,0:T(8,128)(2,1)S(1)} %collective-permute-done.6.low_ref, bf16[448,256]{1,0:T(8,128)(2,1)S(1)} %coeffs.1.own_ref, bf16[448,256]{1,0:T(8,128)(2,1)S(1)} %collective-permute-done.7.high_ref, ...), custom_call_target="tpu_custom_call" | custom-call | tf_op jit(solution)/shard_map/incident_last/pallas_call | solution.py:208
  93.3 14.2 %all_to_all.17 = bf16[32,16,256]{2,1,0:T(8,128)(2,1)S(1)} all-to-all(bf16[32,16,256]{2,1,0:T(8,128)(2,1)S(1)} %incident_last.1), channel_id=1, replica_groups=mesh['x'=4,'z'=8,'y'=4,'c'=2] {'z','y'}, dimensions={0} | all-to-all | bytes 524288 | tf_op jit(solution)/shard_map/all_to_all | solution.py:223
  107.6 5.1 %all-gather = bf16[64,16,256]{2,1,0:T(8,128)(2,1)S(1)} all-gather(bf16[32,16,256]{2,1,0:T(8,128)(2,1)S(1)} %all_to_all.17), channel_id=2, replica_groups=mesh['x'=4,'z'=8,'y'=4,'c'=2] {'c'}, dimensions={0}, use_global_device_ids=true | all-gather | bytes 786432 | tf_op jit(solution)/shard_map/all_gather | solution.py:289
  112.7 2.1 %last.1 = (bf16[288,128]{1,0:T(8,128)(2,1)}, f32[7,8,36]{2,1,0:T(8,128)}) custom-call(bf16[2,32,16,256]{3,2,1,0:T(8,128)(2,1)S(1)} %bitcast.16, bf16[448,128]{1,0:T(8,128)(2,1)S(1)} %bitcast.17, bf16[7,448]{1,0:T(8,128)(2,1)S(1)} %copy-done.2), custom_call_target="tpu_custom_call" | custom-call | tf_op jit(solution)/shard_map/last/pallas_call | solution.py:208
  (13 shorter events, 0.0 us)
Async XLA Ops:
  0.6 52.8 %copy-start.2 = (bf16[7,448]{1,0:T(8,128)(2,1)S(1)}, bf16[7,448]{1,0:T(8,128)(2,1)}, u32[]{:S(2)}) copy-start(bf16[7,448]{1,0:T(8,128)(2,1)} %d_ref.1) | copy-start | bytes 18820
  0.6 4.4 %collective-permute-start = (f32[7,8,36]{2,1,0:T(8,128)}, f32[7,8,36]{2,1,0:T(8,128)S(1)}, u32[]{:S(2)}, u32[]{:S(2)}) collective-permute-start(f32[7,8,36]{2,1,0:T(8,128)} %bitcast.18), channel_id=1, source_target_pairs={{0,1},{1,0},{2,3},{3,2},{4,5},{5,4},{6,7},{7,6},{8,9},{9,8},{10,11... | collective-permute-start | bytes 24200 | tf_op jit(solution)/shard_map/ppermute | solution.py:227
  5.0 1.2 %copy-start = (bf16[2,448,448]{2,1,0:T(8,128)(2,1)S(1)}, bf16[2,448,448]{2,1,0:T(8,128)(2,1)}, u32[]{:S(2)}) copy-start(bf16[2,448,448]{2,1,0:T(8,128)(2,1)} %t_ref.1) | copy-start | bytes 2408452
  6.2 0.7 copy-start.3
  7.0 45.0 %copy-start.4 = (f32[8,36,7]{1,0,2:T(8,128)S(1)}, f32[8,36,7]{1,0,2:T(8,128)}, u32[]{:S(2)}) copy-start(f32[8,36,7]{1,0,2:T(8,128)} %param.8) | copy-start | bytes 24196
  45.3 7.3 %collective-permute-start.1 = (bf16[32,16,1024]{2,1,0:T(8,128)(2,1)S(1)}, bf16[32,16,1024]{2,1,0:T(8,128)(2,1)S(1)}, u32[]{:S(2)}, u32[]{:S(2)}) collective-permute-start(bf16[32,16,1024]{2,1,0:T(8,128)(2,1)S(1)} %all_to_all.15.in_ref), channel_id=1, source_target_pairs={{0,1},{1,0},{2,3},{3,2},{4,5},{5,4},{6,7},{7,6},{8,9},{9,8},{10,11... | collective-permute-start | bytes 3145736 | tf_op jit(solution)/shard_map/ppermute | solution.py:227
  48.8 8.5 %collective-permute-start.3 = (bf16[448,256]{1,0:T(8,128)(2,1)S(1)}, bf16[448,256]{1,0:T(8,128)(2,1)S(1)}, u32[]{:S(2)}, u32[]{:S(2)}) collective-permute-start(bf16[448,256]{1,0:T(8,128)(2,1)S(1)} %first.1.own_ref), channel_id=1, source_target_pairs={{0,64},{64,128},{128,192},{192,0},{1,65},{65,129},{129,193},{193,1... | collective-permute-start | bytes 688136 | tf_op jit(solution)/shard_map/ppermute | solution.py:234
  50.1 7.2 %collective-permute-start.4 = (bf16[448,256]{1,0:T(8,128)(2,1)S(1)}, bf16[448,256]{1,0:T(8,128)(2,1)S(1)}, u32[]{:S(2)}, u32[]{:S(2)}) collective-permute-start(bf16[448,256]{1,0:T(8,128)(2,1)S(1)} %first.1.own_ref), channel_id=1, source_target_pairs={{64,0},{128,64},{192,128},{0,192},{65,1},{129,65},{193,129},{1,193... | collective-permute-start | bytes 688136 | tf_op jit(solution)/shard_map/ppermute | solution.py:234
  52.0 1.4 %collective-permute-start.2 = (f32[7,8,36]{2,1,0:T(8,128)S(1)}, f32[7,8,36]{2,1,0:T(8,128)S(1)}, u32[]{:S(2)}, u32[]{:S(2)}) collective-permute-start(f32[7,8,36]{2,1,0:T(8,128)S(1)} %bitcast.20), channel_id=1, source_target_pairs={{0,1},{1,0},{2,3},{3,2},{4,5},{5,4},{6,7},{7,6},{8,9},{9,8},{10,11... | collective-permute-start | bytes 24200 | tf_op jit(solution)/shard_map/ppermute | solution.py:227
  77.8 34.9 %copy-start.1 = (bf16[128,448]{0,1:T(8,128)(2,1)S(1)}, bf16[128,448]{0,1:T(8,128)(2,1)}, u32[]{:S(2)}) copy-start(bf16[128,448]{0,1:T(8,128)(2,1)} %param.15) | copy-start | bytes 344068
  77.8 3.8 %collective-permute-start.5 = (bf16[32,16,384]{2,1,0:T(8,128)(2,1)S(1)}, bf16[32,16,384]{2,1,0:T(8,128)(2,1)S(1)}, u32[]{:S(2)}, u32[]{:S(2)}) collective-permute-start(bf16[32,16,384]{2,1,0:T(8,128)(2,1)S(1)} %all_to_all.16.in_ref), channel_id=1, source_target_pairs={{0,1},{1,0},{2,3},{3,2},{4,5},{5,4},{6,7},{7,6},{8,9},{9,8},{10,11... | collective-permute-start | bytes 1179656 | tf_op jit(solution)/shard_map/ppermute | solution.py:227
  83.8 8.1 %collective-permute-start.6 = (bf16[448,256]{1,0:T(8,128)(2,1)S(1)}, bf16[448,256]{1,0:T(8,128)(2,1)S(1)}, u32[]{:S(2)}, u32[]{:S(2)}) collective-permute-start(bf16[448,256]{1,0:T(8,128)(2,1)S(1)} %coeffs.1.own_ref), channel_id=1, source_target_pairs={{0,64},{64,128},{128,192},{192,0},{1,65},{65,129},{129,193},{193,1... | collective-permute-start | bytes 688136 | tf_op jit(solution)/shard_map/ppermute | solution.py:234
  84.8 7.1 %collective-permute-start.7 = (bf16[448,256]{1,0:T(8,128)(2,1)S(1)}, bf16[448,256]{1,0:T(8,128)(2,1)S(1)}, u32[]{:S(2)}, u32[]{:S(2)}) collective-permute-start(bf16[448,256]{1,0:T(8,128)(2,1)S(1)} %coeffs.1.own_ref), channel_id=1, source_target_pairs={{64,0},{128,64},{192,128},{0,192},{65,1},{129,65},{193,129},{1,193... | collective-permute-start | bytes 688136 | tf_op jit(solution)/shard_map/ppermute | solution.py:234

commit v3 on v2

v3 whole, which is shorter than its diff:
```python
import jax
import jax.numpy as jnp
from jax import lax
from jax.experimental import pallas as pl
from jax.experimental.pallas import tpu as pltpu
from jax.sharding import Mesh, PartitionSpec as P

ITERS = 2
Z, Y, C = 8, 4, 2
PLANE = ("z", "y")
CHIPS = Z * Y
F32, BF16, I32 = jnp.float32, jnp.bfloat16, jnp.int32

BD, H, S, M = 8, 36, 7, 448
HC, R, BLK, L = H // C, S * C, 16, 256
LAN = HC * BD
ROWS = CHIPS * BLK
HALF = M // C
SOURCES = 3 * BD
EMPTY = SOURCES * BD


def iota(shape, dim):
    return lax.broadcasted_iota(I32, shape, dim)


def ones(cond):
    return jnp.where(cond, 1.0, 0.0).astype(BF16)


def dot(left, right, dims=(1, 0), exact=False):
    return lax.dot_general(
        left,
        right,
        (((dims[0],), (dims[1],)), ((), ())),
        preferred_element_type=F32,
        precision=lax.Precision.HIGHEST if exact else None,
    )


def shift(rows, cols, start, to, width):
    row, col = iota((rows, cols), 0), iota((rows, cols), 1)
    return ones((row - start == col - to) & (col >= to) & (col < to + width))


def padding():
    row, col = iota((ROWS, M), 0), iota((ROWS, M), 1)
    return ones((col == row - 2 * (row >> 4)) & ((row & 15) < R))


def packing():
    row, col = iota((M, ROWS), 0), iota((M, ROWS), 1)
    return ones((row == col - 2 * (col >> 4)) & ((col & 15) < R))


def packed(field):
    rows = field.shape[0]
    frow, fcol = iota((128, 128), 0), iota((128, 128), 1)
    tail = dot(field[:, 128:].astype(BF16), ones(frow == (fcol & 15)))
    row, lane = iota((rows, 128), 0), iota((rows, 128), 1)
    tail = jnp.where(((lane >> 4) == (row & 7)) & ((row & 15) < R), tail, 0.0).astype(BF16)
    to, col = iota((rows, rows), 0), iota((rows, rows), 1)
    same = (to >> 4) == (col >> 4)
    tail = dot(ones(same & ((to & 15) == R + ((col & 15) >> 3)) & ((col & 15) < R)), tail)
    return jnp.where((row & 15) < R, field[:, :128], tail).astype(BF16)


def unpacked(blocks):
    row, lane = iota((M, 128), 0), iota((M, 128), 1)
    place = row - R * ((row * 4682) >> 16)
    to, col = iota((M, ROWS), 0), iota((M, ROWS), 1)
    chip = (to * 4682) >> 16
    spare = ones(col == BLK * chip + R + ((to - R * chip) >> 3))
    tail = jnp.where((lane >> 4) == (place & 7), dot(spare, blocks), 0.0).astype(BF16)
    frow, fcol = iota((128, 128), 0), iota((128, 128), 1)
    tail = dot(tail, ones((fcol == (frow & 15)) & (fcol < 16)))
    return jnp.concatenate([dot(packing(), blocks), tail], axis=1).astype(BF16)


def chip_field(own, other, core, exact):
    kind = F32 if exact else BF16
    head, lane = iota((H, L), 0), iota((H, L), 1)
    spread = ones((head == core * HC + (lane >> 3)) & (lane < LAN)).astype(kind)
    row, lane = iota((S * BD, L), 0), iota((S * BD, L), 1)
    total = 0.0
    for value, place in ((own, core), (other, 1 - core)):
        wide = dot(value.reshape(S * BD, H).astype(kind), spread, exact=exact)
        wide = jnp.where((row & 7) == (lane & 7), wide, 0.0)
        to, col = iota((BLK, S * BD), 0), iota((BLK, S * BD), 1)
        gather = ones((col >> 3) == to - S * place).astype(kind)
        total = total + dot(gather, wide.astype(kind), exact=exact)
    return total


def send_kernel(where_am_i, source, target, live, t_hbm, d_hbm, out_ref, t_ref, d_ref, sems):
    copies = [pltpu.make_async_copy(d_hbm, d_ref, sems.at[0])]
    copies += [pltpu.make_async_copy(t_hbm.at[p], t_ref.at[p], sems.at[1 + p]) for p in range(2)]
    for copy in copies:
        copy.start()
    buoy = where_am_i[1]
    pad = padding()
    widen = shift(64, 128, 0, 0, 64)
    row, col = iota((M, M), 0), iota((M, M), 1)
    row = row - HALF * (buoy & 1)
    twice = ones((row == jnp.where(col < HALF, col, col - HALF)))
    to, slot_row = iota((BLK, S), 0), iota((BLK, S), 1)
    lane = iota((S, M), 1)
    brow, blane = iota((BLK, 128), 0), iota((BLK, 128), 1)
    copies[0].wait()
    both = dot(d_ref[...], twice)
    low = jnp.where(lane < HALF, both, 0.0).astype(BF16)
    high = jnp.where(lane < HALF, 0.0, both).astype(BF16)
    for p in range(2):
        spare = 0.0
        for k, part in enumerate((low, high)):
            first = (to == R) & (slot_row == 2 * p + k)
            second = (to == R + 1) & (slot_row == 4 + 2 * p + k)
            spare = spare + dot(ones(first | second), part)
        number = 0.0
        if p == 1:
            for k in range(2):
                at = (source[k] - (buoy - 1) * BD) * BD + target[k] - buoy * BD
                at = jnp.where(live[k] == 1, jnp.clip(at, 0, EMPTY), EMPTY)
                number = jnp.where((brow == BLK - 1) & (blane == k), at.astype(F32), number)
        copies[1 + p].wait()
        for q in range(3):
            part = dot(pad, t_ref[p, :, 128 * q : 128 * (q + 1)]).reshape(CHIPS, BLK, 128)
            extra = spare[:, 128 * q : 128 * (q + 1)]
            if p == 1 and q == 2:
                extra = extra + number
            at = 512 * p + 128 * q
            out_ref[:, :, at : at + 128] = (part + extra[None]).astype(BF16)
        last = dot(t_ref[p, :, 384:M], widen).astype(BF16)
        extra = dot(spare[:, 384:M].astype(BF16), widen)
        part = dot(pad, last).reshape(CHIPS, BLK, 128) + extra[None]
        out_ref[:, :, 512 * p + 384 : 512 * p + 512] = part.astype(BF16)


def begin_kernel(where_am_i, own_ref, other_ref, in_ref, out_ref):
    del in_ref
    field = chip_field(own_ref[...], other_ref[...], where_am_i[0], False)
    block = packed(field)
    lane = iota((BLK, 128), 1)
    corner = (
        dot(block, shift(128, 128, 0, 64, 64)),
        jnp.where(lane >= 64, block.astype(F32), 0.0),
    )
    for p in range(2):
        at = 512 * p + 384
        tile = out_ref[:, :, at : at + 128].astype(F32) + corner[p][None]
        out_ref[:, :, at : at + 128] = tile.astype(BF16)


def first_kernel(in_ref, out_ref):
    third = in_ref[:, :, 384:512].reshape(ROWS, 128)
    last = in_ref[:, :, 896:1024].reshape(ROWS, 128)
    lane = iota((ROWS, 128), 1)
    block = dot(third, shift(128, 128, 64, 0, 64)) + jnp.where(lane >= 64, last.astype(F32), 0.0)
    out_ref[...] = block.astype(BF16)


def place_kernel(
    where_am_i, own_at, other_at, in_ref, other_ref, amb_ref, amb_other_ref, w_ref, a_ref, d_ref
):
    core = where_am_i[0]
    w_ref[...] = jnp.zeros_like(w_ref)
    for j in range(CHIPS):
        for p in range(2):
            w_ref[own_at[j, p]] = in_ref[j, :, 512 * p : 512 * (p + 1)]
            w_ref[other_at[j, p]] = other_ref[j, :, 512 * p : 512 * (p + 1)]
    a_ref[...] = chip_field(amb_ref[...], amb_other_ref[...], core, True)
    to, col = iota((ROWS, CHIPS * 8), 0), iota((ROWS, CHIPS * 8), 1)
    same = (to >> 4) == (col >> 3)
    spot = (to & 15, (col & 7) - 6)
    halves = [0.0, 0.0]
    for ref, place in ((in_ref, core), (other_ref, 1 - core)):
        for p in range(2):
            part = ref[:, 8:, 512 * p : 512 * p + M].reshape(CHIPS * 8, M)
            for k in range(2):
                line = spot[0] - S * place - 2 * p - k
                pick = ones(same & (((line == 0) & (spot[1] == 0)) | ((line == 4) & (spot[1] == 1))))
                if p == 1 and k == 1:
                    pick = ones(same & (line == 0) & (spot[1] == 0))
                halves[k] = halves[k] + dot(pick, part)
    d_ref[...] = (
        dot(halves[0].astype(BF16), shift(M, L, 0, 0, HALF))
        + dot(halves[1].astype(BF16), shift(M, L, HALF, 0, HALF))
    ).astype(BF16)


def weighted(w_ref, group, field):
    lane = iota((BD * BLK, L), 1)
    total = jnp.zeros((BD * BLK, L), F32)
    for b in range(BD):
        part = dot(w_ref[BD * group + b, :, :M], field)
        total = total + jnp.where((lane & 7) == b, part, 0.0)
    return total


def own_kernel(w_ref, own_ref, out_ref):
    out_ref[...] = weighted(w_ref, 1, unpacked(own_ref[...]))


def incident_kernel(w_ref, low_ref, high_ref, part_ref, a_ref, out_ref):
    total = part_ref[...]
    total = total + weighted(w_ref, 0, unpacked(low_ref[...]))
    total = total + weighted(w_ref, 2, unpacked(high_ref[...]))
    row, col = iota((L, L), 0), iota((L, L), 1)
    same = ones(((row >> 3) == (col >> 3)) & (row < LAN)).astype(F32)
    total = dot(total, same, exact=True)
    row, lane = iota((BLK, L), 0), iota((BLK, L), 1)
    mine = a_ref[...]
    for t in range(BD):
        mine = mine + jnp.where((lane & 7) == t, total[BLK * t : BLK * (t + 1)], 0.0)
    mine = jnp.where((row < R) & (lane < LAN), mine, 0.0)
    out_ref[...] = jnp.broadcast_to(packed(mine)[None], (CHIPS, BLK, 128))


def coeffs_kernel(where_am_i, in_ref, d_ref, d_other_ref, out_ref):
    field = unpacked(in_ref[...].reshape(ROWS, 128))
    even = (where_am_i[1] & 1) == 0
    upper, lower = field[:HALF].astype(F32), field[HALF:].astype(F32)
    first = jnp.where(even, upper, lower).astype(BF16)
    second = jnp.where(even, lower, upper).astype(BF16)
    out_ref[...] = packed(dot(d_ref[:, :HALF], first) + dot(d_other_ref[:, :HALF], second))


def last_kernel(in_ref, p_ref, d_ref, src_ref, out_ref):
    out = 0.0
    for c in range(C):
        field = unpacked(in_ref[c].reshape(ROWS, 128))
        part = dot(field, p_ref[...], dims=(0, 0))
        src_ref[LAN * c : LAN * (c + 1), :] = part[:LAN].astype(BF16)
        row, col = iota((L, BD * 128), 0), iota((L, BD * 128), 1)
        to = (row & 7) * 128 + (row >> 3) + HC * c
        wide = dot(field, ones((col == to) & (row < LAN))).astype(BF16)
        out = out + dot(d_ref[...], wide)
    for b in range(BD):
        out_ref[:, b, :] = out[:, 128 * b : 128 * b + H]


VM = pl.BlockSpec(memory_space=pltpu.VMEM)
SM = pl.BlockSpec(memory_space=pltpu.SMEM)
HBM = pl.BlockSpec(memory_space=pl.ANY)


def call(kernel, scalars, arrays, shapes, name, **kwargs):
    return pl.pallas_call(
        kernel,
        out_shape=shapes,
        in_specs=[SM] * len(scalars) + [VM] * len(arrays),
        out_specs=[VM] * len(shapes) if isinstance(shapes, tuple) else VM,
        compiler_params=pltpu.CompilerParams(vmem_limit_bytes=40 << 20),
        name=name,
        **kwargs,
    )(*scalars, *arrays)


def shape(*dims, dtype=BF16):
    return jax.ShapeDtypeStruct(dims, dtype)


def exchange(blocks):
    return lax.all_to_all(blocks, PLANE, 0, 0, tiled=True)


def swapped(value):
    return lax.ppermute(value, "c", [(0, 1), (1, 0)])


def from_previous(value):
    count = lax.axis_size("x")
    return lax.ppermute(value, "x", [(i, (i + 1) % count) for i in range(count)])


def from_next(value):
    count = lax.axis_size("x")
    return lax.ppermute(value, "x", [((i + 1) % count, i) for i in range(count)])


def slot_numbers(blocks):
    return blocks[:, BLK - 1, 768:770].astype(I32)


def shards(
    ambient, initial_out, translation, pair_source, pair_target, pair_live, diffract, panel_rows
):
    where_am_i = jnp.stack([lax.axis_index("c"), lax.axis_index("x")]).astype(I32)
    begin = initial_out.transpose(2, 0, 1)
    waves = ambient.transpose(2, 0, 1)
    begin_other = swapped(begin)
    message = pl.pallas_call(
        send_kernel,
        out_shape=shape(CHIPS, BLK, 1024),
        in_specs=[SM] * 4 + [HBM] * 2,
        out_specs=VM,
        scratch_shapes=[
            pltpu.VMEM(translation.shape, BF16),
            pltpu.VMEM(diffract.shape, BF16),
            pltpu.SemaphoreType.DMA((3,)),
        ],
        compiler_params=pltpu.CompilerParams(vmem_limit_bytes=40 << 20),
        name="send",
    )(where_am_i, pair_source, pair_target, pair_live, translation, diffract)
    message = call(
        begin_kernel,
        (where_am_i,),
        (begin, begin_other, message),
        shape(CHIPS, BLK, 1024),
        "begin",
        input_output_aliases={3: 0},
    )
    got = exchange(message)
    got, waves, panel_rows = lax.optimization_barrier((got, waves, panel_rows))
    coeffs = call(first_kernel, (), (got,), shape(ROWS, 128), "first")
    low, high = from_previous(coeffs), from_next(coeffs)
    got_other = swapped(got)
    matrices, own_waves, half = call(
        place_kernel,
        (where_am_i, slot_numbers(got), slot_numbers(got_other)),
        (got, got_other, waves, swapped(waves)),
        (shape(EMPTY + BD, BLK, 512), shape(BLK, L, dtype=F32), shape(ROWS, L)),
        "place",
    )
    matrices = matrices.reshape(SOURCES + 1, BD * BLK, 512)
    other_half = from_previous(half)

    for step in range(ITERS):
        if step:
            coeffs = call(
                coeffs_kernel, (where_am_i,), (got, half, other_half), shape(ROWS, 128), "coeffs"
            )
            low, high = from_previous(coeffs), from_next(coeffs)
        part = call(own_kernel, (), (matrices, coeffs), shape(BD * BLK, L, dtype=F32), "own")
        message = call(
            incident_kernel,
            (),
            (matrices, low, high, part, own_waves),
            shape(CHIPS, BLK, 128),
            "incident",
        )
        got = exchange(message)
    whole = lax.all_gather(got, "c", axis=0, tiled=False)
    sources, outgoing = call(
        last_kernel,
        (),
        (whole, panel_rows.T, diffract),
        (shape(H * BD, panel_rows.shape[0]), shape(S, BD, H, dtype=F32)),
        "last",
    )
    sources = sources.reshape(H, BD, panel_rows.shape[0]).transpose(1, 0, 2)
    return outgoing.transpose(1, 2, 0), sources


def solution(mesh):
    fine = Mesh(mesh.devices.reshape(mesh.shape["buoy"], Z, Y, C), ("x", "z", "y", "c"))
    dom = ("z", "y", "c")
    in_specs = (
        P("x", None, dom),
        P("x", None, dom),
        P(("x",) + dom, None, None),
        P(("x",) + dom),
        P(("x",) + dom),
        P(("x",) + dom),
        P(dom, None),
        P(dom, None),
    )
    out_specs = (P("x", None, dom), P("x", None, dom))
    return jax.shard_map(shards, mesh=fine, in_specs=in_specs, out_specs=out_specs, check_vma=False)
```

time: 115 us -> 111 us (0.965)
  Pallas kernels: 12.7 us -> 21.8 us
  waiting for transfers between devices: 9.32 us -> 1.88 us
  blocking collectives: 74 us -> 69.9 us
  starting transfers between devices: 14.5 us -> 11.5 us
  local copies, waits for them, and re-layouts: 2.77 us -> 4.59 us
    ppermute x4 -> x5, waiting for transfers between devices: 7.26 us -> 1.11 us  [the longest x3 1.11 us: from_previous(): lax.ppermute(value, 'x', [(i, (i + 1) % count) for i in range(count)])]
    pallas_call x7 -> x9, Pallas kernels: 12.7 us -> 18.4 us  [call(): pl.pallas_call(kernel, out_shape=shapes, in_specs=[SM] * len(scalars) + [...]
    all_to_all x3, blocking collectives: 68.9 us -> 63.6 us  [exchange(): return lax.all_to_all(blocks, PLANE, 0, 0, tiled=True)]
    pallas_call x0 -> x1, Pallas kernels: none -> 3.41 us  [shards(): pl.pallas_call(send_kernel, out_shape=shape(CHIPS, BLK, 1024), in_specs=[...]
    ppermute x4 -> x3, starting transfers between devices: 8.98 us -> 5.63 us  [swapped(): return lax.ppermute(value, 'c', [(0, 1), (1, 0)])]
    unnamed x10 -> x16, local copies, waits for them, and re-layouts: 1.94 us -> 4.59 us
    ppermute x4 -> x3, waiting for transfers between devices: 2.06 us -> 0.77 us  [swapped(): return lax.ppermute(value, 'c', [(0, 1), (1, 0)])]
    all_gather x1, blocking collectives: 5.13 us -> 6.31 us  [shards(): whole = lax.all_gather(got, 'c', axis=0, tiled=False)]
  transfers between devices with their start and end apart: 8 -> 8, of which waited for: 5 -> 2; matrix products, arithmetic and copies ran while one was open for 1% -> 0% of each run, Pallas kernels for 2% -> 8%
where the time goes in v3:
time: 111 us
  blocking collectives  69.9 us (63%)
  Pallas kernels  21.8 us (20%)
  starting transfers between devices  11.5 us (10%)
  local copies, waits for them, and re-layouts  4.59 us (4%)
  waiting for transfers between devices  1.88 us (2%)
    all_to_all x3, blocking collectives, exchange(): return lax.all_to_all(blocks, PLANE, 0, 0, tiled=True)  63.6 us
    pallas_call x9, Pallas kernels, call(): pl.pallas_call(kernel, out_shape=shapes, in_specs=[SM] * len(scalars) + [...  18.4 us
    all_gather x1, blocking collectives, shards(): whole = lax.all_gather(got, 'c', axis=0, tiled=False)  6.31 us
    ppermute x3, starting transfers between devices, swapped(): return lax.ppermute(value, 'c', [(0, 1), (1, 0)])  5.63 us
    unnamed x16, local copies, waits for them, and re-layouts  4.59 us
    pallas_call x1, Pallas kernels, shards(): pl.pallas_call(send_kernel, out_shape=shape(CHIPS, BLK, 1024), in_specs=[...  3.41 us
    ppermute x2, starting transfers between devices, from_next(): lax.ppermute(value, 'x', [((i + 1) % count, i) for i in range(count)])  3.03 us
    ppermute x3, starting transfers between devices, from_previous(): lax.ppermute(value, 'x', [(i, (i + 1) % count) for i in range(count)])  2.82 us
  transfers between devices with their start and end apart: 8, of which 2 were waited for; matrix products, arithmetic and copies ran while one was open for 0% of the time, Pallas kernels for 8%

profile of v3, /device:TPU:1, one launch (start us, length us, event | category | flops | bytes accessed | tf_op | source)
XLA Modules:
  0.0 110.5 jit_solution(9045532831859884225)
XLA Ops:
  0.6 3.3 %collective-permute-start = (f32[7,8,36]{2,1,0:T(8,128)}, f32[7,8,36]{2,1,0:T(8,128)S(1)}, u32[]{:S(2)}, u32[]{:S(2)}) collective-permute-start(f32[7,8,36]{2,1,0:T(8,128)} %bitcast.21), channel_id=1, source_target_pairs={{0,1},{1,0},{2,3},{3,2},{4,5},{5,4},{6,7},{7,6},{8,9},{9,8},{10,11... | collective-permute-start | bytes 24200 | tf_op jit(solution)/shard_map/ppermute | solution.py:268
  4.0 0.1 pad_add_fusion.where_am_i
  4.0 1.2 %copy-done = bf16[2,448,448]{2,1,0:T(8,128)(2,1)S(1)} copy-done((bf16[2,448,448]{2,1,0:T(8,128)(2,1)S(1)}, bf16[2,448,448]{2,1,0:T(8,128)(2,1)}, u32[]{:S(2)}) %copy-start) | copy-done | bytes 802840
  5.2 0.7 copy-done.2
  5.9 0.7 copy-done.5
  6.6 0.7 copy-done.6
  7.2 0.7 copy-done.7
  7.9 3.4 %send.1.in_ref = bf16[32,16,1024]{2,1,0:T(8,128)(2,1)S(1)} custom-call(s32[2]{0:T(128)S(1)} %pad_add_fusion.where_am_i, s32[2]{0:T(128)S(1)} %copy-done.5, s32[2]{0:T(128)S(1)} %copy-done.6, s32[2]{0:T(128)S(1)} %copy-done.7, bf16[2,448,448]{2,1,0:T(8,128)(2,1)S(1)} %copy-done, bf16[7,448]{1,0:T(8,128)(2,1)S(1)} %copy-done.2), custom_call_target="tpu_custom_call" | custom-call | tf_op jit(solution)/shard_map/send/pallas_call | solution.py:292
  11.3 0.0 copy-start.3
  11.3 0.7 copy-done.3
  12.1 1.2 %begin.1 = bf16[32,16,1024]{2,1,0:T(8,128)(2,1)S(1)} custom-call(s32[2]{0:T(128)S(1)} %pad_add_fusion.where_am_i, f32[7,8,36]{2,1,0:T(8,128)S(1)} %bitcast.22, f32[7,8,36]{2,1,0:T(8,128)S(1)} %collective-permute-done.other_ref, bf16[32,16,1024]{2,1,0:T(8,128)(2,1)S(1)} %send.1.in_ref), custom_call_target="tpu_custom_call", output_to_operand_aliasing={{}: (3, {})} | custom-call | tf_op jit(solution)/shard_map/begin/pallas_call | solution.py:248
  13.3 36.5 %all_to_all.15.in_ref = bf16[32,16,1024]{2,1,0:T(8,128)(2,1)S(1)} all-to-all(bf16[32,16,1024]{2,1,0:T(8,128)(2,1)S(1)} %begin.1), channel_id=1, replica_groups=mesh['x'=4,'z'=8,'y'=4,'c'=2] {'z','y'}, dimensions={0} | all-to-all | bytes 2097152 | tf_op jit(solution)/shard_map/all_to_all | solution.py:264
  49.8 1.7 %collective-permute-start.1 = (bf16[32,16,1024]{2,1,0:T(8,128)(2,1)S(1)}, bf16[32,16,1024]{2,1,0:T(8,128)(2,1)S(1)}, u32[]{:S(2)}, u32[]{:S(2)}) collective-permute-start(bf16[32,16,1024]{2,1,0:T(8,128)(2,1)S(1)} %all_to_all.15.in_ref), channel_id=1, source_target_pairs={{0,1},{1,0},{2,3},{3,2},{4,5},{5,4},{6,7},{7,6},{8,9},{9,8},{10,11... | collective-permute-start | bytes 3145736 | tf_op jit(solution)/shard_map/ppermute | solution.py:268
  51.5 0.2 first.1.own_ref
  51.7 1.3 %collective-permute-start.3 = (bf16[512,128]{1,0:T(8,128)(2,1)S(1)}, bf16[512,128]{1,0:T(8,128)(2,1)S(1)}, u32[]{:S(2)}, u32[]{:S(2)}) collective-permute-start(bf16[512,128]{1,0:T(8,128)(2,1)S(1)} %first.1.own_ref), channel_id=1, source_target_pairs={{0,64},{64,128},{128,192},{192,0},{1,65},{65,129},{129,193},{193,1... | collective-permute-start | bytes 393224 | tf_op jit(solution)/shard_map/ppermute | solution.py:273
  53.0 1.5 %collective-permute-start.4 = (bf16[512,128]{1,0:T(8,128)(2,1)S(1)}, bf16[512,128]{1,0:T(8,128)(2,1)S(1)}, u32[]{:S(2)}, u32[]{:S(2)}) collective-permute-start(bf16[512,128]{1,0:T(8,128)(2,1)S(1)} %first.1.own_ref), channel_id=1, source_target_pairs={{64,0},{128,64},{192,128},{0,192},{65,1},{129,65},{193,129},{1,193... | collective-permute-start | bytes 393224 | tf_op jit(solution)/shard_map/ppermute | solution.py:278
  54.5 0.6 collective-permute-start.2
  55.1 0.8 collective-permute-done.2.amb_other_ref
  55.9 4.2 %place.1 = (bf16[200,16,512]{2,1,0:T(8,128)(2,1)S(1)}, f32[16,256]{1,0:T(8,128)S(1)}, bf16[512,256]{1,0:T(8,128)(2,1)S(1)}) custom-call(s32[2]{0:T(128)S(1)} %pad_add_fusion.where_am_i, s32[32,2]{1,0:T(8,128)S(1)} %bitcast.19, s32[32,2]{1,0:T(8,128)S(1)} %bitcast.20, bf16[32,16,1024]{2,1,0:T(8,128)(2,1)S(1)} %all_to_all.15.in_ref, ...), custom_call_target="tpu_custom_call" | custom-call | tf_op jit(solution)/shard_map/place/pallas_call | solution.py:248
  60.1 0.3 collective-permute-start.5
  60.4 1.2 %own.2.part_ref = f32[128,256]{1,0:T(8,128)S(1)} custom-call(bf16[25,128,512]{2,1,0:T(8,128)(2,1)S(1)} %bitcast.13, bf16[512,128]{1,0:T(8,128)(2,1)S(1)} %first.1.own_ref), custom_call_target="tpu_custom_call" | custom-call | tf_op jit(solution)/shard_map/own/pallas_call | solution.py:248
  61.6 2.7 %incident.2 = bf16[32,16,128]{2,1,0:T(8,128)(2,1)S(1)} custom-call(bf16[25,128,512]{2,1,0:T(8,128)(2,1)S(1)} %bitcast.14, bf16[512,128]{1,0:T(8,128)(2,1)S(1)} %collective-permute-done.3.low_ref, bf16[512,128]{1,0:T(8,128)(2,1)S(1)} %collective-permute-done.4.high_ref, f32[128,256]{1,0:T(8,128)S(1)} %own.2.part_ref, f32[16,256]{1,0:T(8,128)S(1)} %get-tuple-element.13.a_ref), custom_call_target="tpu_custom_call" | custom-call | tf_op jit(solution)/shard_map/incident/pallas_call | solution.py:248
  64.3 14.4 %all_to_all.16.in_ref = bf16[32,16,128]{2,1,0:T(8,128)(2,1)S(1)} all-to-all(bf16[32,16,128]{2,1,0:T(8,128)(2,1)S(1)} %incident.2), channel_id=1, replica_groups=mesh['x'=4,'z'=8,'y'=4,'c'=2] {'z','y'}, dimensions={0} | all-to-all | bytes 262144 | tf_op jit(solution)/shard_map/all_to_all | solution.py:264
  78.7 2.1 %coeffs.1.own_ref = bf16[512,128]{1,0:T(8,128)(2,1)S(1)} custom-call(s32[2]{0:T(128)S(1)} %pad_add_fusion.where_am_i, bf16[32,16,128]{2,1,0:T(8,128)(2,1)S(1)} %all_to_all.16.in_ref, bf16[512,256]{1,0:T(8,128)(2,1)S(1)} %get-tuple-element.14.d_ref, bf16[512,256]{1,0:T(8,128)(2,1)S(1)} %collective-permute-done.5.d_other_ref), custom_call_target="tpu_custom_call" | custom-call | tf_op jit(solution)/shard_map/coeffs/pallas_call | solution.py:248
  80.8 1.3 %collective-permute-start.6 = (bf16[512,128]{1,0:T(8,128)(2,1)S(1)}, bf16[512,128]{1,0:T(8,128)(2,1)S(1)}, u32[]{:S(2)}, u32[]{:S(2)}) collective-permute-start(bf16[512,128]{1,0:T(8,128)(2,1)S(1)} %coeffs.1.own_ref), channel_id=1, source_target_pairs={{0,64},{64,128},{128,192},{192,0},{1,65},{65,129},{129,193},{193,1... | collective-permute-start | bytes 393224 | tf_op jit(solution)/shard_map/ppermute | solution.py:273
  82.0 1.6 %collective-permute-start.7 = (bf16[512,128]{1,0:T(8,128)(2,1)S(1)}, bf16[512,128]{1,0:T(8,128)(2,1)S(1)}, u32[]{:S(2)}, u32[]{:S(2)}) collective-permute-start(bf16[512,128]{1,0:T(8,128)(2,1)S(1)} %coeffs.1.own_ref), channel_id=1, source_target_pairs={{64,0},{128,64},{192,128},{0,192},{65,1},{129,65},{193,129},{1,193... | collective-permute-start | bytes 393224 | tf_op jit(solution)/shard_map/ppermute | solution.py:278
  83.6 1.2 %own.3.part_ref = f32[128,256]{1,0:T(8,128)S(1)} custom-call(bf16[25,128,512]{2,1,0:T(8,128)(2,1)S(1)} %bitcast.15, bf16[512,128]{1,0:T(8,128)(2,1)S(1)} %coeffs.1.own_ref), custom_call_target="tpu_custom_call" | custom-call | tf_op jit(solution)/shard_map/own/pallas_call | solution.py:248
  84.8 1.1 collective-permute-done.6.low_ref
  85.9 2.7 %incident.3 = bf16[32,16,128]{2,1,0:T(8,128)(2,1)S(1)} custom-call(bf16[25,128,512]{2,1,0:T(8,128)(2,1)S(1)} %bitcast.16, bf16[512,128]{1,0:T(8,128)(2,1)S(1)} %collective-permute-done.6.low_ref, bf16[512,128]{1,0:T(8,128)(2,1)S(1)} %collective-permute-done.7.high_ref, f32[128,256]{1,0:T(8,128)S(1)} %own.3.part_ref, f32[16,256]{1,0:T(8,128)S(1)} %get-tuple-element.13.a_ref), custom_call_target="tpu_custom_call" | custom-call | tf_op jit(solution)/shard_map/incident/pallas_call | solution.py:248
  88.6 12.6 %all_to_all.17 = bf16[32,16,128]{2,1,0:T(8,128)(2,1)S(1)} all-to-all(bf16[32,16,128]{2,1,0:T(8,128)(2,1)S(1)} %incident.3), channel_id=1, replica_groups=mesh['x'=4,'z'=8,'y'=4,'c'=2] {'z','y'}, dimensions={0} | all-to-all | bytes 262144 | tf_op jit(solution)/shard_map/all_to_all | solution.py:264
  101.2 6.3 %all-gather = bf16[64,16,128]{2,1,0:T(8,128)(2,1)S(1)} all-gather(bf16[32,16,128]{2,1,0:T(8,128)(2,1)S(1)} %all_to_all.17), channel_id=2, replica_groups=mesh['x'=4,'z'=8,'y'=4,'c'=2] {'c'}, dimensions={0}, use_global_device_ids=true | all-gather | bytes 393216 | tf_op jit(solution)/shard_map/all_gather | solution.py:343
  107.5 3.1 %last.1 = (bf16[288,128]{1,0:T(8,128)(2,1)}, f32[7,8,36]{2,1,0:T(8,128)}) custom-call(bf16[2,32,16,128]{3,2,1,0:T(8,128)(2,1)S(1)} %bitcast.17, bf16[448,128]{1,0:T(8,128)(2,1)S(1)} %bitcast.18, bf16[7,448]{1,0:T(8,128)(2,1)S(1)} %copy-done.2), custom_call_target="tpu_custom_call" | custom-call | tf_op jit(solution)/shard_map/last/pallas_call | solution.py:248
  (17 shorter events, 0.1 us)
Async XLA Ops:
  0.6 10.7 %collective-permute-start = (f32[7,8,36]{2,1,0:T(8,128)}, f32[7,8,36]{2,1,0:T(8,128)S(1)}, u32[]{:S(2)}, u32[]{:S(2)}) collective-permute-start(f32[7,8,36]{2,1,0:T(8,128)} %bitcast.21), channel_id=1, source_target_pairs={{0,1},{1,0},{2,3},{3,2},{4,5},{5,4},{6,7},{7,6},{8,9},{9,8},{10,11... | collective-permute-start | bytes 24200 | tf_op jit(solution)/shard_map/ppermute | solution.py:268
  4.0 1.2 %copy-start = (bf16[2,448,448]{2,1,0:T(8,128)(2,1)S(1)}, bf16[2,448,448]{2,1,0:T(8,128)(2,1)}, u32[]{:S(2)}) copy-start(bf16[2,448,448]{2,1,0:T(8,128)(2,1)} %t_hbm.1) | copy-start | bytes 2408452
  5.2 0.7 copy-start.2
  5.9 0.7 copy-start.5
  6.6 0.7 copy-start.6
  7.2 0.7 copy-start.7
  7.9 46.6 %copy-start.4 = (f32[8,36,7]{1,0,2:T(8,128)S(1)}, f32[8,36,7]{1,0,2:T(8,128)}, u32[]{:S(2)}) copy-start(f32[8,36,7]{1,0,2:T(8,128)} %param.8) | copy-start | bytes 24196
  11.3 0.8 copy-start.3
  49.8 5.3 %collective-permute-start.1 = (bf16[32,16,1024]{2,1,0:T(8,128)(2,1)S(1)}, bf16[32,16,1024]{2,1,0:T(8,128)(2,1)S(1)}, u32[]{:S(2)}, u32[]{:S(2)}) collective-permute-start(bf16[32,16,1024]{2,1,0:T(8,128)(2,1)S(1)} %all_to_all.15.in_ref), channel_id=1, source_target_pairs={{0,1},{1,0},{2,3},{3,2},{4,5},{5,4},{6,7},{7,6},{8,9},{9,8},{10,11... | collective-permute-start | bytes 3145736 | tf_op jit(solution)/shard_map/ppermute | solution.py:268
  51.7 9.9 %collective-permute-start.3 = (bf16[512,128]{1,0:T(8,128)(2,1)S(1)}, bf16[512,128]{1,0:T(8,128)(2,1)S(1)}, u32[]{:S(2)}, u32[]{:S(2)}) collective-permute-start(bf16[512,128]{1,0:T(8,128)(2,1)S(1)} %first.1.own_ref), channel_id=1, source_target_pairs={{0,64},{64,128},{128,192},{192,0},{1,65},{65,129},{129,193},{193,1... | collective-permute-start | bytes 393224 | tf_op jit(solution)/shard_map/ppermute | solution.py:273
  53.0 8.6 %collective-permute-start.4 = (bf16[512,128]{1,0:T(8,128)(2,1)S(1)}, bf16[512,128]{1,0:T(8,128)(2,1)S(1)}, u32[]{:S(2)}, u32[]{:S(2)}) collective-permute-start(bf16[512,128]{1,0:T(8,128)(2,1)S(1)} %first.1.own_ref), channel_id=1, source_target_pairs={{64,0},{128,64},{192,128},{0,192},{65,1},{129,65},{193,129},{1,193... | collective-permute-start | bytes 393224 | tf_op jit(solution)/shard_map/ppermute | solution.py:278
  54.5 1.4 %collective-permute-start.2 = (f32[7,8,36]{2,1,0:T(8,128)S(1)}, f32[7,8,36]{2,1,0:T(8,128)S(1)}, u32[]{:S(2)}, u32[]{:S(2)}) collective-permute-start(f32[7,8,36]{2,1,0:T(8,128)S(1)} %bitcast.23), channel_id=1, source_target_pairs={{0,1},{1,0},{2,3},{3,2},{4,5},{5,4},{6,7},{7,6},{8,9},{9,8},{10,11... | collective-permute-start | bytes 24200 | tf_op jit(solution)/shard_map/ppermute | solution.py:268
  60.1 18.6 %collective-permute-start.5 = (bf16[512,256]{1,0:T(8,128)(2,1)S(1)}, bf16[512,256]{1,0:T(8,128)(2,1)S(1)}, u32[]{:S(2)}, u32[]{:S(2)}) collective-permute-start(bf16[512,256]{1,0:T(8,128)(2,1)S(1)} %get-tuple-element.14.d_ref), channel_id=1, source_target_pairs={{0,64},{64,128},{128,192},{192,0},{1,65},{65,129},{129,193},{193,1... | collective-permute-start | bytes 786440 | tf_op jit(solution)/shard_map/ppermute | solution.py:273
  80.8 26.7 %copy-start.1 = (bf16[128,448]{0,1:T(8,128)(2,1)S(1)}, bf16[128,448]{0,1:T(8,128)(2,1)}, u32[]{:S(2)}) copy-start(bf16[128,448]{0,1:T(8,128)(2,1)} %param.15) | copy-start | bytes 344068
  80.8 5.1 %collective-permute-start.6 = (bf16[512,128]{1,0:T(8,128)(2,1)S(1)}, bf16[512,128]{1,0:T(8,128)(2,1)S(1)}, u32[]{:S(2)}, u32[]{:S(2)}) collective-permute-start(bf16[512,128]{1,0:T(8,128)(2,1)S(1)} %coeffs.1.own_ref), channel_id=1, source_target_pairs={{0,64},{64,128},{128,192},{192,0},{1,65},{65,129},{129,193},{193,1... | collective-permute-start | bytes 393224 | tf_op jit(solution)/shard_map/ppermute | solution.py:273
  82.0 3.8 %collective-permute-start.7 = (bf16[512,128]{1,0:T(8,128)(2,1)S(1)}, bf16[512,128]{1,0:T(8,128)(2,1)S(1)}, u32[]{:S(2)}, u32[]{:S(2)}) collective-permute-start(bf16[512,128]{1,0:T(8,128)(2,1)S(1)} %coeffs.1.own_ref), channel_id=1, source_target_pairs={{64,0},{128,64},{192,128},{0,192},{65,1},{129,65},{193,129},{1,193... | collective-permute-start | bytes 393224 | tf_op jit(solution)/shard_map/ppermute | solution.py:278

commit v4 on v3

v4 whole, which is shorter than its diff:
```python
import jax
import jax.numpy as jnp
from jax import lax
from jax.experimental import pallas as pl
from jax.experimental.pallas import tpu as pltpu
from jax.sharding import Mesh, PartitionSpec as P

ITERS = 2
Z, Y, C = 8, 4, 2
PLANE = ("z", "y")
CHIPS = Z * Y
F32, BF16, I32 = jnp.float32, jnp.bfloat16, jnp.int32

BD, H, S, M = 8, 36, 7, 448
HC, R, BLK, L = H // C, S * C, 16, 256
LAN = HC * BD
ROWS = CHIPS * BLK
HALF = M // C
SOURCES = 3 * BD
EMPTY = SOURCES * BD


def iota(shape, dim):
    return lax.broadcasted_iota(I32, shape, dim)


def ones(cond):
    return jnp.where(cond, 1.0, 0.0).astype(BF16)


def dot(left, right, dims=(1, 0), exact=False):
    return lax.dot_general(
        left,
        right,
        (((dims[0],), (dims[1],)), ((), ())),
        preferred_element_type=F32,
        precision=lax.Precision.HIGHEST if exact else None,
    )


def shift(rows, cols, start, to, width):
    row, col = iota((rows, cols), 0), iota((rows, cols), 1)
    return ones((row - start == col - to) & (col >= to) & (col < to + width))


def padding():
    row, col = iota((ROWS, M), 0), iota((ROWS, M), 1)
    return ones((col == row - 2 * (row >> 4)) & ((row & 15) < R))


def packing():
    row, col = iota((M, ROWS), 0), iota((M, ROWS), 1)
    return ones((row == col - 2 * (col >> 4)) & ((col & 15) < R))


def two_terms(value):
    high = value.astype(BF16)
    return high, (value - high.astype(F32)).astype(BF16)


def blocks_iota(rows):
    dims = (rows // BLK, BLK, 128)
    return iota(dims, 1), iota(dims, 2)


def packed(field):
    rows = field.shape[0]
    frow, fcol = iota((128, 128), 0), iota((128, 128), 1)
    tail = dot(field[:, 128:].astype(BF16), ones(frow == (fcol & 15))).reshape(-1, BLK, 128)
    row, lane = blocks_iota(rows)
    tail = jnp.where(((lane >> 4) == (row & 7)) & (row < R), tail, 0.0)
    low = jnp.sum(tail[:, :8], axis=1, keepdims=True)
    high = jnp.sum(tail[:, 8:], axis=1, keepdims=True)
    main = field[:, :128].reshape(-1, BLK, 128)
    return jnp.where(row < R, main, jnp.where(row == R, low, high)).astype(BF16)


def unpacked(blocks):
    blocks = blocks.astype(F32)
    row, lane = blocks_iota(ROWS)
    tail = jnp.where(row < 8, blocks[:, R : R + 1], blocks[:, R + 1 :])
    tail = jnp.where(((lane >> 4) == (row & 7)) & (row < R), tail, 0.0)
    frow, fcol = iota((128, 128), 0), iota((128, 128), 1)
    fold = ones((fcol == (frow & 15)) & (fcol < 16))
    tail = dot(tail.reshape(ROWS, 128).astype(BF16), fold)
    main = jnp.where(row < R, blocks, 0.0).reshape(ROWS, 128)
    return jnp.concatenate([main, tail], axis=1).astype(BF16)


def chip_field(own, other, core, exact):
    kind = F32 if exact else BF16
    head, lane = iota((H, L), 0), iota((H, L), 1)
    spread = ones((head == core * HC + (lane >> 3)) & (lane < LAN)).astype(kind)
    row, lane = iota((S * BD, L), 0), iota((S * BD, L), 1)
    total = 0.0
    for value, place in ((own, core), (other, 1 - core)):
        wide = dot(value.reshape(S * BD, H).astype(kind), spread, exact=exact)
        wide = jnp.where((row & 7) == (lane & 7), wide, 0.0)
        to, col = iota((BLK, S * BD), 0), iota((BLK, S * BD), 1)
        gather = ones((col >> 3) == to - S * place).astype(kind)
        total = total + dot(gather, wide.astype(kind), exact=exact)
    return total


def send_kernel(
    where_am_i, source_hbm, target_hbm, live_hbm, t_hbm, d_hbm, begin_hbm, out_ref, begin_ref, t_ref, d_ref,
    source, target, live, sems
):
    moves = ((d_hbm, d_ref), (t_hbm.at[0], t_ref.at[0]), (t_hbm.at[1], t_ref.at[1]), (begin_hbm, begin_ref))
    moves += ((source_hbm, source), (target_hbm, target), (live_hbm, live))
    copies = [pltpu.make_async_copy(a, b, sems.at[i]) for i, (a, b) in enumerate(moves)]
    for copy in copies:
        copy.start()
    buoy = where_am_i[1]
    pad, pack = padding(), packing()
    row, col = iota((M, L), 0), iota((M, L), 1)
    half = ones((row == HALF * (buoy & 1) + col - 2 * (col >> 4)) & ((col & 15) < R))
    to, line = iota((BLK, S), 0), iota((BLK, S), 1)
    brow, blane = iota((BLK, L), 0), iota((BLK, L), 1)
    for i in (0, 4, 5, 6):
        copies[i].wait()
    number = 0.0
    for k in range(2):
        at = (source[k] - (buoy - 1) * BD) * BD + target[k] - buoy * BD
        at = jnp.where(live[k] == 1, jnp.clip(at, 0, EMPTY), EMPTY)
        number = jnp.where((brow == BLK - 1) & (blane == k), at.astype(F32), number)
    own = dot(d_ref[...], half).astype(BF16)
    for p in range(2):
        copies[1 + p].wait()
        wide = dot(t_ref[p], pack).astype(BF16)
        for k in range(2):
            spare = ((to == R) & (line == 2 * p + k)) | ((to == R + 1) & (line == 4 + 2 * p + k))
            extra = dot(ones(spare), own)
            if p == 1 and k == 1:
                extra = extra + number
            part = dot(pad, wide[:, L * k : L * (k + 1)]).reshape(CHIPS, BLK, L) + extra[None]
            at = 512 * p + L * k
            out_ref[:, :, at : at + L] = part.astype(BF16)
    copies[3].wait()


def gaps(p, rows, dim):
    dims = (rows, 128) if dim == 0 else (128, rows)
    place, lane = iota(dims, dim), iota(dims, 1 - dim)
    return ones((lane == 64 * p + 2 * (place >> 4) + (place & 15) - R) & ((place & 15) >= R))


def begin_kernel(where_am_i, own_ref, other_ref, in_ref, out_ref):
    del in_ref
    field = chip_field(own_ref[...], other_ref[...], where_am_i[0], False)
    block = packed(field).reshape(BLK, 128)
    for p in range(2):
        extra = dot(block, gaps(p, 512, 1)).astype(BF16)
        at = 512 * p
        out_ref[:, :, at : at + 512] = out_ref[:, :, at : at + 512] + extra[None]


def first_kernel(in_ref, out_ref):
    block = 0.0
    for p in range(2):
        part = in_ref[:, :, 512 * p : 512 * (p + 1)].reshape(ROWS, 512)
        block = block + dot(part, gaps(p, 512, 0))
    out_ref[...] = block.reshape(CHIPS, BLK, 128).astype(BF16)


def place_kernel(
    where_am_i, own_at, other_at, in_ref, other_ref, amb_ref, amb_other_ref, w_ref, a_ref, d_ref
):
    core = where_am_i[0]
    w_ref[...] = jnp.zeros_like(w_ref)
    for j in range(CHIPS):
        for p in range(2):
            w_ref[own_at[j, 0, p]] = in_ref[j, :, 512 * p : 512 * (p + 1)]
            w_ref[other_at[j, 0, p]] = other_ref[j, :, 512 * p : 512 * (p + 1)]
    a_ref[...] = chip_field(amb_ref[...], amb_other_ref[...], core, True)
    to, col = iota((ROWS, CHIPS * 8), 0), iota((ROWS, CHIPS * 8), 1)
    key = jnp.where((to >> 4) == (col >> 3), (to & 15) * 8 + (col & 7), -1)
    total = 0.0
    for ref, place in ((in_ref, core), (other_ref, 1 - core)):
        for q in range(4):
            part = ref[:, 8:, L * q : L * (q + 1)].reshape(CHIPS * 8, L)
            pick = key == 8 * (S * place + q) + 6
            if q < 3:
                pick = pick | (key == 8 * (S * place + q + 4) + 7)
            total = total + dot(ones(pick), part)
    d_ref[...] = total.astype(BF16)


def weighted(w_ref, group, field):
    lane = iota((BD * BLK, L), 1)
    total = jnp.zeros((BD * BLK, L), F32)
    for b in range(BD):
        part = dot(w_ref[BD * group + b], field)
        total = total + jnp.where((lane & 7) == b, part, 0.0)
    return total


def own_kernel(w_ref, own_ref, out_ref):
    out_ref[...] = weighted(w_ref, 1, unpacked(own_ref[...]))


def incident_kernel(w_ref, low_ref, high_ref, part_ref, a_ref, out_ref):
    total = part_ref[...]
    total = total + weighted(w_ref, 0, unpacked(low_ref[...]))
    total = total + weighted(w_ref, 2, unpacked(high_ref[...]))
    row, col = iota((L, L), 0), iota((L, L), 1)
    same = ones(((row >> 3) == (col >> 3)) & (row < LAN))
    high, rest = two_terms(total)
    total = dot(high, same) + dot(rest, same)
    row, lane = iota((BLK, L), 0), iota((BLK, L), 1)
    mine = a_ref[...]
    for t in range(BD):
        mine = mine + jnp.where((lane & 7) == t, total[BLK * t : BLK * (t + 1)], 0.0)
    mine = jnp.where((row < R) & (lane < LAN), mine, 0.0)
    out_ref[...] = jnp.broadcast_to(packed(mine), (CHIPS, BLK, 128))


def coeffs_kernel(where_am_i, in_ref, d_ref, d_other_ref, out_ref):
    field = unpacked(in_ref[...])
    even = (where_am_i[1] & 1) == 0
    upper, lower = field[:L].astype(F32), field[L:].astype(F32)
    first = jnp.where(even, upper, lower).astype(BF16)
    second = jnp.where(even, lower, upper).astype(BF16)
    out_ref[...] = packed(dot(d_ref[...], first) + dot(d_other_ref[...], second))


def ready_kernel(p_ref, d_ref, p_out, d_out, lanes_out):
    p_out[...] = dot(padding(), p_ref[...]).astype(BF16)
    d_out[...] = dot(d_ref[...], packing()).astype(BF16)
    row, col = iota((L, BD * 128), 0), iota((L, BD * 128), 1)
    to = (row & 7) * 128 + (row >> 3)
    for c in range(C):
        lanes_out[c] = ones((col == to + HC * c) & (row < LAN))


def last_kernel(in_ref, p_ref, d_ref, lanes_ref, src_ref, out_ref):
    out = 0.0
    for c in range(C):
        field = unpacked(in_ref[c])
        part = dot(field, p_ref[...], dims=(0, 0))
        src_ref[LAN * c : LAN * (c + 1), :] = part[:LAN].astype(BF16)
        value = dot(d_ref[...], field)
        for _ in range(3):
            term = value.astype(BF16)
            value = value - term.astype(F32)
            out = out + dot(term, lanes_ref[c])
    for b in range(BD):
        out_ref[:, b, :] = out[:, 128 * b : 128 * b + H]


VM = pl.BlockSpec(memory_space=pltpu.VMEM)
SM = pl.BlockSpec(memory_space=pltpu.SMEM)
HBM = pl.BlockSpec(memory_space=pltpu.HBM)


def call(kernel, scalars, arrays, shapes, name, **kwargs):
    return pl.pallas_call(
        kernel,
        out_shape=shapes,
        in_specs=[SM] * len(scalars) + [VM] * len(arrays),
        out_specs=[VM] * len(shapes) if isinstance(shapes, tuple) else VM,
        compiler_params=pltpu.CompilerParams(vmem_limit_bytes=40 << 20),
        name=name,
        **kwargs,
    )(*scalars, *arrays)


def shape(*dims, dtype=BF16):
    return jax.ShapeDtypeStruct(dims, dtype)


def exchange(blocks):
    return lax.all_to_all(blocks, PLANE, 0, 0, tiled=True)


def swapped(value):
    return lax.ppermute(value, "c", [(0, 1), (1, 0)])


def from_previous(value):
    count = lax.axis_size("x")
    return lax.ppermute(value, "x", [(i, (i + 1) % count) for i in range(count)])


def from_next(value):
    count = lax.axis_size("x")
    return lax.ppermute(value, "x", [((i + 1) % count, i) for i in range(count)])


def slot_numbers(blocks):
    return blocks[:, BLK - 1 :, 768:770].astype(I32)


def shards(
    ambient, initial_out, translation, pair_source, pair_target, pair_live, diffract, panel_rows
):
    where_am_i = jnp.stack([lax.axis_index("c"), lax.axis_index("x")]).astype(I32)
    begin = initial_out.transpose(2, 0, 1)
    waves = ambient.transpose(2, 0, 1)
    begin_other = swapped(begin)
    waves_other = swapped(waves)
    message, begin = pl.pallas_call(
        send_kernel,
        out_shape=(shape(CHIPS, BLK, 1024), shape(*begin.shape, dtype=F32)),
        in_specs=[SM] + [HBM] * 6,
        out_specs=[VM] * 2,
        scratch_shapes=[
            pltpu.VMEM(translation.shape, BF16),
            pltpu.VMEM(diffract.shape, BF16),
            pltpu.SMEM(pair_source.shape, I32),
            pltpu.SMEM(pair_source.shape, I32),
            pltpu.SMEM(pair_source.shape, I32),
            pltpu.SemaphoreType.DMA((7,)),
        ],
        compiler_params=pltpu.CompilerParams(vmem_limit_bytes=40 << 20),
        name="send",
    )(
        where_am_i,
        *[
            pltpu.with_memory_space_constraint(value, pltpu.HBM)
            for value in (pair_source, pair_target, pair_live, translation, diffract, begin)
        ],
    )
    message, waves_other = lax.optimization_barrier((message, waves_other))
    message = call(
        begin_kernel,
        (where_am_i,),
        (begin, begin_other, message),
        shape(CHIPS, BLK, 1024),
        "begin",
        input_output_aliases={3: 0},
    )
    got = exchange(message)
    got, waves = lax.optimization_barrier((got, waves))
    coeffs = call(first_kernel, (), (got,), shape(CHIPS, BLK, 128), "first")
    low, high = from_previous(coeffs), from_next(coeffs)
    got_other = swapped(got)
    matrices, own_waves, half = call(
        place_kernel,
        (where_am_i, slot_numbers(got), slot_numbers(got_other)),
        (got, got_other, waves, waves_other),
        (shape(EMPTY + BD, BLK, 512), shape(BLK, L, dtype=F32), shape(ROWS, L)),
        "place",
    )
    matrices = matrices.reshape(SOURCES + 1, BD * BLK, 512)
    other_half = from_previous(half)

    for step in range(ITERS):
        if step:
            coeffs = call(
                coeffs_kernel,
                (where_am_i,),
                (got, half, other_half),
                shape(CHIPS, BLK, 128),
                "coeffs",
            )
            low, high = from_previous(coeffs), from_next(coeffs)
            coeffs, panel_rows, diffract = lax.optimization_barrier((coeffs, panel_rows, diffract))
            ready = call(
                ready_kernel,
                (),
                (panel_rows.T, diffract),
                (shape(ROWS, panel_rows.shape[0]), shape(S, ROWS), shape(C, L, BD * 128)),
                "ready",
            )
            low, ready = lax.optimization_barrier((low, ready))
        part = call(own_kernel, (), (matrices, coeffs), shape(BD * BLK, L, dtype=F32), "own")
        message = call(
            incident_kernel,
            (),
            (matrices, low, high, part, own_waves),
            shape(CHIPS, BLK, 128),
            "incident",
        )
        got = exchange(message)
    whole = lax.all_gather(got, "c", axis=0, tiled=False)
    sources, outgoing = call(
        last_kernel,
        (),
        (whole, *ready),
        (shape(H * BD, panel_rows.shape[0]), shape(S, BD, H, dtype=F32)),
        "last",
    )
    sources = sources.reshape(H, BD, panel_rows.shape[0]).transpose(1, 0, 2)
    return outgoing.transpose(1, 2, 0), sources


def solution(mesh):
    fine = Mesh(mesh.devices.reshape(mesh.shape["buoy"], Z, Y, C), ("x", "z", "y", "c"))
    dom = ("z", "y", "c")
    in_specs = (
        P("x", None, dom),
        P("x", None, dom),
        P(("x",) + dom, None, None),
        P(("x",) + dom),
        P(("x",) + dom),
        P(("x",) + dom),
        P(dom, None),
        P(dom, None),
    )
    out_specs = (P("x", None, dom), P("x", None, dom))
    return jax.shard_map(shards, mesh=fine, in_specs=in_specs, out_specs=out_specs, check_vma=False)
```

time: 111 us -> 98.3 us (0.89)
  Pallas kernels: 21.8 us -> 14.8 us
  local copies, waits for them, and re-layouts: 4.59 us -> 0.01 us
    pallas_call x9 -> x10, Pallas kernels: 18.4 us -> 11.6 us  [call(): pl.pallas_call(kernel, out_shape=shapes, in_specs=[SM] * len(scalars) + [...]
    unnamed x16 -> x6, local copies, waits for them, and re-layouts: 4.59 us -> 0.01 us
  transfers between devices with their start and end apart: 8 -> 8, of which waited for: 2 -> 2; matrix products, arithmetic and copies ran while one was open for 0% -> 0% of each run, Pallas kernels for 8% -> 6%
where the time goes in v4:
time: 98.3 us; the launch traced here: 98.1 us
  blocking collectives  69 us (70%)
  Pallas kernels  14.8 us (15%)
  starting transfers between devices  12 us (12%)
  waiting for transfers between devices  1.36 us (1%)
    all_to_all x3, blocking collectives, exchange(): return lax.all_to_all(blocks, PLANE, 0, 0, tiled=True)  62.6 us
    pallas_call x10, Pallas kernels, call(): pl.pallas_call(kernel, out_shape=shapes, in_specs=[SM] * len(scalars) + [...  11.6 us
    all_gather x1, blocking collectives, shards(): whole = lax.all_gather(got, 'c', axis=0, tiled=False)  6.38 us
    ppermute x3, starting transfers between devices, swapped(): return lax.ppermute(value, 'c', [(0, 1), (1, 0)])  6.17 us
    pallas_call x1, Pallas kernels, shards(): pl.pallas_call(send_kernel, out_shape=(shape(CHIPS, BLK, 1024), shape(*be...  3.19 us
    ppermute x2, starting transfers between devices, from_next(): lax.ppermute(value, 'x', [((i + 1) % count, i) for i in range(count)])  3.03 us
    ppermute x3, starting transfers between devices, from_previous(): lax.ppermute(value, 'x', [(i, (i + 1) % count) for i in range(count)])  2.8 us
  transfers between devices with their start and end apart: 8, of which 2 were waited for; matrix products, arithmetic and copies ran while one was open for 0% of the time, Pallas kernels for 6%

profile of v4, /device:TPU:1, one launch (start us, length us, event | category | flops | bytes accessed | tf_op | source)
XLA Modules:
  0.0 98.1 jit_solution(9674612665332938824)
XLA Ops:
  0.6 3.3 %collective-permute-start.1 = (f32[7,8,36]{2,1,0:T(8,128)}, f32[7,8,36]{2,1,0:T(8,128)S(1)}, u32[]{:S(2)}, u32[]{:S(2)}) collective-permute-start(f32[7,8,36]{2,1,0:T(8,128)} %bitcast.17), channel_id=1, source_target_pairs={{0,1},{1,0},{2,3},{3,2},{4,5},{5,4},{6,7},{7,6},{8,9},{9,8},{10,11... | collective-permute-start | bytes 24200 | tf_op jit(solution)/shard_map/ppermute | solution.py:277
  4.0 0.1 collective-permute-start
  4.1 0.1 pad_add_fusion.where_am_i
  4.1 3.2 %send.1 = (bf16[32,16,1024]{2,1,0:T(8,128)(2,1)S(1)}, f32[7,8,36]{2,1,0:T(8,128)S(1)}) custom-call(s32[2]{0:T(128)S(1)} %pad_add_fusion.where_am_i, s32[2]{0:T(128)} %source_hbm.1, s32[2]{0:T(128)} %target_hbm.1, s32[2]{0:T(128)} %live_hbm.1, bf16[2,448,448]{2,1,0:T(8,128)(2,1)} %t_hbm.1, bf16[7,448]{1,0:T(8,128)(2,1)} %d_ref, f32[7,8,36]{2,1,0:T(8,128)} %bitcast.20), custom_call_target="tpu_custom_call" | custom-call | tf_op jit(solution)/shard_map/send/pallas_call | solution.py:302
  7.3 0.0 collective-permute-done.1.amb_other_ref
  7.4 0.0 collective-permute-done.other_ref
  7.4 1.2 %begin.1 = bf16[32,16,1024]{2,1,0:T(8,128)(2,1)S(1)} custom-call(s32[2]{0:T(128)S(1)} %pad_add_fusion.where_am_i, f32[7,8,36]{2,1,0:T(8,128)S(1)} %get-tuple-element.23.own_ref, f32[7,8,36]{2,1,0:T(8,128)S(1)} %collective-permute-done.other_ref, bf16[32,16,1024]{2,1,0:T(8,128)(2,1)S(1)} %get-tuple-element.25.in_ref), custom_call_target="tpu_custom_call", output_to_operand_aliasing={{}: (3, {})} | custom-call | tf_op jit(solution)/shard_map/begin/pallas_call | solution.py:257
  8.5 35.5 %all_to_all.15.in_ref = bf16[32,16,1024]{2,1,0:T(8,128)(2,1)S(1)} all-to-all(bf16[32,16,1024]{2,1,0:T(8,128)(2,1)S(1)} %begin.1), channel_id=1, replica_groups=mesh['x'=4,'z'=8,'y'=4,'c'=2] {'z','y'}, dimensions={0} | all-to-all | bytes 2097152 | tf_op jit(solution)/shard_map/all_to_all | solution.py:273
  44.1 2.7 %collective-permute-start.2 = (bf16[32,16,1024]{2,1,0:T(8,128)(2,1)S(1)}, bf16[32,16,1024]{2,1,0:T(8,128)(2,1)S(1)}, u32[]{:S(2)}, u32[]{:S(2)}) collective-permute-start(bf16[32,16,1024]{2,1,0:T(8,128)(2,1)S(1)} %all_to_all.15.in_ref), channel_id=1, source_target_pairs={{0,1},{1,0},{2,3},{3,2},{4,5},{5,4},{6,7},{7,6},{8,9},{9,8},{10,11... | collective-permute-start | bytes 3145736 | tf_op jit(solution)/shard_map/ppermute | solution.py:277
  46.8 0.4 first.1.own_ref
  47.3 1.3 %collective-permute-start.3 = (bf16[32,16,128]{2,1,0:T(8,128)(2,1)S(1)}, bf16[32,16,128]{2,1,0:T(8,128)(2,1)S(1)}, u32[]{:S(2)}, u32[]{:S(2)}) collective-permute-start(bf16[32,16,128]{2,1,0:T(8,128)(2,1)S(1)} %first.1.own_ref), channel_id=1, source_target_pairs={{0,64},{64,128},{128,192},{192,0},{1,65},{65,129},{129,193},{193,1... | collective-permute-start | bytes 393224 | tf_op jit(solution)/shard_map/ppermute | solution.py:282
  48.6 1.5 %collective-permute-start.4 = (bf16[32,16,128]{2,1,0:T(8,128)(2,1)S(1)}, bf16[32,16,128]{2,1,0:T(8,128)(2,1)S(1)}, u32[]{:S(2)}, u32[]{:S(2)}) collective-permute-start(bf16[32,16,128]{2,1,0:T(8,128)(2,1)S(1)} %first.1.own_ref), channel_id=1, source_target_pairs={{64,0},{128,64},{192,128},{0,192},{65,1},{129,65},{193,129},{1,193... | collective-permute-start | bytes 393224 | tf_op jit(solution)/shard_map/ppermute | solution.py:287
  50.1 0.0 collective-permute-done.2.other_ref
  50.1 2.5 %place.1 = (bf16[200,16,512]{2,1,0:T(8,128)(2,1)S(1)}, f32[16,256]{1,0:T(8,128)S(1)}, bf16[512,256]{1,0:T(8,128)(2,1)S(1)}) custom-call(s32[2]{0:T(128)S(1)} %pad_add_fusion.where_am_i, s32[32,1,2]{2,1,0:T(1,128)S(1)} %slice_convert_fusion.1.own_at, s32[32,1,2]{2,1,0:T(1,128)S(1)} %slice_convert_fusion.other_at, ...), custom_call_target="tpu_custom_call" | custom-call | tf_op jit(solution)/shard_map/place/pallas_call | solution.py:257
  52.6 0.3 collective-permute-start.5
  53.0 0.6 own.2.part_ref
  53.6 0.1 collective-permute-done.3.low_ref
  53.7 0.0 collective-permute-done.4.high_ref
  53.7 1.4 %incident.2 = bf16[32,16,128]{2,1,0:T(8,128)(2,1)S(1)} custom-call(bf16[25,128,512]{2,1,0:T(8,128)(2,1)S(1)} %bitcast.12, bf16[32,16,128]{2,1,0:T(8,128)(2,1)S(1)} %collective-permute-done.3.low_ref, bf16[32,16,128]{2,1,0:T(8,128)(2,1)S(1)} %collective-permute-done.4.high_ref, f32[128,256]{1,0:T(8,128)S(1)} %own.2.part_ref, ...), custom_call_target="tpu_custom_call" | custom-call | tf_op jit(solution)/shard_map/incident/pallas_call | solution.py:257
  55.1 14.5 %all_to_all.16.in_ref = bf16[32,16,128]{2,1,0:T(8,128)(2,1)S(1)} all-to-all(bf16[32,16,128]{2,1,0:T(8,128)(2,1)S(1)} %incident.2), channel_id=1, replica_groups=mesh['x'=4,'z'=8,'y'=4,'c'=2] {'z','y'}, dimensions={0} | all-to-all | bytes 262144 | tf_op jit(solution)/shard_map/all_to_all | solution.py:273
  69.5 0.0 collective-permute-done.5.d_other_ref
  69.5 1.2 %coeffs.1.own_ref = bf16[32,16,128]{2,1,0:T(8,128)(2,1)S(1)} custom-call(s32[2]{0:T(128)S(1)} %pad_add_fusion.where_am_i, bf16[32,16,128]{2,1,0:T(8,128)(2,1)S(1)} %all_to_all.16.in_ref, bf16[512,256]{1,0:T(8,128)(2,1)S(1)} %get-tuple-element.31.d_ref, bf16[512,256]{1,0:T(8,128)(2,1)S(1)} %collective-permute-done.5.d_other_ref), custom_call_target="tpu_custom_call" | custom-call | tf_op jit(solution)/shard_map/coeffs/pallas_call | solution.py:257
  70.7 1.2 %collective-permute-start.6 = (bf16[32,16,128]{2,1,0:T(8,128)(2,1)S(1)}, bf16[32,16,128]{2,1,0:T(8,128)(2,1)S(1)}, u32[]{:S(2)}, u32[]{:S(2)}) collective-permute-start(bf16[32,16,128]{2,1,0:T(8,128)(2,1)S(1)} %coeffs.1.own_ref), channel_id=1, source_target_pairs={{0,64},{64,128},{128,192},{192,0},{1,65},{65,129},{129,193},{193,1... | collective-permute-start | bytes 393224 | tf_op jit(solution)/shard_map/ppermute | solution.py:282
  71.9 1.6 %collective-permute-start.7 = (bf16[32,16,128]{2,1,0:T(8,128)(2,1)S(1)}, bf16[32,16,128]{2,1,0:T(8,128)(2,1)S(1)}, u32[]{:S(2)}, u32[]{:S(2)}) collective-permute-start(bf16[32,16,128]{2,1,0:T(8,128)(2,1)S(1)} %coeffs.1.own_ref), channel_id=1, source_target_pairs={{64,0},{128,64},{192,128},{0,192},{65,1},{129,65},{193,129},{1,193... | collective-permute-start | bytes 393224 | tf_op jit(solution)/shard_map/ppermute | solution.py:287
  73.5 0.6 own.3.part_ref
  74.1 0.5 ready.1
  74.6 1.2 %collective-permute-done.6.low_ref = bf16[32,16,128]{2,1,0:T(8,128)(2,1)S(1)} collective-permute-done((bf16[32,16,128]{2,1,0:T(8,128)(2,1)S(1)}, bf16[32,16,128]{2,1,0:T(8,128)(2,1)S(1)}, u32[]{:S(2)}, u32[]{:S(2)}) %collective-permute-start.6) | collective-permute-done | bytes 131104 | tf_op jit(solution)/shard_map/ppermute | solution.py:282
  75.8 0.0 collective-permute-done.7.high_ref
  75.8 1.4 %incident.3 = bf16[32,16,128]{2,1,0:T(8,128)(2,1)S(1)} custom-call(bf16[25,128,512]{2,1,0:T(8,128)(2,1)S(1)} %bitcast.14, bf16[32,16,128]{2,1,0:T(8,128)(2,1)S(1)} %collective-permute-done.6.low_ref, bf16[32,16,128]{2,1,0:T(8,128)(2,1)S(1)} %collective-permute-done.7.high_ref, f32[128,256]{1,0:T(8,128)S(1)} %own.3.part_ref, ...), custom_call_target="tpu_custom_call" | custom-call | tf_op jit(solution)/shard_map/incident/pallas_call | solution.py:257
  77.2 12.6 %all_to_all.17 = bf16[32,16,128]{2,1,0:T(8,128)(2,1)S(1)} all-to-all(bf16[32,16,128]{2,1,0:T(8,128)(2,1)S(1)} %incident.3), channel_id=1, replica_groups=mesh['x'=4,'z'=8,'y'=4,'c'=2] {'z','y'}, dimensions={0} | all-to-all | bytes 262144 | tf_op jit(solution)/shard_map/all_to_all | solution.py:273
  89.9 6.4 %all-gather = bf16[64,16,128]{2,1,0:T(8,128)(2,1)S(1)} all-gather(bf16[32,16,128]{2,1,0:T(8,128)(2,1)S(1)} %all_to_all.17), channel_id=2, replica_groups=mesh['x'=4,'z'=8,'y'=4,'c'=2] {'c'}, dimensions={0}, use_global_device_ids=true | all-gather | bytes 393216 | tf_op jit(solution)/shard_map/all_gather | solution.py:376
  96.2 1.9 %last.1 = (bf16[288,128]{1,0:T(8,128)(2,1)}, f32[7,8,36]{2,1,0:T(8,128)}) custom-call(bf16[2,32,16,128]{3,2,1,0:T(8,128)(2,1)S(1)} %bitcast.15, bf16[512,128]{1,0:T(8,128)(2,1)S(1)} %get-tuple-element.39.p_ref, bf16[7,512]{1,0:T(8,128)(2,1)S(1)} %get-tuple-element.40.d_ref, bf16[2,256,1024]{2,1,0:T(8,128)(2,1)S(1)} %get-tuple-element.41.lanes_ref), custom_call_target="tpu_custom_call" | custom-call | tf_op jit(solution)/shard_map/last/pallas_call | solution.py:257
  (8 shorter events, 0.1 us)
Async XLA Ops:
  0.6 49.5 %copy-start.2 = (f32[8,36,7]{1,0,2:T(8,128)S(1)}, f32[8,36,7]{1,0,2:T(8,128)}, u32[]{:S(2)}) copy-start(f32[8,36,7]{1,0,2:T(8,128)} %param.8) | copy-start | bytes 24196
  0.6 6.7 %collective-permute-start.1 = (f32[7,8,36]{2,1,0:T(8,128)}, f32[7,8,36]{2,1,0:T(8,128)S(1)}, u32[]{:S(2)}, u32[]{:S(2)}) collective-permute-start(f32[7,8,36]{2,1,0:T(8,128)} %bitcast.17), channel_id=1, source_target_pairs={{0,1},{1,0},{2,3},{3,2},{4,5},{5,4},{6,7},{7,6},{8,9},{9,8},{10,11... | collective-permute-start | bytes 24200 | tf_op jit(solution)/shard_map/ppermute | solution.py:277
  4.0 3.4 %collective-permute-start = (f32[7,8,36]{2,1,0:T(8,128)}, f32[7,8,36]{2,1,0:T(8,128)S(1)}, u32[]{:S(2)}, u32[]{:S(2)}) collective-permute-start(f32[7,8,36]{2,1,0:T(8,128)} %bitcast.19), channel_id=1, source_target_pairs={{0,1},{1,0},{2,3},{3,2},{4,5},{5,4},{6,7},{7,6},{8,9},{9,8},{10,11... | collective-permute-start | bytes 24200 | tf_op jit(solution)/shard_map/ppermute | solution.py:277
  44.1 6.0 %collective-permute-start.2 = (bf16[32,16,1024]{2,1,0:T(8,128)(2,1)S(1)}, bf16[32,16,1024]{2,1,0:T(8,128)(2,1)S(1)}, u32[]{:S(2)}, u32[]{:S(2)}) collective-permute-start(bf16[32,16,1024]{2,1,0:T(8,128)(2,1)S(1)} %all_to_all.15.in_ref), channel_id=1, source_target_pairs={{0,1},{1,0},{2,3},{3,2},{4,5},{5,4},{6,7},{7,6},{8,9},{9,8},{10,11... | collective-permute-start | bytes 3145736 | tf_op jit(solution)/shard_map/ppermute | solution.py:277
  47.3 6.4 %collective-permute-start.3 = (bf16[32,16,128]{2,1,0:T(8,128)(2,1)S(1)}, bf16[32,16,128]{2,1,0:T(8,128)(2,1)S(1)}, u32[]{:S(2)}, u32[]{:S(2)}) collective-permute-start(bf16[32,16,128]{2,1,0:T(8,128)(2,1)S(1)} %first.1.own_ref), channel_id=1, source_target_pairs={{0,64},{64,128},{128,192},{192,0},{1,65},{65,129},{129,193},{193,1... | collective-permute-start | bytes 393224 | tf_op jit(solution)/shard_map/ppermute | solution.py:282
  48.6 5.1 %collective-permute-start.4 = (bf16[32,16,128]{2,1,0:T(8,128)(2,1)S(1)}, bf16[32,16,128]{2,1,0:T(8,128)(2,1)S(1)}, u32[]{:S(2)}, u32[]{:S(2)}) collective-permute-start(bf16[32,16,128]{2,1,0:T(8,128)(2,1)S(1)} %first.1.own_ref), channel_id=1, source_target_pairs={{64,0},{128,64},{192,128},{0,192},{65,1},{129,65},{193,129},{1,193... | collective-permute-start | bytes 393224 | tf_op jit(solution)/shard_map/ppermute | solution.py:287
  52.6 16.9 %collective-permute-start.5 = (bf16[512,256]{1,0:T(8,128)(2,1)S(1)}, bf16[512,256]{1,0:T(8,128)(2,1)S(1)}, u32[]{:S(2)}, u32[]{:S(2)}) collective-permute-start(bf16[512,256]{1,0:T(8,128)(2,1)S(1)} %get-tuple-element.31.d_ref), channel_id=1, source_target_pairs={{0,64},{64,128},{128,192},{192,0},{1,65},{65,129},{129,193},{193,1... | collective-permute-start | bytes 786440 | tf_op jit(solution)/shard_map/ppermute | solution.py:282
  53.7 20.4 %copy-start = (bf16[128,448]{0,1:T(8,128)(2,1)S(1)}, bf16[128,448]{0,1:T(8,128)(2,1)}, u32[]{:S(2)}) copy-start(bf16[128,448]{0,1:T(8,128)(2,1)} %param.15) | copy-start | bytes 344068
  53.7 20.4 %copy-start.1 = (bf16[7,448]{1,0:T(8,128)(2,1)S(1)}, bf16[7,448]{1,0:T(8,128)(2,1)}, u32[]{:S(2)}) copy-start(bf16[7,448]{1,0:T(8,128)(2,1)} %d_ref) | copy-start | bytes 18820
  70.7 5.1 %collective-permute-start.6 = (bf16[32,16,128]{2,1,0:T(8,128)(2,1)S(1)}, bf16[32,16,128]{2,1,0:T(8,128)(2,1)S(1)}, u32[]{:S(2)}, u32[]{:S(2)}) collective-permute-start(bf16[32,16,128]{2,1,0:T(8,128)(2,1)S(1)} %coeffs.1.own_ref), channel_id=1, source_target_pairs={{0,64},{64,128},{128,192},{192,0},{1,65},{65,129},{129,193},{193,1... | collective-permute-start | bytes 393224 | tf_op jit(solution)/shard_map/ppermute | solution.py:282
  71.9 3.9 %collective-permute-start.7 = (bf16[32,16,128]{2,1,0:T(8,128)(2,1)S(1)}, bf16[32,16,128]{2,1,0:T(8,128)(2,1)S(1)}, u32[]{:S(2)}, u32[]{:S(2)}) collective-permute-start(bf16[32,16,128]{2,1,0:T(8,128)(2,1)S(1)} %coeffs.1.own_ref), channel_id=1, source_target_pairs={{64,0},{128,64},{192,128},{0,192},{65,1},{129,65},{193,129},{1,193... | collective-permute-start | bytes 393224 | tf_op jit(solution)/shard_map/ppermute | solution.py:287

commit v5 on v4

--- a/solution.py
+++ b/solution.py
@@ -173,17 +173,22 @@
             w_ref[own_at[j, 0, p]] = in_ref[j, :, 512 * p : 512 * (p + 1)]
             w_ref[other_at[j, 0, p]] = other_ref[j, :, 512 * p : 512 * (p + 1)]
     a_ref[...] = chip_field(amb_ref[...], amb_other_ref[...], core, True)
-    to, col = iota((ROWS, CHIPS * 8), 0), iota((ROWS, CHIPS * 8), 1)
-    key = jnp.where((to >> 4) == (col >> 3), (to & 15) * 8 + (col & 7), -1)
-    total = 0.0
-    for ref, place in ((in_ref, core), (other_ref, 1 - core)):
-        for q in range(4):
-            part = ref[:, 8:, L * q : L * (q + 1)].reshape(CHIPS * 8, L)
-            pick = key == 8 * (S * place + q) + 6
-            if q < 3:
-                pick = pick | (key == 8 * (S * place + q + 4) + 7)
-            total = total + dot(ones(pick), part)
-    d_ref[...] = total.astype(BF16)
+    part_rows, width = 8 * BLK, 4 * 64
+    to, col = iota((part_rows, width), 0), iota((part_rows, width), 1)
+    line = (to & 15) - (col >> 6)
+    picks = []
+    for place in (core, 1 - core):
+        upper = (line == S * place) & ((col & 7) == 6)
+        lower = (line == S * place + 4) & ((col & 7) == 7) & ((col >> 6) < 3)
+        picks.append(ones(((to >> 4) == ((col >> 3) & 7)) & (upper | lower)))
+    for g in range(CHIPS // 8):
+        total = 0.0
+        for ref, pick in zip((in_ref, other_ref), picks):
+            cells = [
+                ref[8 * g : 8 * (g + 1), 8:, L * q : L * (q + 1)].reshape(64, L) for q in range(4)
+            ]
+            total = total + dot(pick, jnp.concatenate(cells, axis=0))
+        d_ref[part_rows * g : part_rows * (g + 1), :] = total.astype(BF16)
 
 
 def weighted(w_ref, group, field):
@@ -215,13 +220,16 @@
     out_ref[...] = jnp.broadcast_to(packed(mine), (CHIPS, BLK, 128))
 
 
-def coeffs_kernel(where_am_i, in_ref, d_ref, d_other_ref, out_ref):
-    field = unpacked(in_ref[...])
+def product_kernel(where_am_i, w_ref, d_ref, d_other_ref, out_ref):
     even = (where_am_i[1] & 1) == 0
-    upper, lower = field[:L].astype(F32), field[L:].astype(F32)
-    first = jnp.where(even, upper, lower).astype(BF16)
-    second = jnp.where(even, lower, upper).astype(BF16)
-    out_ref[...] = packed(dot(d_ref[...], first) + dot(d_other_ref[...], second))
+    own, other = d_ref[...].astype(F32), d_other_ref[...].astype(F32)
+    halves = (
+        jnp.where(even, own, other).astype(BF16),
+        jnp.where(even, other, own).astype(BF16),
+    )
+    for s in range(SOURCES):
+        for k in range(2):
+            out_ref[s, :, L * k : L * (k + 1)] = dot(w_ref[s], halves[k]).astype(BF16)
 
 
 def ready_kernel(p_ref, d_ref, p_out, d_out, lanes_out):
@@ -233,17 +241,25 @@
         lanes_out[c] = ones((col == to + HC * c) & (row < LAN))
 
 
-def last_kernel(in_ref, p_ref, d_ref, lanes_ref, src_ref, out_ref):
-    out = 0.0
-    for c in range(C):
-        field = unpacked(in_ref[c])
-        part = dot(field, p_ref[...], dims=(0, 0))
-        src_ref[LAN * c : LAN * (c + 1), :] = part[:LAN].astype(BF16)
-        value = dot(d_ref[...], field)
-        for _ in range(3):
-            term = value.astype(BF16)
-            value = value - term.astype(F32)
-            out = out + dot(term, lanes_ref[c])
+def outputs(blocks, p_ref, d_ref, lanes):
+    field = unpacked(blocks)
+    sources = dot(field, p_ref[...], dims=(0, 0))[:LAN].astype(BF16)
+    high, rest = two_terms(dot(d_ref[...], field))
+    return sources, dot(high, lanes) + dot(rest, lanes)
+
+
+def last_own_kernel(where_am_i, in_ref, p_ref, d_ref, lanes_ref, src_ref, out_ref):
+    src_ref[...], out_ref[...] = outputs(in_ref[...], p_ref, d_ref, lanes_ref[where_am_i[0]])
+
+
+def last_kernel(
+    where_am_i, in_ref, p_ref, d_ref, lanes_ref, own_src_ref, own_out_ref, src_ref, out_ref
+):
+    core = where_am_i[0]
+    other, out = outputs(in_ref[...], p_ref, d_ref, lanes_ref[1 - core])
+    out = out + own_out_ref[...]
+    src_ref[pl.ds(pl.multiple_of(LAN * core, BLK), LAN), :] = own_src_ref[...]
+    src_ref[pl.ds(pl.multiple_of(LAN * (1 - core), BLK), LAN), :] = other
     for b in range(BD):
         out_ref[:, b, :] = out[:, 128 * b : 128 * b + H]
 
@@ -345,17 +361,21 @@
     matrices = matrices.reshape(SOURCES + 1, BD * BLK, 512)
     other_half = from_previous(half)
 
+    field = coeffs
     for step in range(ITERS):
         if step:
-            coeffs = call(
-                coeffs_kernel,
+            got, other_half = lax.optimization_barrier((got, other_half))
+            field, low, high = got, from_previous(got), from_next(got)
+            field, half, panel_rows, diffract = lax.optimization_barrier(
+                (field, half, panel_rows, diffract)
+            )
+            matrices = call(
+                product_kernel,
                 (where_am_i,),
-                (got, half, other_half),
-                shape(CHIPS, BLK, 128),
-                "coeffs",
+                (matrices, half, other_half),
+                shape(SOURCES, BD * BLK, 512),
+                "product",
             )
-            low, high = from_previous(coeffs), from_next(coeffs)
-            coeffs, panel_rows, diffract = lax.optimization_barrier((coeffs, panel_rows, diffract))
             ready = call(
                 ready_kernel,
                 (),
@@ -364,7 +384,7 @@
                 "ready",
             )
             low, ready = lax.optimization_barrier((low, ready))
-        part = call(own_kernel, (), (matrices, coeffs), shape(BD * BLK, L, dtype=F32), "own")
+        part = call(own_kernel, (), (matrices, field), shape(BD * BLK, L, dtype=F32), "own")
         message = call(
             incident_kernel,
             (),
@@ -373,11 +393,18 @@
             "incident",
         )
         got = exchange(message)
-    whole = lax.all_gather(got, "c", axis=0, tiled=False)
+    other = swapped(got)
+    own_sources, own_outgoing = call(
+        last_own_kernel,
+        (where_am_i,),
+        (got, *ready),
+        (shape(LAN, panel_rows.shape[0]), shape(S, BD * 128, dtype=F32)),
+        "last_own",
+    )
     sources, outgoing = call(
         last_kernel,
-        (),
-        (whole, *ready),
+        (where_am_i,),
+        (other, *ready, own_sources, own_outgoing),
         (shape(H * BD, panel_rows.shape[0]), shape(S, BD, H, dtype=F32)),
         "last",
     )

time: 98.3 us -> 100 us (1.017)
  blocking collectives: 69 us -> 62.6 us
  starting transfers between devices: 12 us -> 16.7 us
  Pallas kernels: 14.8 us -> 16.6 us
  waiting for transfers between devices: 1.36 us -> 2.8 us
    all_gather x1 -> x0, blocking collectives: 6.38 us -> none  [shards(): whole = lax.all_gather(got, 'c', axis=0, tiled=False)]
    ppermute x3 -> x4, starting transfers between devices: 6.17 us -> 10.9 us  [swapped(): return lax.ppermute(value, 'c', [(0, 1), (1, 0)])]
    ppermute x3, starting transfers between devices: 2.8 us -> 0.52 us  [from_previous(): lax.ppermute(value, 'x', [(i, (i + 1) % count) for i in range(count)])]
    ppermute x2, starting transfers between devices: 3.03 us -> 5.23 us  [from_next(): lax.ppermute(value, 'x', [((i + 1) % count, i) for i in range(count)])]
    pallas_call x10 -> x11, Pallas kernels: 11.6 us -> 13.4 us  [call(): pl.pallas_call(kernel, out_shape=shapes, in_specs=[SM] * len(scalars) + [...]
    ppermute x3, waiting for transfers between devices: 1.34 us -> 2.78 us  [from_previous(): lax.ppermute(value, 'x', [(i, (i + 1) % count) for i in range(count)])]
  transfers between devices with their start and end apart: 8 -> 9, of which waited for: 2 -> 1; matrix products, arithmetic and copies ran while one was open for 0% -> 0% of each run, Pallas kernels for 6% -> 9%
where the time goes in v5:
time: 100 us; the launch traced here: 99.9 us
  blocking collectives  62.6 us (63%)
  starting transfers between devices  16.7 us (17%)
  Pallas kernels  16.6 us (17%)
  waiting for transfers between devices  2.8 us (3%)
    all_to_all x3, blocking collectives, exchange(): return lax.all_to_all(blocks, PLANE, 0, 0, tiled=True)  62.6 us
    pallas_call x11, Pallas kernels, call(): pl.pallas_call(kernel, out_shape=shapes, in_specs=[SM] * len(scalars) + [...  13.4 us
    ppermute x4, starting transfers between devices, swapped(): return lax.ppermute(value, 'c', [(0, 1), (1, 0)])  10.9 us
    ppermute x2, starting transfers between devices, from_next(): lax.ppermute(value, 'x', [((i + 1) % count, i) for i in range(count)])  5.23 us
    pallas_call x1, Pallas kernels, shards(): pl.pallas_call(send_kernel, out_shape=(shape(CHIPS, BLK, 1024), shape(*be...  3.19 us
    ppermute x3, waiting for transfers between devices, from_previous(): lax.ppermute(value, 'x', [(i, (i + 1) % count) for i in range(count)])  2.78 us
  transfers between devices with their start and end apart: 9, of which 1 were waited for; matrix products, arithmetic and copies ran while one was open for 0% of the time, Pallas kernels for 9%

profile of v5, /device:TPU:1, one launch (start us, length us, event | category | flops | bytes accessed | tf_op | source)
XLA Modules:
  0.0 99.9 jit_solution(3709039403161734173)
XLA Ops:
  0.6 3.3 %collective-permute-start.1 = (f32[7,8,36]{2,1,0:T(8,128)}, f32[7,8,36]{2,1,0:T(8,128)S(1)}, u32[]{:S(2)}, u32[]{:S(2)}) collective-permute-start(f32[7,8,36]{2,1,0:T(8,128)} %bitcast.14), channel_id=1, source_target_pairs={{0,1},{1,0},{2,3},{3,2},{4,5},{5,4},{6,7},{7,6},{8,9},{9,8},{10,11... | collective-permute-start | bytes 24200 | tf_op jit(solution)/shard_map/ppermute | solution.py:293
  4.0 0.1 collective-permute-start
  4.1 0.1 pad_add_fusion.where_am_i
  4.1 3.2 %send.1 = (bf16[32,16,1024]{2,1,0:T(8,128)(2,1)S(1)}, f32[7,8,36]{2,1,0:T(8,128)S(1)}) custom-call(s32[2]{0:T(128)S(1)} %pad_add_fusion.where_am_i, s32[2]{0:T(128)} %source_hbm.1, s32[2]{0:T(128)} %target_hbm.1, s32[2]{0:T(128)} %live_hbm.1, bf16[2,448,448]{2,1,0:T(8,128)(2,1)} %t_hbm.1, bf16[7,448]{1,0:T(8,128)(2,1)} %d_ref, f32[7,8,36]{2,1,0:T(8,128)} %bitcast.17), custom_call_target="tpu_custom_call" | custom-call | tf_op jit(solution)/shard_map/send/pallas_call | solution.py:318
  7.3 0.0 collective-permute-done.1.amb_other_ref
  7.4 0.0 collective-permute-done.other_ref
  7.4 1.2 %begin.1 = bf16[32,16,1024]{2,1,0:T(8,128)(2,1)S(1)} custom-call(s32[2]{0:T(128)S(1)} %pad_add_fusion.where_am_i, f32[7,8,36]{2,1,0:T(8,128)S(1)} %get-tuple-element.28.own_ref, f32[7,8,36]{2,1,0:T(8,128)S(1)} %collective-permute-done.other_ref, bf16[32,16,1024]{2,1,0:T(8,128)(2,1)S(1)} %get-tuple-element.30.in_ref), custom_call_target="tpu_custom_call", output_to_operand_aliasing={{}: (3, {})} | custom-call | tf_op jit(solution)/shard_map/begin/pallas_call | solution.py:273
  8.5 35.5 %all_to_all.15.in_ref = bf16[32,16,1024]{2,1,0:T(8,128)(2,1)S(1)} all-to-all(bf16[32,16,1024]{2,1,0:T(8,128)(2,1)S(1)} %begin.1), channel_id=1, replica_groups=mesh['x'=4,'z'=8,'y'=4,'c'=2] {'z','y'}, dimensions={0} | all-to-all | bytes 2097152 | tf_op jit(solution)/shard_map/all_to_all | solution.py:289
  44.1 2.7 %collective-permute-start.2 = (bf16[32,16,1024]{2,1,0:T(8,128)(2,1)S(1)}, bf16[32,16,1024]{2,1,0:T(8,128)(2,1)S(1)}, u32[]{:S(2)}, u32[]{:S(2)}) collective-permute-start(bf16[32,16,1024]{2,1,0:T(8,128)(2,1)S(1)} %all_to_all.15.in_ref), channel_id=1, source_target_pairs={{0,1},{1,0},{2,3},{3,2},{4,5},{5,4},{6,7},{7,6},{8,9},{9,8},{10,11... | collective-permute-start | bytes 3145736 | tf_op jit(solution)/shard_map/ppermute | solution.py:293
  46.8 0.4 first.1.own_ref
  47.3 2.6 %collective-permute-start.4 = (bf16[32,16,128]{2,1,0:T(8,128)(2,1)S(1)}, bf16[32,16,128]{2,1,0:T(8,128)(2,1)S(1)}, u32[]{:S(2)}, u32[]{:S(2)}) collective-permute-start(bf16[32,16,128]{2,1,0:T(8,128)(2,1)S(1)} %first.1.own_ref), channel_id=1, source_target_pairs={{64,0},{128,64},{192,128},{0,192},{65,1},{129,65},{193,129},{1,193... | collective-permute-start | bytes 393224 | tf_op jit(solution)/shard_map/ppermute | solution.py:303
  49.8 0.0 collective-permute-start.3
  49.9 0.0 collective-permute-done.2.other_ref
  49.9 2.0 %place.1 = (bf16[200,16,512]{2,1,0:T(8,128)(2,1)S(1)}, f32[16,256]{1,0:T(8,128)S(1)}, bf16[512,256]{1,0:T(8,128)(2,1)S(1)}) custom-call(s32[2]{0:T(128)S(1)} %pad_add_fusion.where_am_i, s32[32,1,2]{2,1,0:T(1,128)S(1)} %slice_convert_fusion.1.own_at, s32[32,1,2]{2,1,0:T(1,128)S(1)} %slice_convert_fusion.other_at, ...), custom_call_target="tpu_custom_call" | custom-call | tf_op jit(solution)/shard_map/place/pallas_call | solution.py:273
  51.9 0.5 collective-permute-start.5
  52.5 0.6 own.2.part_ref
  53.1 2.8 %collective-permute-done.3.low_ref = bf16[32,16,128]{2,1,0:T(8,128)(2,1)S(1)} collective-permute-done((bf16[32,16,128]{2,1,0:T(8,128)(2,1)S(1)}, bf16[32,16,128]{2,1,0:T(8,128)(2,1)S(1)}, u32[]{:S(2)}, u32[]{:S(2)}) %collective-permute-start.3) | collective-permute-done | bytes 131104 | tf_op jit(solution)/shard_map/ppermute | solution.py:298
  55.8 1.4 %incident.2 = bf16[32,16,128]{2,1,0:T(8,128)(2,1)S(1)} custom-call(bf16[25,128,512]{2,1,0:T(8,128)(2,1)S(1)} %bitcast.11, bf16[32,16,128]{2,1,0:T(8,128)(2,1)S(1)} %collective-permute-done.3.low_ref, bf16[32,16,128]{2,1,0:T(8,128)(2,1)S(1)} %collective-permute-done.4.high_ref, f32[128,256]{1,0:T(8,128)S(1)} %own.2.part_ref, ...), custom_call_target="tpu_custom_call" | custom-call | tf_op jit(solution)/shard_map/incident/pallas_call | solution.py:273
  57.2 14.5 %all_to_all.16.own_ref = bf16[32,16,128]{2,1,0:T(8,128)(2,1)S(1)} all-to-all(bf16[32,16,128]{2,1,0:T(8,128)(2,1)S(1)} %incident.2), channel_id=1, replica_groups=mesh['x'=4,'z'=8,'y'=4,'c'=2] {'z','y'}, dimensions={0} | all-to-all | bytes 262144 | tf_op jit(solution)/shard_map/all_to_all | solution.py:289
  71.7 2.7 %collective-permute-start.7 = (bf16[32,16,128]{2,1,0:T(8,128)(2,1)S(1)}, bf16[32,16,128]{2,1,0:T(8,128)(2,1)S(1)}, u32[]{:S(2)}, u32[]{:S(2)}) collective-permute-start(bf16[32,16,128]{2,1,0:T(8,128)(2,1)S(1)} %all_to_all.16.own_ref), channel_id=1, source_target_pairs={{64,0},{128,64},{192,128},{0,192},{65,1},{129,65},{193,129},{1,193... | collective-permute-start | bytes 393224 | tf_op jit(solution)/shard_map/ppermute | solution.py:303
  74.4 2.4 %product.1.w_ref = bf16[24,128,512]{2,1,0:T(8,128)(2,1)S(1)} custom-call(s32[2]{0:T(128)S(1)} %pad_add_fusion.where_am_i, bf16[25,128,512]{2,1,0:T(8,128)(2,1)S(1)} %bitcast.12, bf16[512,256]{1,0:T(8,128)(2,1)S(1)} %get-tuple-element.38.d_ref, bf16[512,256]{1,0:T(8,128)(2,1)S(1)} %collective-permute-done.5.d_other_ref), custom_call_target="tpu_custom_call" | custom-call | tf_op jit(solution)/shard_map/product/pallas_call | solution.py:273
  76.8 0.0 copy-start
  76.8 0.0 copy-start.1
  76.8 0.6 own.3.part_ref
  77.4 0.3 copy-done
  77.7 0.5 ready.1
  78.2 0.0 collective-permute-done.6.low_ref
  78.2 1.4 %incident.3 = bf16[32,16,128]{2,1,0:T(8,128)(2,1)S(1)} custom-call(bf16[24,128,512]{2,1,0:T(8,128)(2,1)S(1)} %product.1.w_ref, bf16[32,16,128]{2,1,0:T(8,128)(2,1)S(1)} %collective-permute-done.6.low_ref, bf16[32,16,128]{2,1,0:T(8,128)(2,1)S(1)} %collective-permute-done.7.high_ref, f32[128,256]{1,0:T(8,128)S(1)} %own.3.part_ref, ...), custom_call_target="tpu_custom_call" | custom-call | tf_op jit(solution)/shard_map/incident/pallas_call | solution.py:273
  79.6 12.6 %all_to_all.17.in_ref = bf16[32,16,128]{2,1,0:T(8,128)(2,1)S(1)} all-to-all(bf16[32,16,128]{2,1,0:T(8,128)(2,1)S(1)} %incident.3), channel_id=1, replica_groups=mesh['x'=4,'z'=8,'y'=4,'c'=2] {'z','y'}, dimensions={0} | all-to-all | bytes 262144 | tf_op jit(solution)/shard_map/all_to_all | solution.py:289
  92.2 4.7 %collective-permute-start.8 = (bf16[32,16,128]{2,1,0:T(8,128)(2,1)S(1)}, bf16[32,16,128]{2,1,0:T(8,128)(2,1)S(1)}, u32[]{:S(2)}, u32[]{:S(2)}) collective-permute-start(bf16[32,16,128]{2,1,0:T(8,128)(2,1)S(1)} %all_to_all.17.in_ref), channel_id=1, source_target_pairs={{0,1},{1,0},{2,3},{3,2},{4,5},{5,4},{6,7},{7,6},{8,9},{9,8},{10,11... | collective-permute-start | bytes 393224 | tf_op jit(solution)/shard_map/ppermute | solution.py:293
  96.9 1.2 %last_own.1 = (bf16[144,128]{1,0:T(8,128)(2,1)S(1)}, f32[7,1024]{1,0:T(8,128)S(1)}) custom-call(s32[2]{0:T(128)S(1)} %pad_add_fusion.where_am_i, bf16[32,16,128]{2,1,0:T(8,128)(2,1)S(1)} %all_to_all.17.in_ref, bf16[512,128]{1,0:T(8,128)(2,1)S(1)} %get-tuple-element.47.p_ref, bf16[7,512]{1,0:T(8,128)(2,1)S(1)} %get-tuple-element.48.d_ref, ...), custom_call_target="tpu_custom_call" | custom-call | tf_op jit(solution)/shard_map/last_own/pallas_call | solution.py:273
  98.1 1.8 %last.1 = (bf16[288,128]{1,0:T(8,128)(2,1)}, f32[7,8,36]{2,1,0:T(8,128)}) custom-call(s32[2]{0:T(128)S(1)} %pad_add_fusion.where_am_i, bf16[32,16,128]{2,1,0:T(8,128)(2,1)S(1)} %collective-permute-done.8.in_ref, bf16[512,128]{1,0:T(8,128)(2,1)S(1)} %get-tuple-element.47.p_ref, bf16[7,512]{1,0:T(8,128)(2,1)S(1)} %get-tuple-element.48.d_ref, ...), custom_call_target="tpu_custom_call" | custom-call | tf_op jit(solution)/shard_map/last/pallas_call | solution.py:273
  (10 shorter events, 0.1 us)
Async XLA Ops:
  0.6 49.3 %copy-start.2 = (f32[8,36,7]{1,0,2:T(8,128)S(1)}, f32[8,36,7]{1,0,2:T(8,128)}, u32[]{:S(2)}) copy-start(f32[8,36,7]{1,0,2:T(8,128)} %param.8) | copy-start | bytes 24196
  0.6 6.7 %collective-permute-start.1 = (f32[7,8,36]{2,1,0:T(8,128)}, f32[7,8,36]{2,1,0:T(8,128)S(1)}, u32[]{:S(2)}, u32[]{:S(2)}) collective-permute-start(f32[7,8,36]{2,1,0:T(8,128)} %bitcast.14), channel_id=1, source_target_pairs={{0,1},{1,0},{2,3},{3,2},{4,5},{5,4},{6,7},{7,6},{8,9},{9,8},{10,11... | collective-permute-start | bytes 24200 | tf_op jit(solution)/shard_map/ppermute | solution.py:293
  4.0 3.4 %collective-permute-start = (f32[7,8,36]{2,1,0:T(8,128)}, f32[7,8,36]{2,1,0:T(8,128)S(1)}, u32[]{:S(2)}, u32[]{:S(2)}) collective-permute-start(f32[7,8,36]{2,1,0:T(8,128)} %bitcast.16), channel_id=1, source_target_pairs={{0,1},{1,0},{2,3},{3,2},{4,5},{5,4},{6,7},{7,6},{8,9},{9,8},{10,11... | collective-permute-start | bytes 24200 | tf_op jit(solution)/shard_map/ppermute | solution.py:293
  44.1 5.8 %collective-permute-start.2 = (bf16[32,16,1024]{2,1,0:T(8,128)(2,1)S(1)}, bf16[32,16,1024]{2,1,0:T(8,128)(2,1)S(1)}, u32[]{:S(2)}, u32[]{:S(2)}) collective-permute-start(bf16[32,16,1024]{2,1,0:T(8,128)(2,1)S(1)} %all_to_all.15.in_ref), channel_id=1, source_target_pairs={{0,1},{1,0},{2,3},{3,2},{4,5},{5,4},{6,7},{7,6},{8,9},{9,8},{10,11... | collective-permute-start | bytes 3145736 | tf_op jit(solution)/shard_map/ppermute | solution.py:293
  47.3 5.8 %collective-permute-start.4 = (bf16[32,16,128]{2,1,0:T(8,128)(2,1)S(1)}, bf16[32,16,128]{2,1,0:T(8,128)(2,1)S(1)}, u32[]{:S(2)}, u32[]{:S(2)}) collective-permute-start(bf16[32,16,128]{2,1,0:T(8,128)(2,1)S(1)} %first.1.own_ref), channel_id=1, source_target_pairs={{64,0},{128,64},{192,128},{0,192},{65,1},{129,65},{193,129},{1,193... | collective-permute-start | bytes 393224 | tf_op jit(solution)/shard_map/ppermute | solution.py:303
  49.8 6.0 %collective-permute-start.3 = (bf16[32,16,128]{2,1,0:T(8,128)(2,1)S(1)}, bf16[32,16,128]{2,1,0:T(8,128)(2,1)S(1)}, u32[]{:S(2)}, u32[]{:S(2)}) collective-permute-start(bf16[32,16,128]{2,1,0:T(8,128)(2,1)S(1)} %first.1.own_ref), channel_id=1, source_target_pairs={{0,64},{64,128},{128,192},{192,0},{1,65},{65,129},{129,193},{193,1... | collective-permute-start | bytes 393224 | tf_op jit(solution)/shard_map/ppermute | solution.py:298
  51.9 19.7 %collective-permute-start.5 = (bf16[512,256]{1,0:T(8,128)(2,1)S(1)}, bf16[512,256]{1,0:T(8,128)(2,1)S(1)}, u32[]{:S(2)}, u32[]{:S(2)}) collective-permute-start(bf16[512,256]{1,0:T(8,128)(2,1)S(1)} %get-tuple-element.38.d_ref), channel_id=1, source_target_pairs={{0,64},{64,128},{128,192},{192,0},{1,65},{65,129},{129,193},{193,1... | collective-permute-start | bytes 786440 | tf_op jit(solution)/shard_map/ppermute | solution.py:298
  71.7 6.5 %collective-permute-start.6 = (bf16[32,16,128]{2,1,0:T(8,128)(2,1)S(1)}, bf16[32,16,128]{2,1,0:T(8,128)(2,1)S(1)}, u32[]{:S(2)}, u32[]{:S(2)}) collective-permute-start(bf16[32,16,128]{2,1,0:T(8,128)(2,1)S(1)} %all_to_all.16.own_ref), channel_id=1, source_target_pairs={{0,64},{64,128},{128,192},{192,0},{1,65},{65,129},{129,193},{193,1... | collective-permute-start | bytes 393224 | tf_op jit(solution)/shard_map/ppermute | solution.py:298
  71.7 6.5 %collective-permute-start.7 = (bf16[32,16,128]{2,1,0:T(8,128)(2,1)S(1)}, bf16[32,16,128]{2,1,0:T(8,128)(2,1)S(1)}, u32[]{:S(2)}, u32[]{:S(2)}) collective-permute-start(bf16[32,16,128]{2,1,0:T(8,128)(2,1)S(1)} %all_to_all.16.own_ref), channel_id=1, source_target_pairs={{64,0},{128,64},{192,128},{0,192},{65,1},{129,65},{193,129},{1,193... | collective-permute-start | bytes 393224 | tf_op jit(solution)/shard_map/ppermute | solution.py:303
  76.8 0.9 copy-start
  76.8 0.9 copy-start.1
  92.2 5.9 %collective-permute-start.8 = (bf16[32,16,128]{2,1,0:T(8,128)(2,1)S(1)}, bf16[32,16,128]{2,1,0:T(8,128)(2,1)S(1)}, u32[]{:S(2)}, u32[]{:S(2)}) collective-permute-start(bf16[32,16,128]{2,1,0:T(8,128)(2,1)S(1)} %all_to_all.17.in_ref), channel_id=1, source_target_pairs={{0,1},{1,0},{2,3},{3,2},{4,5},{5,4},{6,7},{7,6},{8,9},{9,8},{10,11... | collective-permute-start | bytes 393224 | tf_op jit(solution)/shard_map/ppermute | solution.py:293

commit v6 on v5

--- a/solution.py
+++ b/solution.py
@@ -112,7 +112,7 @@
     for copy in copies:
         copy.start()
     buoy = where_am_i[1]
-    pad, pack = padding(), packing()
+    pack = packing()
     row, col = iota((M, L), 0), iota((M, L), 1)
     half = ones((row == HALF * (buoy & 1) + col - 2 * (col >> 4)) & ((col & 15) < R))
     to, line = iota((BLK, S), 0), iota((BLK, S), 1)
@@ -125,17 +125,23 @@
         at = jnp.where(live[k] == 1, jnp.clip(at, 0, EMPTY), EMPTY)
         number = jnp.where((brow == BLK - 1) & (blane == k), at.astype(F32), number)
     own = dot(d_ref[...], half).astype(BF16)
+    brow = iota((BLK, 2 * L), 0)
     for p in range(2):
-        copies[1 + p].wait()
-        wide = dot(t_ref[p], pack).astype(BF16)
+        extra = []
         for k in range(2):
             spare = ((to == R) & (line == 2 * p + k)) | ((to == R + 1) & (line == 4 + 2 * p + k))
-            extra = dot(ones(spare), own)
-            if p == 1 and k == 1:
-                extra = extra + number
-            part = dot(pad, wide[:, L * k : L * (k + 1)]).reshape(CHIPS, BLK, L) + extra[None]
-            at = 512 * p + L * k
-            out_ref[:, :, at : at + L] = part.astype(BF16)
+            extra.append(dot(ones(spare), own))
+        if p == 1:
+            extra[1] = extra[1] + number
+        extra = jnp.concatenate(extra, axis=1)
+        copies[1 + p].wait()
+        wide = dot(t_ref[p], pack)
+        for j in range(CHIPS):
+            rows = wide[R * j : min(R * j + BLK, M)]
+            if j == CHIPS - 1:
+                rows = jnp.concatenate([rows, jnp.zeros((BLK - R, 2 * L), F32)], axis=0)
+            rows = jnp.where(brow < R, rows, extra)
+            out_ref[j, :, 2 * L * p : 2 * L * (p + 1)] = rows.astype(BF16)
     copies[3].wait()
 
 
@@ -220,16 +226,13 @@
     out_ref[...] = jnp.broadcast_to(packed(mine), (CHIPS, BLK, 128))
 
 
-def product_kernel(where_am_i, w_ref, d_ref, d_other_ref, out_ref):
+def coeffs_kernel(where_am_i, in_ref, d_ref, d_other_ref, out_ref):
+    field = unpacked(in_ref[...])
     even = (where_am_i[1] & 1) == 0
-    own, other = d_ref[...].astype(F32), d_other_ref[...].astype(F32)
-    halves = (
-        jnp.where(even, own, other).astype(BF16),
-        jnp.where(even, other, own).astype(BF16),
-    )
-    for s in range(SOURCES):
-        for k in range(2):
-            out_ref[s, :, L * k : L * (k + 1)] = dot(w_ref[s], halves[k]).astype(BF16)
+    upper, lower = field[:L].astype(F32), field[L:].astype(F32)
+    first = jnp.where(even, upper, lower).astype(BF16)
+    second = jnp.where(even, lower, upper).astype(BF16)
+    out_ref[...] = packed(dot(d_ref[...], first) + dot(d_other_ref[...], second))
 
 
 def ready_kernel(p_ref, d_ref, p_out, d_out, lanes_out):
@@ -361,21 +364,17 @@
     matrices = matrices.reshape(SOURCES + 1, BD * BLK, 512)
     other_half = from_previous(half)
 
-    field = coeffs
     for step in range(ITERS):
         if step:
-            got, other_half = lax.optimization_barrier((got, other_half))
-            field, low, high = got, from_previous(got), from_next(got)
-            field, half, panel_rows, diffract = lax.optimization_barrier(
-                (field, half, panel_rows, diffract)
+            coeffs = call(
+                coeffs_kernel,
+                (where_am_i,),
+                (got, half, other_half),
+                shape(CHIPS, BLK, 128),
+                "coeffs",
             )
-            matrices = call(
-                product_kernel,
-                (where_am_i,),
-                (matrices, half, other_half),
-                shape(SOURCES, BD * BLK, 512),
-                "product",
-            )
+            low, high = from_previous(coeffs), from_next(coeffs)
+            coeffs, panel_rows, diffract = lax.optimization_barrier((coeffs, panel_rows, diffract))
             ready = call(
                 ready_kernel,
                 (),
@@ -384,7 +383,7 @@
                 "ready",
             )
             low, ready = lax.optimization_barrier((low, ready))
-        part = call(own_kernel, (), (matrices, field), shape(BD * BLK, L, dtype=F32), "own")
+        part = call(own_kernel, (), (matrices, coeffs), shape(BD * BLK, L, dtype=F32), "own")
         message = call(
             incident_kernel,
             (),

time: 100 us -> 97.1 us (0.971)
  Pallas kernels: 16.6 us -> 14.7 us
    ppermute x3, starting transfers between devices: 0.52 us -> 2.65 us  [from_previous(): lax.ppermute(value, 'x', [(i, (i + 1) % count) for i in range(count)])]
    ppermute x2, starting transfers between devices: 5.23 us -> 3.2 us  [from_next(): lax.ppermute(value, 'x', [((i + 1) % count, i) for i in range(count)])]
    pallas_call x11, Pallas kernels: 13.4 us -> 12.2 us  [call(): pl.pallas_call(kernel, out_shape=shapes, in_specs=[SM] * len(scalars) + [...]
  transfers between devices with their start and end apart: 9 -> 9, of which waited for: 1 -> 2; matrix products, arithmetic and copies ran while one was open for 0% -> 0% of each run, Pallas kernels for 9% -> 7%
where the time goes in v6:
time: 97.1 us; the launch traced here: 96.9 us
  blocking collectives  62.7 us (65%)
  starting transfers between devices  16.8 us (17%)
  Pallas kernels  14.7 us (15%)
  waiting for transfers between devices  1.85 us (2%)
    all_to_all x3, blocking collectives, exchange(): return lax.all_to_all(blocks, PLANE, 0, 0, tiled=True)  62.7 us
    pallas_call x11, Pallas kernels, call(): pl.pallas_call(kernel, out_shape=shapes, in_specs=[SM] * len(scalars) + [...  12.2 us
    ppermute x4, starting transfers between devices, swapped(): return lax.ppermute(value, 'c', [(0, 1), (1, 0)])  10.9 us
    ppermute x2, starting transfers between devices, from_next(): lax.ppermute(value, 'x', [((i + 1) % count, i) for i in range(count)])  3.2 us
    ppermute x3, starting transfers between devices, from_previous(): lax.ppermute(value, 'x', [(i, (i + 1) % count) for i in range(count)])  2.65 us
    pallas_call x1, Pallas kernels, shards(): pl.pallas_call(send_kernel, out_shape=(shape(CHIPS, BLK, 1024), shape(*be...  2.53 us
  transfers between devices with their start and end apart: 9, of which 2 were waited for; matrix products, arithmetic and copies ran while one was open for 0% of the time, Pallas kernels for 7%

profile of v6, /device:TPU:1, one launch (start us, length us, event | category | flops | bytes accessed | tf_op | source)
XLA Modules:
  0.0 96.9 jit_solution(179654295013892902)
XLA Ops:
  0.6 3.3 %collective-permute-start.1 = (f32[7,8,36]{2,1,0:T(8,128)}, f32[7,8,36]{2,1,0:T(8,128)S(1)}, u32[]{:S(2)}, u32[]{:S(2)}) collective-permute-start(f32[7,8,36]{2,1,0:T(8,128)} %bitcast.15), channel_id=1, source_target_pairs={{0,1},{1,0},{2,3},{3,2},{4,5},{5,4},{6,7},{7,6},{8,9},{9,8},{10,11... | collective-permute-start | bytes 24200 | tf_op jit(solution)/shard_map/ppermute | solution.py:296
  4.0 0.1 collective-permute-start
  4.1 0.1 pad_add_fusion.where_am_i
  4.1 2.5 %send.1 = (bf16[32,16,1024]{2,1,0:T(8,128)(2,1)S(1)}, f32[7,8,36]{2,1,0:T(8,128)S(1)}) custom-call(s32[2]{0:T(128)S(1)} %pad_add_fusion.where_am_i, s32[2]{0:T(128)} %source_hbm.1, s32[2]{0:T(128)} %target_hbm.1, s32[2]{0:T(128)} %live_hbm.1, bf16[2,448,448]{2,1,0:T(8,128)(2,1)} %t_hbm.1, bf16[7,448]{1,0:T(8,128)(2,1)} %d_ref, f32[7,8,36]{2,1,0:T(8,128)} %bitcast.18), custom_call_target="tpu_custom_call" | custom-call | tf_op jit(solution)/shard_map/send/pallas_call | solution.py:321
  6.7 0.0 collective-permute-done.1.amb_other_ref
  6.7 0.0 collective-permute-done.other_ref
  6.7 1.2 %begin.1 = bf16[32,16,1024]{2,1,0:T(8,128)(2,1)S(1)} custom-call(s32[2]{0:T(128)S(1)} %pad_add_fusion.where_am_i, f32[7,8,36]{2,1,0:T(8,128)S(1)} %get-tuple-element.25.own_ref, f32[7,8,36]{2,1,0:T(8,128)S(1)} %collective-permute-done.other_ref, bf16[32,16,1024]{2,1,0:T(8,128)(2,1)S(1)} %get-tuple-element.27.in_ref), custom_call_target="tpu_custom_call", output_to_operand_aliasing={{}: (3, {})} | custom-call | tf_op jit(solution)/shard_map/begin/pallas_call | solution.py:276
  7.9 35.5 %all_to_all.15.in_ref = bf16[32,16,1024]{2,1,0:T(8,128)(2,1)S(1)} all-to-all(bf16[32,16,1024]{2,1,0:T(8,128)(2,1)S(1)} %begin.1), channel_id=1, replica_groups=mesh['x'=4,'z'=8,'y'=4,'c'=2] {'z','y'}, dimensions={0} | all-to-all | bytes 2097152 | tf_op jit(solution)/shard_map/all_to_all | solution.py:292
  43.4 2.7 %collective-permute-start.2 = (bf16[32,16,1024]{2,1,0:T(8,128)(2,1)S(1)}, bf16[32,16,1024]{2,1,0:T(8,128)(2,1)S(1)}, u32[]{:S(2)}, u32[]{:S(2)}) collective-permute-start(bf16[32,16,1024]{2,1,0:T(8,128)(2,1)S(1)} %all_to_all.15.in_ref), channel_id=1, source_target_pairs={{0,1},{1,0},{2,3},{3,2},{4,5},{5,4},{6,7},{7,6},{8,9},{9,8},{10,11... | collective-permute-start | bytes 3145736 | tf_op jit(solution)/shard_map/ppermute | solution.py:296
  46.2 0.4 first.1.own_ref
  46.6 1.3 %collective-permute-start.3 = (bf16[32,16,128]{2,1,0:T(8,128)(2,1)S(1)}, bf16[32,16,128]{2,1,0:T(8,128)(2,1)S(1)}, u32[]{:S(2)}, u32[]{:S(2)}) collective-permute-start(bf16[32,16,128]{2,1,0:T(8,128)(2,1)S(1)} %first.1.own_ref), channel_id=1, source_target_pairs={{0,64},{64,128},{128,192},{192,0},{1,65},{65,129},{129,193},{193,1... | collective-permute-start | bytes 393224 | tf_op jit(solution)/shard_map/ppermute | solution.py:301
  47.9 1.5 %collective-permute-start.4 = (bf16[32,16,128]{2,1,0:T(8,128)(2,1)S(1)}, bf16[32,16,128]{2,1,0:T(8,128)(2,1)S(1)}, u32[]{:S(2)}, u32[]{:S(2)}) collective-permute-start(bf16[32,16,128]{2,1,0:T(8,128)(2,1)S(1)} %first.1.own_ref), channel_id=1, source_target_pairs={{64,0},{128,64},{192,128},{0,192},{65,1},{129,65},{193,129},{1,193... | collective-permute-start | bytes 393224 | tf_op jit(solution)/shard_map/ppermute | solution.py:306
  49.4 0.0 collective-permute-done.2.other_ref
  49.5 2.0 %place.1 = (bf16[200,16,512]{2,1,0:T(8,128)(2,1)S(1)}, f32[16,256]{1,0:T(8,128)S(1)}, bf16[512,256]{1,0:T(8,128)(2,1)S(1)}) custom-call(s32[2]{0:T(128)S(1)} %pad_add_fusion.where_am_i, s32[32,1,2]{2,1,0:T(1,128)S(1)} %slice_convert_fusion.1.own_at, s32[32,1,2]{2,1,0:T(1,128)S(1)} %slice_convert_fusion.other_at, ...), custom_call_target="tpu_custom_call" | custom-call | tf_op jit(solution)/shard_map/place/pallas_call | solution.py:276
  51.5 0.3 collective-permute-start.5
  51.8 0.6 own.2.part_ref
  52.4 0.6 collective-permute-done.3.low_ref
  53.0 0.0 collective-permute-done.4.high_ref
  53.0 1.4 %incident.2 = bf16[32,16,128]{2,1,0:T(8,128)(2,1)S(1)} custom-call(bf16[25,128,512]{2,1,0:T(8,128)(2,1)S(1)} %bitcast.11, bf16[32,16,128]{2,1,0:T(8,128)(2,1)S(1)} %collective-permute-done.3.low_ref, bf16[32,16,128]{2,1,0:T(8,128)(2,1)S(1)} %collective-permute-done.4.high_ref, f32[128,256]{1,0:T(8,128)S(1)} %own.2.part_ref, ...), custom_call_target="tpu_custom_call" | custom-call | tf_op jit(solution)/shard_map/incident/pallas_call | solution.py:276
  54.4 14.5 %all_to_all.16.in_ref = bf16[32,16,128]{2,1,0:T(8,128)(2,1)S(1)} all-to-all(bf16[32,16,128]{2,1,0:T(8,128)(2,1)S(1)} %incident.2), channel_id=1, replica_groups=mesh['x'=4,'z'=8,'y'=4,'c'=2] {'z','y'}, dimensions={0} | all-to-all | bytes 262144 | tf_op jit(solution)/shard_map/all_to_all | solution.py:292
  68.9 1.2 %coeffs.1.own_ref = bf16[32,16,128]{2,1,0:T(8,128)(2,1)S(1)} custom-call(s32[2]{0:T(128)S(1)} %pad_add_fusion.where_am_i, bf16[32,16,128]{2,1,0:T(8,128)(2,1)S(1)} %all_to_all.16.in_ref, bf16[512,256]{1,0:T(8,128)(2,1)S(1)} %get-tuple-element.33.d_ref, bf16[512,256]{1,0:T(8,128)(2,1)S(1)} %collective-permute-done.5.d_other_ref), custom_call_target="tpu_custom_call" | custom-call | tf_op jit(solution)/shard_map/coeffs/pallas_call | solution.py:276
  70.1 1.0 %collective-permute-start.6 = (bf16[32,16,128]{2,1,0:T(8,128)(2,1)S(1)}, bf16[32,16,128]{2,1,0:T(8,128)(2,1)S(1)}, u32[]{:S(2)}, u32[]{:S(2)}) collective-permute-start(bf16[32,16,128]{2,1,0:T(8,128)(2,1)S(1)} %coeffs.1.own_ref), channel_id=1, source_target_pairs={{0,64},{64,128},{128,192},{192,0},{1,65},{65,129},{129,193},{193,1... | collective-permute-start | bytes 393224 | tf_op jit(solution)/shard_map/ppermute | solution.py:301
  71.1 1.7 %collective-permute-start.7 = (bf16[32,16,128]{2,1,0:T(8,128)(2,1)S(1)}, bf16[32,16,128]{2,1,0:T(8,128)(2,1)S(1)}, u32[]{:S(2)}, u32[]{:S(2)}) collective-permute-start(bf16[32,16,128]{2,1,0:T(8,128)(2,1)S(1)} %coeffs.1.own_ref), channel_id=1, source_target_pairs={{64,0},{128,64},{192,128},{0,192},{65,1},{129,65},{193,129},{1,193... | collective-permute-start | bytes 393224 | tf_op jit(solution)/shard_map/ppermute | solution.py:306
  72.9 0.6 own.3.part_ref
  73.5 0.5 ready.1
  74.0 1.2 %collective-permute-done.6.low_ref = bf16[32,16,128]{2,1,0:T(8,128)(2,1)S(1)} collective-permute-done((bf16[32,16,128]{2,1,0:T(8,128)(2,1)S(1)}, bf16[32,16,128]{2,1,0:T(8,128)(2,1)S(1)}, u32[]{:S(2)}, u32[]{:S(2)}) %collective-permute-start.6) | collective-permute-done | bytes 131104 | tf_op jit(solution)/shard_map/ppermute | solution.py:301
  75.2 0.0 collective-permute-done.7.high_ref
  75.2 1.4 %incident.3 = bf16[32,16,128]{2,1,0:T(8,128)(2,1)S(1)} custom-call(bf16[25,128,512]{2,1,0:T(8,128)(2,1)S(1)} %bitcast.13, bf16[32,16,128]{2,1,0:T(8,128)(2,1)S(1)} %collective-permute-done.6.low_ref, bf16[32,16,128]{2,1,0:T(8,128)(2,1)S(1)} %collective-permute-done.7.high_ref, f32[128,256]{1,0:T(8,128)S(1)} %own.3.part_ref, ...), custom_call_target="tpu_custom_call" | custom-call | tf_op jit(solution)/shard_map/incident/pallas_call | solution.py:276
  76.6 12.7 %all_to_all.17.in_ref = bf16[32,16,128]{2,1,0:T(8,128)(2,1)S(1)} all-to-all(bf16[32,16,128]{2,1,0:T(8,128)(2,1)S(1)} %incident.3), channel_id=1, replica_groups=mesh['x'=4,'z'=8,'y'=4,'c'=2] {'z','y'}, dimensions={0} | all-to-all | bytes 262144 | tf_op jit(solution)/shard_map/all_to_all | solution.py:292
  89.2 4.7 %collective-permute-start.8 = (bf16[32,16,128]{2,1,0:T(8,128)(2,1)S(1)}, bf16[32,16,128]{2,1,0:T(8,128)(2,1)S(1)}, u32[]{:S(2)}, u32[]{:S(2)}) collective-permute-start(bf16[32,16,128]{2,1,0:T(8,128)(2,1)S(1)} %all_to_all.17.in_ref), channel_id=1, source_target_pairs={{0,1},{1,0},{2,3},{3,2},{4,5},{5,4},{6,7},{7,6},{8,9},{9,8},{10,11... | collective-permute-start | bytes 393224 | tf_op jit(solution)/shard_map/ppermute | solution.py:296
  94.0 1.2 %last_own.1 = (bf16[144,128]{1,0:T(8,128)(2,1)S(1)}, f32[7,1024]{1,0:T(8,128)S(1)}) custom-call(s32[2]{0:T(128)S(1)} %pad_add_fusion.where_am_i, bf16[32,16,128]{2,1,0:T(8,128)(2,1)S(1)} %all_to_all.17.in_ref, bf16[512,128]{1,0:T(8,128)(2,1)S(1)} %get-tuple-element.41.p_ref, bf16[7,512]{1,0:T(8,128)(2,1)S(1)} %get-tuple-element.42.d_ref, ...), custom_call_target="tpu_custom_call" | custom-call | tf_op jit(solution)/shard_map/last_own/pallas_call | solution.py:276
  95.1 1.8 %last.1 = (bf16[288,128]{1,0:T(8,128)(2,1)}, f32[7,8,36]{2,1,0:T(8,128)}) custom-call(s32[2]{0:T(128)S(1)} %pad_add_fusion.where_am_i, bf16[32,16,128]{2,1,0:T(8,128)(2,1)S(1)} %collective-permute-done.8.in_ref, bf16[512,128]{1,0:T(8,128)(2,1)S(1)} %get-tuple-element.41.p_ref, bf16[7,512]{1,0:T(8,128)(2,1)S(1)} %get-tuple-element.42.d_ref, ...), custom_call_target="tpu_custom_call" | custom-call | tf_op jit(solution)/shard_map/last/pallas_call | solution.py:276
  (10 shorter events, 0.1 us)
Async XLA Ops:
  0.6 48.8 %copy-start.2 = (f32[8,36,7]{1,0,2:T(8,128)S(1)}, f32[8,36,7]{1,0,2:T(8,128)}, u32[]{:S(2)}) copy-start(f32[8,36,7]{1,0,2:T(8,128)} %param.8) | copy-start | bytes 24196
  0.6 6.0 %collective-permute-start.1 = (f32[7,8,36]{2,1,0:T(8,128)}, f32[7,8,36]{2,1,0:T(8,128)S(1)}, u32[]{:S(2)}, u32[]{:S(2)}) collective-permute-start(f32[7,8,36]{2,1,0:T(8,128)} %bitcast.15), channel_id=1, source_target_pairs={{0,1},{1,0},{2,3},{3,2},{4,5},{5,4},{6,7},{7,6},{8,9},{9,8},{10,11... | collective-permute-start | bytes 24200 | tf_op jit(solution)/shard_map/ppermute | solution.py:296
  4.0 2.7 %collective-permute-start = (f32[7,8,36]{2,1,0:T(8,128)}, f32[7,8,36]{2,1,0:T(8,128)S(1)}, u32[]{:S(2)}, u32[]{:S(2)}) collective-permute-start(f32[7,8,36]{2,1,0:T(8,128)} %bitcast.17), channel_id=1, source_target_pairs={{0,1},{1,0},{2,3},{3,2},{4,5},{5,4},{6,7},{7,6},{8,9},{9,8},{10,11... | collective-permute-start | bytes 24200 | tf_op jit(solution)/shard_map/ppermute | solution.py:296
  43.4 6.0 %collective-permute-start.2 = (bf16[32,16,1024]{2,1,0:T(8,128)(2,1)S(1)}, bf16[32,16,1024]{2,1,0:T(8,128)(2,1)S(1)}, u32[]{:S(2)}, u32[]{:S(2)}) collective-permute-start(bf16[32,16,1024]{2,1,0:T(8,128)(2,1)S(1)} %all_to_all.15.in_ref), channel_id=1, source_target_pairs={{0,1},{1,0},{2,3},{3,2},{4,5},{5,4},{6,7},{7,6},{8,9},{9,8},{10,11... | collective-permute-start | bytes 3145736 | tf_op jit(solution)/shard_map/ppermute | solution.py:296
  46.6 6.4 %collective-permute-start.3 = (bf16[32,16,128]{2,1,0:T(8,128)(2,1)S(1)}, bf16[32,16,128]{2,1,0:T(8,128)(2,1)S(1)}, u32[]{:S(2)}, u32[]{:S(2)}) collective-permute-start(bf16[32,16,128]{2,1,0:T(8,128)(2,1)S(1)} %first.1.own_ref), channel_id=1, source_target_pairs={{0,64},{64,128},{128,192},{192,0},{1,65},{65,129},{129,193},{193,1... | collective-permute-start | bytes 393224 | tf_op jit(solution)/shard_map/ppermute | solution.py:301
  47.9 5.1 %collective-permute-start.4 = (bf16[32,16,128]{2,1,0:T(8,128)(2,1)S(1)}, bf16[32,16,128]{2,1,0:T(8,128)(2,1)S(1)}, u32[]{:S(2)}, u32[]{:S(2)}) collective-permute-start(bf16[32,16,128]{2,1,0:T(8,128)(2,1)S(1)} %first.1.own_ref), channel_id=1, source_target_pairs={{64,0},{128,64},{192,128},{0,192},{65,1},{129,65},{193,129},{1,193... | collective-permute-start | bytes 393224 | tf_op jit(solution)/shard_map/ppermute | solution.py:306
  51.5 17.4 %collective-permute-start.5 = (bf16[512,256]{1,0:T(8,128)(2,1)S(1)}, bf16[512,256]{1,0:T(8,128)(2,1)S(1)}, u32[]{:S(2)}, u32[]{:S(2)}) collective-permute-start(bf16[512,256]{1,0:T(8,128)(2,1)S(1)} %get-tuple-element.33.d_ref), channel_id=1, source_target_pairs={{0,64},{64,128},{128,192},{192,0},{1,65},{65,129},{129,193},{193,1... | collective-permute-start | bytes 786440 | tf_op jit(solution)/shard_map/ppermute | solution.py:301
  53.0 20.4 %copy-start = (bf16[128,448]{0,1:T(8,128)(2,1)S(1)}, bf16[128,448]{0,1:T(8,128)(2,1)}, u32[]{:S(2)}) copy-start(bf16[128,448]{0,1:T(8,128)(2,1)} %param.15) | copy-start | bytes 344068
  53.0 20.4 %copy-start.1 = (bf16[7,448]{1,0:T(8,128)(2,1)S(1)}, bf16[7,448]{1,0:T(8,128)(2,1)}, u32[]{:S(2)}) copy-start(bf16[7,448]{1,0:T(8,128)(2,1)} %d_ref) | copy-start | bytes 18820
  70.1 5.1 %collective-permute-start.6 = (bf16[32,16,128]{2,1,0:T(8,128)(2,1)S(1)}, bf16[32,16,128]{2,1,0:T(8,128)(2,1)S(1)}, u32[]{:S(2)}, u32[]{:S(2)}) collective-permute-start(bf16[32,16,128]{2,1,0:T(8,128)(2,1)S(1)} %coeffs.1.own_ref), channel_id=1, source_target_pairs={{0,64},{64,128},{128,192},{192,0},{1,65},{65,129},{129,193},{193,1... | collective-permute-start | bytes 393224 | tf_op jit(solution)/shard_map/ppermute | solution.py:301
  71.1 4.1 %collective-permute-start.7 = (bf16[32,16,128]{2,1,0:T(8,128)(2,1)S(1)}, bf16[32,16,128]{2,1,0:T(8,128)(2,1)S(1)}, u32[]{:S(2)}, u32[]{:S(2)}) collective-permute-start(bf16[32,16,128]{2,1,0:T(8,128)(2,1)S(1)} %coeffs.1.own_ref), channel_id=1, source_target_pairs={{64,0},{128,64},{192,128},{0,192},{65,1},{129,65},{193,129},{1,193... | collective-permute-start | bytes 393224 | tf_op jit(solution)/shard_map/ppermute | solution.py:306
  89.2 5.9 %collective-permute-start.8 = (bf16[32,16,128]{2,1,0:T(8,128)(2,1)S(1)}, bf16[32,16,128]{2,1,0:T(8,128)(2,1)S(1)}, u32[]{:S(2)}, u32[]{:S(2)}) collective-permute-start(bf16[32,16,128]{2,1,0:T(8,128)(2,1)S(1)} %all_to_all.17.in_ref), channel_id=1, source_target_pairs={{0,1},{1,0},{2,3},{3,2},{4,5},{5,4},{6,7},{7,6},{8,9},{9,8},{10,11... | collective-permute-start | bytes 393224 | tf_op jit(solution)/shard_map/ppermute | solution.py:296

commit v7 on v6

--- a/solution.py
+++ b/solution.py
@@ -1,3 +1,5 @@
+import functools
+
 import jax
 import jax.numpy as jnp
 from jax import lax
@@ -102,63 +104,47 @@
     return total
 
 
+def gaps(p, rows, dim):
+    dims = (rows, 128) if dim == 0 else (128, rows)
+    place, lane = iota(dims, dim), iota(dims, 1 - dim)
+    return ones((lane == 64 * p + 2 * (place >> 4) + (place & 15) - R) & ((place & 15) >= R))
+
+
 def send_kernel(
-    where_am_i, source_hbm, target_hbm, live_hbm, t_hbm, d_hbm, begin_hbm, out_ref, begin_ref, t_ref, d_ref,
-    source, target, live, sems
+    where_am_i, source_hbm, target_hbm, live_hbm, d_hbm, own_ref, other_ref, wide_ref, out_ref, d_ref, source, target,
+    live, sems
 ):
-    moves = ((d_hbm, d_ref), (t_hbm.at[0], t_ref.at[0]), (t_hbm.at[1], t_ref.at[1]), (begin_hbm, begin_ref))
-    moves += ((source_hbm, source), (target_hbm, target), (live_hbm, live))
+    moves = ((d_hbm, d_ref), (source_hbm, source), (target_hbm, target), (live_hbm, live))
     copies = [pltpu.make_async_copy(a, b, sems.at[i]) for i, (a, b) in enumerate(moves)]
     for copy in copies:
         copy.start()
+    field = chip_field(own_ref[...], other_ref[...], where_am_i[0], False)
+    block = packed(field).reshape(BLK, 128)
+    fills = [dot(block, gaps(p, 2 * L, 1)) for p in range(2)]
     buoy = where_am_i[1]
-    pack = packing()
     row, col = iota((M, L), 0), iota((M, L), 1)
     half = ones((row == HALF * (buoy & 1) + col - 2 * (col >> 4)) & ((col & 15) < R))
     to, line = iota((BLK, S), 0), iota((BLK, S), 1)
-    brow, blane = iota((BLK, L), 0), iota((BLK, L), 1)
-    for i in (0, 4, 5, 6):
-        copies[i].wait()
-    number = 0.0
+    brow, blane = iota((BLK, 2 * L), 0), iota((BLK, 2 * L), 1)
+    for copy in copies:
+        copy.wait()
     for k in range(2):
         at = (source[k] - (buoy - 1) * BD) * BD + target[k] - buoy * BD
         at = jnp.where(live[k] == 1, jnp.clip(at, 0, EMPTY), EMPTY)
-        number = jnp.where((brow == BLK - 1) & (blane == k), at.astype(F32), number)
+        fills[1] = jnp.where((brow == BLK - 1) & (blane == L + k), at.astype(F32), fills[1])
     own = dot(d_ref[...], half).astype(BF16)
-    brow = iota((BLK, 2 * L), 0)
     for p in range(2):
         extra = []
         for k in range(2):
             spare = ((to == R) & (line == 2 * p + k)) | ((to == R + 1) & (line == 4 + 2 * p + k))
             extra.append(dot(ones(spare), own))
-        if p == 1:
-            extra[1] = extra[1] + number
-        extra = jnp.concatenate(extra, axis=1)
-        copies[1 + p].wait()
-        wide = dot(t_ref[p], pack)
+        extra = jnp.concatenate(extra, axis=1) + fills[p]
         for j in range(CHIPS):
-            rows = wide[R * j : min(R * j + BLK, M)]
+            rows = wide_ref[p, R * j : min(R * j + BLK, M), :]
             if j == CHIPS - 1:
                 rows = jnp.concatenate([rows, jnp.zeros((BLK - R, 2 * L), F32)], axis=0)
-            rows = jnp.where(brow < R, rows, extra)
+            rows = jnp.where(brow < R, rows, 0.0) + extra
             out_ref[j, :, 2 * L * p : 2 * L * (p + 1)] = rows.astype(BF16)
-    copies[3].wait()
-
-
-def gaps(p, rows, dim):
-    dims = (rows, 128) if dim == 0 else (128, rows)
-    place, lane = iota(dims, dim), iota(dims, 1 - dim)
-    return ones((lane == 64 * p + 2 * (place >> 4) + (place & 15) - R) & ((place & 15) >= R))
-
-
-def begin_kernel(where_am_i, own_ref, other_ref, in_ref, out_ref):
-    del in_ref
-    field = chip_field(own_ref[...], other_ref[...], where_am_i[0], False)
-    block = packed(field).reshape(BLK, 128)
-    for p in range(2):
-        extra = dot(block, gaps(p, 512, 1)).astype(BF16)
-        at = 512 * p
-        out_ref[:, :, at : at + 512] = out_ref[:, :, at : at + 512] + extra[None]
 
 
 def first_kernel(in_ref, out_ref):
@@ -210,10 +196,15 @@
     out_ref[...] = weighted(w_ref, 1, unpacked(own_ref[...]))
 
 
-def incident_kernel(w_ref, low_ref, high_ref, part_ref, a_ref, out_ref):
+def low_kernel(w_ref, low_ref, part_ref, out_ref):
+    out_ref[...] = part_ref[...] + weighted(w_ref, 0, unpacked(low_ref[...]))
+
+
+def incident_kernel(groups, w_ref, *refs):
+    fields, (part_ref, a_ref, out_ref) = refs[: len(groups)], refs[len(groups) :]
     total = part_ref[...]
-    total = total + weighted(w_ref, 0, unpacked(low_ref[...]))
-    total = total + weighted(w_ref, 2, unpacked(high_ref[...]))
+    for group, field in zip(groups, fields):
+        total = total + weighted(w_ref, group, unpacked(field[...]))
     row, col = iota((L, L), 0), iota((L, L), 1)
     same = ones(((row >> 3) == (col >> 3)) & (row < LAN))
     high, rest = two_terms(total)
@@ -318,18 +309,21 @@
     waves = ambient.transpose(2, 0, 1)
     begin_other = swapped(begin)
     waves_other = swapped(waves)
-    message, begin = pl.pallas_call(
+    wide = lax.dot_general(
+        translation, packing(), (((2,), (0,)), ((), ())), preferred_element_type=F32
+    )
+    wide, waves_other = lax.optimization_barrier((wide, waves_other))
+    message = pl.pallas_call(
         send_kernel,
-        out_shape=(shape(CHIPS, BLK, 1024), shape(*begin.shape, dtype=F32)),
-        in_specs=[SM] + [HBM] * 6,
-        out_specs=[VM] * 2,
+        out_shape=shape(CHIPS, BLK, 1024),
+        in_specs=[SM] + [HBM] * 4 + [VM] * 3,
+        out_specs=VM,
         scratch_shapes=[
-            pltpu.VMEM(translation.shape, BF16),
             pltpu.VMEM(diffract.shape, BF16),
             pltpu.SMEM(pair_source.shape, I32),
             pltpu.SMEM(pair_source.shape, I32),
             pltpu.SMEM(pair_source.shape, I32),
-            pltpu.SemaphoreType.DMA((7,)),
+            pltpu.SemaphoreType.DMA((4,)),
         ],
         compiler_params=pltpu.CompilerParams(vmem_limit_bytes=40 << 20),
         name="send",
@@ -337,17 +331,11 @@
         where_am_i,
         *[
             pltpu.with_memory_space_constraint(value, pltpu.HBM)
-            for value in (pair_source, pair_target, pair_live, translation, diffract, begin)
+            for value in (pair_source, pair_target, pair_live, diffract)
         ],
-    )
-    message, waves_other = lax.optimization_barrier((message, waves_other))
-    message = call(
-        begin_kernel,
-        (where_am_i,),
-        (begin, begin_other, message),
-        shape(CHIPS, BLK, 1024),
-        "begin",
-        input_output_aliases={3: 0},
+        begin,
+        begin_other,
+        wide,
     )
     got = exchange(message)
     got, waves = lax.optimization_barrier((got, waves))
@@ -384,10 +372,15 @@
             )
             low, ready = lax.optimization_barrier((low, ready))
         part = call(own_kernel, (), (matrices, coeffs), shape(BD * BLK, L, dtype=F32), "own")
+        groups, fields = (0, 2), (low, high)
+        if step:
+            low_shape = shape(BD * BLK, L, dtype=F32)
+            part = call(low_kernel, (), (matrices, low, part), low_shape, "low")
+            groups, fields = (2,), (high,)
         message = call(
-            incident_kernel,
+            functools.partial(incident_kernel, groups),
             (),
-            (matrices, low, high, part, own_waves),
+            (matrices, *fields, part, own_waves),
             shape(CHIPS, BLK, 128),
             "incident",
         )

time: 97.1 us -> 96.6 us (level)
  Pallas kernels: 14.7 us -> 13.2 us
    pallas_call x11, Pallas kernels: 12.2 us -> 11.2 us  [call(): pl.pallas_call(kernel, out_shape=shapes, in_specs=[SM] * len(scalars) + [...]
  transfers between devices with their start and end apart: 9 -> 9, of which waited for: 2 -> 4; matrix products, arithmetic and copies ran while one was open for 0% -> 1% of each run, Pallas kernels for 7% -> 8%
where the time goes in v7:
time: 96.6 us; the launch traced here: 96.3 us
  blocking collectives  62.6 us (65%)
  starting transfers between devices  16.5 us (17%)
  Pallas kernels  13.2 us (14%)
  waiting for transfers between devices  2.35 us (2%)
    all_to_all x3, blocking collectives, exchange(): return lax.all_to_all(blocks, PLANE, 0, 0, tiled=True)  62.6 us
    pallas_call x11, Pallas kernels, call(): pl.pallas_call(kernel, out_shape=shapes, in_specs=[SM] * len(scalars) + [...  11.2 us
    ppermute x4, starting transfers between devices, swapped(): return lax.ppermute(value, 'c', [(0, 1), (1, 0)])  10.7 us
    ppermute x2, starting transfers between devices, from_next(): lax.ppermute(value, 'x', [((i + 1) % count, i) for i in range(count)])  3.2 us
    ppermute x3, starting transfers between devices, from_previous(): lax.ppermute(value, 'x', [(i, (i + 1) % count) for i in range(count)])  2.64 us
    pallas_call x1, Pallas kernels, shards(): pl.pallas_call(send_kernel, out_shape=shape(CHIPS, BLK, 1024), in_specs=[...  1.99 us
  transfers between devices with their start and end apart: 9, of which 4 were waited for; matrix products, arithmetic and copies ran while one was open for 1% of the time, Pallas kernels for 8%

profile of v7, /device:TPU:1, one launch (start us, length us, event | category | flops | bytes accessed | tf_op | source)
XLA Modules:
  0.0 96.3 jit_solution(8335795152512758250)
XLA Ops:
  0.6 0.0 copy-start
  0.7 3.3 %collective-permute-start.1 = (f32[7,8,36]{2,1,0:T(8,128)}, f32[7,8,36]{2,1,0:T(8,128)S(1)}, u32[]{:S(2)}, u32[]{:S(2)}) collective-permute-start(f32[7,8,36]{2,1,0:T(8,128)} %bitcast.24), channel_id=1, source_target_pairs={{0,1},{1,0},{2,3},{3,2},{4,5},{5,4},{6,7},{7,6},{8,9},{9,8},{10,11... | collective-permute-start | bytes 24200 | tf_op jit(solution)/shard_map/ppermute | solution.py:287
  4.0 0.1 collective-permute-start
  4.1 0.7 convolution_bitcast_fusion.wide_ref
  4.8 0.1 pad_add_fusion.where_am_i
  4.9 0.2 collective-permute-done.1.amb_other_ref
  5.0 0.3 collective-permute-done.other_ref
  5.4 2.0 %send.1 = bf16[32,16,1024]{2,1,0:T(8,128)(2,1)S(1)} custom-call(s32[2]{0:T(128)S(1)} %pad_add_fusion.where_am_i, s32[2]{0:T(128)} %source_hbm.1, s32[2]{0:T(128)} %target_hbm.1, s32[2]{0:T(128)} %live_hbm.1, bf16[7,448]{1,0:T(8,128)(2,1)} %d_ref, f32[7,8,36]{2,1,0:T(8,128)S(1)} %bitcast.23, f32[7,8,36]{2,1,0:T(8,128)S(1)} %collective-permute-done.other_ref, ...), custom_call_target="tpu_custom_call" | custom-call | tf_op jit(solution)/shard_map/send/pallas_call | solution.py:316
  7.4 35.5 %all_to_all.15.in_ref = bf16[32,16,1024]{2,1,0:T(8,128)(2,1)S(1)} all-to-all(bf16[32,16,1024]{2,1,0:T(8,128)(2,1)S(1)} %send.1), channel_id=1, replica_groups=mesh['x'=4,'z'=8,'y'=4,'c'=2] {'z','y'}, dimensions={0} | all-to-all | bytes 2097152 | tf_op jit(solution)/shard_map/all_to_all | solution.py:283
  42.9 2.8 %collective-permute-start.2 = (bf16[32,16,1024]{2,1,0:T(8,128)(2,1)S(1)}, bf16[32,16,1024]{2,1,0:T(8,128)(2,1)S(1)}, u32[]{:S(2)}, u32[]{:S(2)}) collective-permute-start(bf16[32,16,1024]{2,1,0:T(8,128)(2,1)S(1)} %all_to_all.15.in_ref), channel_id=1, source_target_pairs={{0,1},{1,0},{2,3},{3,2},{4,5},{5,4},{6,7},{7,6},{8,9},{9,8},{10,11... | collective-permute-start | bytes 3145736 | tf_op jit(solution)/shard_map/ppermute | solution.py:287
  45.7 0.4 first.1.own_ref
  46.1 1.3 %collective-permute-start.3 = (bf16[32,16,128]{2,1,0:T(8,128)(2,1)S(1)}, bf16[32,16,128]{2,1,0:T(8,128)(2,1)S(1)}, u32[]{:S(2)}, u32[]{:S(2)}) collective-permute-start(bf16[32,16,128]{2,1,0:T(8,128)(2,1)S(1)} %first.1.own_ref), channel_id=1, source_target_pairs={{0,64},{64,128},{128,192},{192,0},{1,65},{65,129},{129,193},{193,1... | collective-permute-start | bytes 393224 | tf_op jit(solution)/shard_map/ppermute | solution.py:292
  47.4 1.5 %collective-permute-start.4 = (bf16[32,16,128]{2,1,0:T(8,128)(2,1)S(1)}, bf16[32,16,128]{2,1,0:T(8,128)(2,1)S(1)}, u32[]{:S(2)}, u32[]{:S(2)}) collective-permute-start(bf16[32,16,128]{2,1,0:T(8,128)(2,1)S(1)} %first.1.own_ref), channel_id=1, source_target_pairs={{64,0},{128,64},{192,128},{0,192},{65,1},{129,65},{193,129},{1,193... | collective-permute-start | bytes 393224 | tf_op jit(solution)/shard_map/ppermute | solution.py:297
  49.0 2.0 %place.1 = (bf16[200,16,512]{2,1,0:T(8,128)(2,1)S(1)}, f32[16,256]{1,0:T(8,128)S(1)}, bf16[512,256]{1,0:T(8,128)(2,1)S(1)}) custom-call(s32[2]{0:T(128)S(1)} %pad_add_fusion.where_am_i, s32[32,1,2]{2,1,0:T(1,128)S(1)} %slice_convert_fusion.1.own_at, s32[32,1,2]{2,1,0:T(1,128)S(1)} %slice_convert_fusion.other_at, ...), custom_call_target="tpu_custom_call" | custom-call | tf_op jit(solution)/shard_map/place/pallas_call | solution.py:267
  51.0 0.3 collective-permute-start.5
  51.3 0.6 own.2.refs_2_
  51.9 0.6 collective-permute-done.3.refs_0_
  52.6 1.4 %incident.2 = bf16[32,16,128]{2,1,0:T(8,128)(2,1)S(1)} custom-call(bf16[25,128,512]{2,1,0:T(8,128)(2,1)S(1)} %bitcast.17, bf16[32,16,128]{2,1,0:T(8,128)(2,1)S(1)} %collective-permute-done.3.refs_0_, bf16[32,16,128]{2,1,0:T(8,128)(2,1)S(1)} %collective-permute-done.4.refs_1_, f32[128,256]{1,0:T(8,128)S(1)} %own.2.refs_2_, ...), custom_call_target="tpu_custom_call" | custom-call | tf_op jit(solution)/shard_map/incident/pallas_call | solution.py:267
  53.9 14.5 %all_to_all.16.in_ref = bf16[32,16,128]{2,1,0:T(8,128)(2,1)S(1)} all-to-all(bf16[32,16,128]{2,1,0:T(8,128)(2,1)S(1)} %incident.2), channel_id=1, replica_groups=mesh['x'=4,'z'=8,'y'=4,'c'=2] {'z','y'}, dimensions={0} | all-to-all | bytes 262144 | tf_op jit(solution)/shard_map/all_to_all | solution.py:283
  68.4 1.2 %coeffs.1.own_ref = bf16[32,16,128]{2,1,0:T(8,128)(2,1)S(1)} custom-call(s32[2]{0:T(128)S(1)} %pad_add_fusion.where_am_i, bf16[32,16,128]{2,1,0:T(8,128)(2,1)S(1)} %all_to_all.16.in_ref, bf16[512,256]{1,0:T(8,128)(2,1)S(1)} %get-tuple-element.29.d_ref, bf16[512,256]{1,0:T(8,128)(2,1)S(1)} %collective-permute-done.5.d_other_ref), custom_call_target="tpu_custom_call" | custom-call | tf_op jit(solution)/shard_map/coeffs/pallas_call | solution.py:267
  69.6 0.0 copy-start.2
  69.6 1.0 %collective-permute-start.7 = (bf16[32,16,128]{2,1,0:T(8,128)(2,1)S(1)}, bf16[32,16,128]{2,1,0:T(8,128)(2,1)S(1)}, u32[]{:S(2)}, u32[]{:S(2)}) collective-permute-start(bf16[32,16,128]{2,1,0:T(8,128)(2,1)S(1)} %coeffs.1.own_ref), channel_id=1, source_target_pairs={{0,64},{64,128},{128,192},{192,0},{1,65},{65,129},{129,193},{193,1... | collective-permute-start | bytes 393224 | tf_op jit(solution)/shard_map/ppermute | solution.py:292
  70.7 1.7 %collective-permute-start.6 = (bf16[32,16,128]{2,1,0:T(8,128)(2,1)S(1)}, bf16[32,16,128]{2,1,0:T(8,128)(2,1)S(1)}, u32[]{:S(2)}, u32[]{:S(2)}) collective-permute-start(bf16[32,16,128]{2,1,0:T(8,128)(2,1)S(1)} %coeffs.1.own_ref), channel_id=1, source_target_pairs={{64,0},{128,64},{192,128},{0,192},{65,1},{129,65},{193,129},{1,193... | collective-permute-start | bytes 393224 | tf_op jit(solution)/shard_map/ppermute | solution.py:297
  72.4 0.6 own.3.part_ref
  73.0 0.5 ready.1
  73.5 1.2 %collective-permute-done.7.low_ref = bf16[32,16,128]{2,1,0:T(8,128)(2,1)S(1)} collective-permute-done((bf16[32,16,128]{2,1,0:T(8,128)(2,1)S(1)}, bf16[32,16,128]{2,1,0:T(8,128)(2,1)S(1)}, u32[]{:S(2)}, u32[]{:S(2)}) %collective-permute-start.7) | collective-permute-done | bytes 131104 | tf_op jit(solution)/shard_map/ppermute | solution.py:292
  74.7 0.6 low.1.refs_1_
  75.4 0.9 incident.3
  76.3 12.6 %all_to_all.17.in_ref = bf16[32,16,128]{2,1,0:T(8,128)(2,1)S(1)} all-to-all(bf16[32,16,128]{2,1,0:T(8,128)(2,1)S(1)} %incident.3), channel_id=1, replica_groups=mesh['x'=4,'z'=8,'y'=4,'c'=2] {'z','y'}, dimensions={0} | all-to-all | bytes 262144 | tf_op jit(solution)/shard_map/all_to_all | solution.py:283
  88.9 4.5 %collective-permute-start.8 = (bf16[32,16,128]{2,1,0:T(8,128)(2,1)S(1)}, bf16[32,16,128]{2,1,0:T(8,128)(2,1)S(1)}, u32[]{:S(2)}, u32[]{:S(2)}) collective-permute-start(bf16[32,16,128]{2,1,0:T(8,128)(2,1)S(1)} %all_to_all.17.in_ref), channel_id=1, source_target_pairs={{0,1},{1,0},{2,3},{3,2},{4,5},{5,4},{6,7},{7,6},{8,9},{9,8},{10,11... | collective-permute-start | bytes 393224 | tf_op jit(solution)/shard_map/ppermute | solution.py:287
  93.4 1.2 %last_own.1 = (bf16[144,128]{1,0:T(8,128)(2,1)S(1)}, f32[7,1024]{1,0:T(8,128)S(1)}) custom-call(s32[2]{0:T(128)S(1)} %pad_add_fusion.where_am_i, bf16[32,16,128]{2,1,0:T(8,128)(2,1)S(1)} %all_to_all.17.in_ref, bf16[512,128]{1,0:T(8,128)(2,1)S(1)} %get-tuple-element.37.p_ref, bf16[7,512]{1,0:T(8,128)(2,1)S(1)} %get-tuple-element.38.d_ref, ...), custom_call_target="tpu_custom_call" | custom-call | tf_op jit(solution)/shard_map/last_own/pallas_call | solution.py:267
  94.5 1.8 %last.1 = (bf16[288,128]{1,0:T(8,128)(2,1)}, f32[7,8,36]{2,1,0:T(8,128)}) custom-call(s32[2]{0:T(128)S(1)} %pad_add_fusion.where_am_i, bf16[32,16,128]{2,1,0:T(8,128)(2,1)S(1)} %collective-permute-done.8.in_ref, bf16[512,128]{1,0:T(8,128)(2,1)S(1)} %get-tuple-element.37.p_ref, bf16[7,512]{1,0:T(8,128)(2,1)S(1)} %get-tuple-element.38.d_ref, ...), custom_call_target="tpu_custom_call" | custom-call | tf_op jit(solution)/shard_map/last/pallas_call | solution.py:267
  (17 shorter events, 0.1 us)
Async XLA Ops:
  0.6 3.5 %copy-start = (bf16[2,448,448]{2,1,0:T(8,128)(2,1)S(1)}, bf16[2,448,448]{2,1,0:T(8,128)(2,1)}, u32[]{:S(2)}) copy-start(bf16[2,448,448]{2,1,0:T(8,128)(2,1)} %param.10) | copy-start | bytes 2408452
  0.6 4.8 %copy-start.3 = (f32[8,36,7]{1,0,2:T(8,128)S(1)}, f32[8,36,7]{1,0,2:T(8,128)}, u32[]{:S(2)}) copy-start(f32[8,36,7]{1,0,2:T(8,128)} %param.9) | copy-start | bytes 24196
  0.7 4.4 %collective-permute-start.1 = (f32[7,8,36]{2,1,0:T(8,128)}, f32[7,8,36]{2,1,0:T(8,128)S(1)}, u32[]{:S(2)}, u32[]{:S(2)}) collective-permute-start(f32[7,8,36]{2,1,0:T(8,128)} %bitcast.24), channel_id=1, source_target_pairs={{0,1},{1,0},{2,3},{3,2},{4,5},{5,4},{6,7},{7,6},{8,9},{9,8},{10,11... | collective-permute-start | bytes 24200 | tf_op jit(solution)/shard_map/ppermute | solution.py:287
  4.0 1.4 %collective-permute-start = (f32[7,8,36]{2,1,0:T(8,128)}, f32[7,8,36]{2,1,0:T(8,128)S(1)}, u32[]{:S(2)}, u32[]{:S(2)}) collective-permute-start(f32[7,8,36]{2,1,0:T(8,128)} %bitcast.22), channel_id=1, source_target_pairs={{0,1},{1,0},{2,3},{3,2},{4,5},{5,4},{6,7},{7,6},{8,9},{9,8},{10,11... | collective-permute-start | bytes 24200 | tf_op jit(solution)/shard_map/ppermute | solution.py:287
  7.4 41.6 %copy-start.4 = (f32[8,36,7]{1,0,2:T(8,128)S(1)}, f32[8,36,7]{1,0,2:T(8,128)}, u32[]{:S(2)}) copy-start(f32[8,36,7]{1,0,2:T(8,128)} %param.8) | copy-start | bytes 24196
  42.9 6.0 %collective-permute-start.2 = (bf16[32,16,1024]{2,1,0:T(8,128)(2,1)S(1)}, bf16[32,16,1024]{2,1,0:T(8,128)(2,1)S(1)}, u32[]{:S(2)}, u32[]{:S(2)}) collective-permute-start(bf16[32,16,1024]{2,1,0:T(8,128)(2,1)S(1)} %all_to_all.15.in_ref), channel_id=1, source_target_pairs={{0,1},{1,0},{2,3},{3,2},{4,5},{5,4},{6,7},{7,6},{8,9},{9,8},{10,11... | collective-permute-start | bytes 3145736 | tf_op jit(solution)/shard_map/ppermute | solution.py:287
  46.1 6.4 %collective-permute-start.3 = (bf16[32,16,128]{2,1,0:T(8,128)(2,1)S(1)}, bf16[32,16,128]{2,1,0:T(8,128)(2,1)S(1)}, u32[]{:S(2)}, u32[]{:S(2)}) collective-permute-start(bf16[32,16,128]{2,1,0:T(8,128)(2,1)S(1)} %first.1.own_ref), channel_id=1, source_target_pairs={{0,64},{64,128},{128,192},{192,0},{1,65},{65,129},{129,193},{193,1... | collective-permute-start | bytes 393224 | tf_op jit(solution)/shard_map/ppermute | solution.py:292
  47.4 5.1 %collective-permute-start.4 = (bf16[32,16,128]{2,1,0:T(8,128)(2,1)S(1)}, bf16[32,16,128]{2,1,0:T(8,128)(2,1)S(1)}, u32[]{:S(2)}, u32[]{:S(2)}) collective-permute-start(bf16[32,16,128]{2,1,0:T(8,128)(2,1)S(1)} %first.1.own_ref), channel_id=1, source_target_pairs={{64,0},{128,64},{192,128},{0,192},{65,1},{129,65},{193,129},{1,193... | collective-permute-start | bytes 393224 | tf_op jit(solution)/shard_map/ppermute | solution.py:297
  51.0 17.4 %collective-permute-start.5 = (bf16[512,256]{1,0:T(8,128)(2,1)S(1)}, bf16[512,256]{1,0:T(8,128)(2,1)S(1)}, u32[]{:S(2)}, u32[]{:S(2)}) collective-permute-start(bf16[512,256]{1,0:T(8,128)(2,1)S(1)} %get-tuple-element.29.d_ref), channel_id=1, source_target_pairs={{0,64},{64,128},{128,192},{192,0},{1,65},{65,129},{129,193},{193,1... | collective-permute-start | bytes 786440 | tf_op jit(solution)/shard_map/ppermute | solution.py:292
  69.6 3.4 %copy-start.1 = (bf16[128,448]{0,1:T(8,128)(2,1)S(1)}, bf16[128,448]{0,1:T(8,128)(2,1)}, u32[]{:S(2)}) copy-start(bf16[128,448]{0,1:T(8,128)(2,1)} %param.15) | copy-start | bytes 344068
  69.6 3.4 %copy-start.2 = (bf16[7,448]{1,0:T(8,128)(2,1)S(1)}, bf16[7,448]{1,0:T(8,128)(2,1)}, u32[]{:S(2)}) copy-start(bf16[7,448]{1,0:T(8,128)(2,1)} %d_ref) | copy-start | bytes 18820
  69.6 5.1 %collective-permute-start.7 = (bf16[32,16,128]{2,1,0:T(8,128)(2,1)S(1)}, bf16[32,16,128]{2,1,0:T(8,128)(2,1)S(1)}, u32[]{:S(2)}, u32[]{:S(2)}) collective-permute-start(bf16[32,16,128]{2,1,0:T(8,128)(2,1)S(1)} %coeffs.1.own_ref), channel_id=1, source_target_pairs={{0,64},{64,128},{128,192},{192,0},{1,65},{65,129},{129,193},{193,1... | collective-permute-start | bytes 393224 | tf_op jit(solution)/shard_map/ppermute | solution.py:292
  70.7 4.7 %collective-permute-start.6 = (bf16[32,16,128]{2,1,0:T(8,128)(2,1)S(1)}, bf16[32,16,128]{2,1,0:T(8,128)(2,1)S(1)}, u32[]{:S(2)}, u32[]{:S(2)}) collective-permute-start(bf16[32,16,128]{2,1,0:T(8,128)(2,1)S(1)} %coeffs.1.own_ref), channel_id=1, source_target_pairs={{64,0},{128,64},{192,128},{0,192},{65,1},{129,65},{193,129},{1,193... | collective-permute-start | bytes 393224 | tf_op jit(solution)/shard_map/ppermute | solution.py:297
  88.9 5.7 %collective-permute-start.8 = (bf16[32,16,128]{2,1,0:T(8,128)(2,1)S(1)}, bf16[32,16,128]{2,1,0:T(8,128)(2,1)S(1)}, u32[]{:S(2)}, u32[]{:S(2)}) collective-permute-start(bf16[32,16,128]{2,1,0:T(8,128)(2,1)S(1)} %all_to_all.17.in_ref), channel_id=1, source_target_pairs={{0,1},{1,0},{2,3},{3,2},{4,5},{5,4},{6,7},{7,6},{8,9},{9,8},{10,11... | collective-permute-start | bytes 393224 | tf_op jit(solution)/shard_map/ppermute | solution.py:287

commit v8 on v7

--- a/solution.py
+++ b/solution.py
@@ -1,5 +1,3 @@
-import functools
-
 import jax
 import jax.numpy as jnp
 from jax import lax
@@ -7,7 +5,6 @@
 from jax.experimental.pallas import tpu as pltpu
 from jax.sharding import Mesh, PartitionSpec as P
 
-ITERS = 2
 Z, Y, C = 8, 4, 2
 PLANE = ("z", "y")
 CHIPS = Z * Y
@@ -90,17 +87,17 @@
 
 
 def chip_field(own, other, core, exact):
-    kind = F32 if exact else BF16
     head, lane = iota((H, L), 0), iota((H, L), 1)
-    spread = ones((head == core * HC + (lane >> 3)) & (lane < LAN)).astype(kind)
+    spread = ones((head == core * HC + (lane >> 3)) & (lane < LAN))
     row, lane = iota((S * BD, L), 0), iota((S * BD, L), 1)
+    to, col = iota((BLK, S * BD), 0), iota((BLK, S * BD), 1)
     total = 0.0
     for value, place in ((own, core), (other, 1 - core)):
-        wide = dot(value.reshape(S * BD, H).astype(kind), spread, exact=exact)
-        wide = jnp.where((row & 7) == (lane & 7), wide, 0.0)
-        to, col = iota((BLK, S * BD), 0), iota((BLK, S * BD), 1)
-        gather = ones((col >> 3) == to - S * place).astype(kind)
-        total = total + dot(gather, wide.astype(kind), exact=exact)
+        gather = ones((col >> 3) == to - S * place)
+        value = value.reshape(S * BD, H)
+        for term in two_terms(value) if exact else (value.astype(BF16),):
+            wide = jnp.where((row & 7) == (lane & 7), dot(term, spread), 0.0)
+            total = total + dot(gather, wide.astype(BF16))
     return total
 
 
@@ -192,19 +189,33 @@
     return total
 
 
-def own_kernel(w_ref, own_ref, out_ref):
+def coeffs(field, d_ref):
+    return (dot(d_ref[0], field[:L]) + dot(d_ref[1], field[L:])).astype(BF16)
+
+
+def own_kernel(w_ref, own_ref, d_ref, out_ref):
+    out_ref[...] = weighted(w_ref, 1, coeffs(unpacked(own_ref[...]), d_ref))
+
+
+def low_kernel(w_ref, low_ref, d_ref, part_ref, out_ref):
+    out_ref[...] = part_ref[...] + weighted(w_ref, 0, coeffs(unpacked(low_ref[...]), d_ref))
+
+
+def part_kernel(w_ref, own_ref, out_ref):
     out_ref[...] = weighted(w_ref, 1, unpacked(own_ref[...]))
 
 
-def low_kernel(w_ref, low_ref, part_ref, out_ref):
-    out_ref[...] = part_ref[...] + weighted(w_ref, 0, unpacked(low_ref[...]))
-
-
-def incident_kernel(groups, w_ref, *refs):
-    fields, (part_ref, a_ref, out_ref) = refs[: len(groups)], refs[len(groups) :]
-    total = part_ref[...]
-    for group, field in zip(groups, fields):
-        total = total + weighted(w_ref, group, unpacked(field[...]))
+def first_incident_kernel(w_ref, low_ref, high_ref, part_ref, a_ref, out_ref):
+    total = part_ref[...] + weighted(w_ref, 0, unpacked(low_ref[...]))
+    finish(total + weighted(w_ref, 2, unpacked(high_ref[...])), a_ref, out_ref)
+
+
+def last_incident_kernel(w_ref, high_ref, d_ref, part_ref, a_ref, out_ref):
+    total = part_ref[...] + weighted(w_ref, 2, coeffs(unpacked(high_ref[...]), d_ref))
+    finish(total, a_ref, out_ref)
+
+
+def finish(total, a_ref, out_ref):
     row, col = iota((L, L), 0), iota((L, L), 1)
     same = ones(((row >> 3) == (col >> 3)) & (row < LAN))
     high, rest = two_terms(total)
@@ -217,16 +228,10 @@
     out_ref[...] = jnp.broadcast_to(packed(mine), (CHIPS, BLK, 128))
 
 
-def coeffs_kernel(where_am_i, in_ref, d_ref, d_other_ref, out_ref):
-    field = unpacked(in_ref[...])
-    even = (where_am_i[1] & 1) == 0
-    upper, lower = field[:L].astype(F32), field[L:].astype(F32)
-    first = jnp.where(even, upper, lower).astype(BF16)
-    second = jnp.where(even, lower, upper).astype(BF16)
-    out_ref[...] = packed(dot(d_ref[...], first) + dot(d_other_ref[...], second))
-
-
-def ready_kernel(p_ref, d_ref, p_out, d_out, lanes_out):
+def ready_kernel(where_am_i, half_ref, other_ref, p_ref, d_ref, full_out, p_out, d_out, lanes_out):
+    place = where_am_i[1] & 1
+    full_out[place] = half_ref[...]
+    full_out[1 - place] = other_ref[...]
     p_out[...] = dot(padding(), p_ref[...]).astype(BF16)
     d_out[...] = dot(d_ref[...], packing()).astype(BF16)
     row, col = iota((L, BD * 128), 0), iota((L, BD * 128), 1)
@@ -339,8 +344,8 @@
     )
     got = exchange(message)
     got, waves = lax.optimization_barrier((got, waves))
-    coeffs = call(first_kernel, (), (got,), shape(CHIPS, BLK, 128), "first")
-    low, high = from_previous(coeffs), from_next(coeffs)
+    first = call(first_kernel, (), (got,), shape(CHIPS, BLK, 128), "first")
+    low, high = from_previous(first), from_next(first)
     got_other = swapped(got)
     matrices, own_waves, half = call(
         place_kernel,
@@ -352,39 +357,44 @@
     matrices = matrices.reshape(SOURCES + 1, BD * BLK, 512)
     other_half = from_previous(half)
 
-    for step in range(ITERS):
-        if step:
-            coeffs = call(
-                coeffs_kernel,
-                (where_am_i,),
-                (got, half, other_half),
-                shape(CHIPS, BLK, 128),
-                "coeffs",
-            )
-            low, high = from_previous(coeffs), from_next(coeffs)
-            coeffs, panel_rows, diffract = lax.optimization_barrier((coeffs, panel_rows, diffract))
-            ready = call(
-                ready_kernel,
-                (),
-                (panel_rows.T, diffract),
-                (shape(ROWS, panel_rows.shape[0]), shape(S, ROWS), shape(C, L, BD * 128)),
-                "ready",
-            )
-            low, ready = lax.optimization_barrier((low, ready))
-        part = call(own_kernel, (), (matrices, coeffs), shape(BD * BLK, L, dtype=F32), "own")
-        groups, fields = (0, 2), (low, high)
-        if step:
-            low_shape = shape(BD * BLK, L, dtype=F32)
-            part = call(low_kernel, (), (matrices, low, part), low_shape, "low")
-            groups, fields = (2,), (high,)
-        message = call(
-            functools.partial(incident_kernel, groups),
+    part_shape = shape(BD * BLK, L, dtype=F32)
+    part = call(part_kernel, (), (matrices, first), part_shape, "part")
+    got = exchange(
+        call(
+            first_incident_kernel,
             (),
-            (matrices, *fields, part, own_waves),
+            (matrices, low, high, part, own_waves),
             shape(CHIPS, BLK, 128),
-            "incident",
+            "incident_first",
         )
-        got = exchange(message)
+    )
+    got, other_half = lax.optimization_barrier((got, other_half))
+    low, high = from_previous(got), from_next(got)
+    got, half, panel_rows, diffract = lax.optimization_barrier((got, half, panel_rows, diffract))
+    full, *ready = call(
+        ready_kernel,
+        (where_am_i,),
+        (half, other_half, panel_rows.T, diffract),
+        (
+            shape(2, ROWS, L),
+            shape(ROWS, panel_rows.shape[0]),
+            shape(S, ROWS),
+            shape(C, L, BD * 128),
+        ),
+        "ready",
+    )
+    part = call(own_kernel, (), (matrices, got, full), part_shape, "own")
+    low, part = lax.optimization_barrier((low, part))
+    part = call(low_kernel, (), (matrices, low, full, part), part_shape, "low")
+    got = exchange(
+        call(
+            last_incident_kernel,
+            (),
+            (matrices, high, full, part, own_waves),
+            shape(CHIPS, BLK, 128),
+            "incident_last",
+        )
+    )
     other = swapped(got)
     own_sources, own_outgoing = call(
         last_own_kernel,

time: 96.6 us -> 96.4 us (level)
    pallas_call x11 -> x10, Pallas kernels: 11.2 us -> 11.9 us  [call(): pl.pallas_call(kernel, out_shape=shapes, in_specs=[SM] * len(scalars) + [...]
  transfers between devices with their start and end apart: 9 -> 9, of which waited for: 4 -> 4; matrix products, arithmetic and copies ran while one was open for 1% -> 1% of each run, Pallas kernels for 8% -> 9%
where the time goes in v8:
time: 96.4 us; the launch traced here: 96.1 us
  blocking collectives  62.6 us (65%)
  starting transfers between devices  16.4 us (17%)
  Pallas kernels  13.9 us (14%)
  waiting for transfers between devices  1.42 us (1%)
    all_to_all x3, blocking collectives, exchange(): return lax.all_to_all(blocks, PLANE, 0, 0, tiled=True)  62.6 us
    pallas_call x10, Pallas kernels, call(): pl.pallas_call(kernel, out_shape=shapes, in_specs=[SM] * len(scalars) + [...  11.9 us
    ppermute x4, starting transfers between devices, swapped(): return lax.ppermute(value, 'c', [(0, 1), (1, 0)])  10.7 us
    ppermute x2, starting transfers between devices, from_next(): lax.ppermute(value, 'x', [((i + 1) % count, i) for i in range(count)])  3.17 us
    ppermute x3, starting transfers between devices, from_previous(): lax.ppermute(value, 'x', [(i, (i + 1) % count) for i in range(count)])  2.57 us
    pallas_call x1, Pallas kernels, shards(): pl.pallas_call(send_kernel, out_shape=shape(CHIPS, BLK, 1024), in_specs=[...  1.99 us
  transfers between devices with their start and end apart: 9, of which 4 were waited for; matrix products, arithmetic and copies ran while one was open for 1% of the time, Pallas kernels for 9%

profile of v8, /device:TPU:1, one launch (start us, length us, event | category | flops | bytes accessed | tf_op | source)
XLA Modules:
  0.0 96.1 jit_solution(12505891699013985538)
XLA Ops:
  0.6 0.0 copy-start
  0.7 3.3 %collective-permute-start.1 = (f32[7,8,36]{2,1,0:T(8,128)}, f32[7,8,36]{2,1,0:T(8,128)S(1)}, u32[]{:S(2)}, u32[]{:S(2)}) collective-permute-start(f32[7,8,36]{2,1,0:T(8,128)} %bitcast.24), channel_id=1, source_target_pairs={{0,1},{1,0},{2,3},{3,2},{4,5},{5,4},{6,7},{7,6},{8,9},{9,8},{10,11... | collective-permute-start | bytes 24200 | tf_op jit(solution)/shard_map/ppermute | solution.py:292
  4.0 0.1 collective-permute-start
  4.1 0.7 convolution_bitcast_fusion.wide_ref
  4.8 0.1 pad_add_fusion.where_am_i
  4.9 0.2 collective-permute-done.1.amb_other_ref
  5.0 0.3 collective-permute-done.other_ref
  5.4 2.0 %send.1 = bf16[32,16,1024]{2,1,0:T(8,128)(2,1)S(1)} custom-call(s32[2]{0:T(128)S(1)} %pad_add_fusion.where_am_i, s32[2]{0:T(128)} %source_hbm.1, s32[2]{0:T(128)} %target_hbm.1, s32[2]{0:T(128)} %live_hbm.1, bf16[7,448]{1,0:T(8,128)(2,1)} %d_ref, f32[7,8,36]{2,1,0:T(8,128)S(1)} %bitcast.23, f32[7,8,36]{2,1,0:T(8,128)S(1)} %collective-permute-done.other_ref, ...), custom_call_target="tpu_custom_call" | custom-call | tf_op jit(solution)/shard_map/send/pallas_call | solution.py:321
  7.4 0.0 copy-start.4
  7.4 35.5 %all_to_all.15.in_ref = bf16[32,16,1024]{2,1,0:T(8,128)(2,1)S(1)} all-to-all(bf16[32,16,1024]{2,1,0:T(8,128)(2,1)S(1)} %send.1), channel_id=1, replica_groups=mesh['x'=4,'z'=8,'y'=4,'c'=2] {'z','y'}, dimensions={0} | all-to-all | bytes 2097152 | tf_op jit(solution)/shard_map/all_to_all | solution.py:288
  42.9 2.8 %collective-permute-start.2 = (bf16[32,16,1024]{2,1,0:T(8,128)(2,1)S(1)}, bf16[32,16,1024]{2,1,0:T(8,128)(2,1)S(1)}, u32[]{:S(2)}, u32[]{:S(2)}) collective-permute-start(bf16[32,16,1024]{2,1,0:T(8,128)(2,1)S(1)} %all_to_all.15.in_ref), channel_id=1, source_target_pairs={{0,1},{1,0},{2,3},{3,2},{4,5},{5,4},{6,7},{7,6},{8,9},{9,8},{10,11... | collective-permute-start | bytes 3145736 | tf_op jit(solution)/shard_map/ppermute | solution.py:292
  45.7 0.4 first.1.own_ref
  46.1 1.3 %collective-permute-start.3 = (bf16[32,16,128]{2,1,0:T(8,128)(2,1)S(1)}, bf16[32,16,128]{2,1,0:T(8,128)(2,1)S(1)}, u32[]{:S(2)}, u32[]{:S(2)}) collective-permute-start(bf16[32,16,128]{2,1,0:T(8,128)(2,1)S(1)} %first.1.own_ref), channel_id=1, source_target_pairs={{0,64},{64,128},{128,192},{192,0},{1,65},{65,129},{129,193},{193,1... | collective-permute-start | bytes 393224 | tf_op jit(solution)/shard_map/ppermute | solution.py:297
  47.4 1.5 %collective-permute-start.4 = (bf16[32,16,128]{2,1,0:T(8,128)(2,1)S(1)}, bf16[32,16,128]{2,1,0:T(8,128)(2,1)S(1)}, u32[]{:S(2)}, u32[]{:S(2)}) collective-permute-start(bf16[32,16,128]{2,1,0:T(8,128)(2,1)S(1)} %first.1.own_ref), channel_id=1, source_target_pairs={{64,0},{128,64},{192,128},{0,192},{65,1},{129,65},{193,129},{1,193... | collective-permute-start | bytes 393224 | tf_op jit(solution)/shard_map/ppermute | solution.py:302
  49.0 1.9 %place.1 = (bf16[200,16,512]{2,1,0:T(8,128)(2,1)S(1)}, f32[16,256]{1,0:T(8,128)S(1)}, bf16[512,256]{1,0:T(8,128)(2,1)S(1)}) custom-call(s32[2]{0:T(128)S(1)} %pad_add_fusion.where_am_i, s32[32,1,2]{2,1,0:T(1,128)S(1)} %slice_convert_fusion.1.own_at, s32[32,1,2]{2,1,0:T(1,128)S(1)} %slice_convert_fusion.other_at, ...), custom_call_target="tpu_custom_call" | custom-call | tf_op jit(solution)/shard_map/place/pallas_call | solution.py:272
  50.9 0.3 collective-permute-start.5
  51.2 0.6 part.1.part_ref
  51.8 0.7 collective-permute-done.3.low_ref
  52.6 1.3 %incident_first.1 = bf16[32,16,128]{2,1,0:T(8,128)(2,1)S(1)} custom-call(bf16[25,128,512]{2,1,0:T(8,128)(2,1)S(1)} %bitcast.17, bf16[32,16,128]{2,1,0:T(8,128)(2,1)S(1)} %collective-permute-done.3.low_ref, bf16[32,16,128]{2,1,0:T(8,128)(2,1)S(1)} %collective-permute-done.4.high_ref, f32[128,256]{1,0:T(8,128)S(1)} %part.1.part_ref, ...), custom_call_target="tpu_custom_call" | custom-call | tf_op jit(solution)/shard_map/incident_first/pallas_call | solution.py:272
  53.9 14.5 %all_to_all.16.own_ref = bf16[32,16,128]{2,1,0:T(8,128)(2,1)S(1)} all-to-all(bf16[32,16,128]{2,1,0:T(8,128)(2,1)S(1)} %incident_first.1), channel_id=1, replica_groups=mesh['x'=4,'z'=8,'y'=4,'c'=2] {'z','y'}, dimensions={0} | all-to-all | bytes 262144 | tf_op jit(solution)/shard_map/all_to_all | solution.py:288
  68.4 0.0 collective-permute-done.5.other_ref
  68.4 1.0 %collective-permute-start.7 = (bf16[32,16,128]{2,1,0:T(8,128)(2,1)S(1)}, bf16[32,16,128]{2,1,0:T(8,128)(2,1)S(1)}, u32[]{:S(2)}, u32[]{:S(2)}) collective-permute-start(bf16[32,16,128]{2,1,0:T(8,128)(2,1)S(1)} %all_to_all.16.own_ref), channel_id=1, source_target_pairs={{0,64},{64,128},{128,192},{192,0},{1,65},{65,129},{129,193},{193,1... | collective-permute-start | bytes 393224 | tf_op jit(solution)/shard_map/ppermute | solution.py:297
  69.4 1.7 %collective-permute-start.6 = (bf16[32,16,128]{2,1,0:T(8,128)(2,1)S(1)}, bf16[32,16,128]{2,1,0:T(8,128)(2,1)S(1)}, u32[]{:S(2)}, u32[]{:S(2)}) collective-permute-start(bf16[32,16,128]{2,1,0:T(8,128)(2,1)S(1)} %all_to_all.16.own_ref), channel_id=1, source_target_pairs={{64,0},{128,64},{192,128},{0,192},{65,1},{129,65},{193,129},{1,193... | collective-permute-start | bytes 393224 | tf_op jit(solution)/shard_map/ppermute | solution.py:302
  71.1 1.1 %ready.1 = (bf16[2,512,256]{2,1,0:T(8,128)(2,1)S(1)}, bf16[512,128]{1,0:T(8,128)(2,1)S(1)}, bf16[7,512]{1,0:T(8,128)(2,1)S(1)}, bf16[2,256,1024]{2,1,0:T(8,128)(2,1)S(1)}) custom-call(s32[2]{0:T(128)S(1)} %pad_add_fusion.where_am_i, bf16[512,256]{1,0:T(8,128)(2,1)S(1)} %get-tuple-element.33.half_ref, bf16[512,256]{1,0:T(8,128)(2,1)S(1)} %collective-permute-done.5.other_ref, ...), custom_call_target="tpu_custom_call" | custom-call | tf_op jit(solution)/shard_map/ready/pallas_call | solution.py:272
  72.1 1.1 %own.1.part_ref = f32[128,256]{1,0:T(8,128)S(1)} custom-call(bf16[25,128,512]{2,1,0:T(8,128)(2,1)S(1)} %bitcast.18, bf16[32,16,128]{2,1,0:T(8,128)(2,1)S(1)} %all_to_all.16.own_ref, bf16[2,512,256]{2,1,0:T(8,128)(2,1)S(1)} %get-tuple-element.37.d_ref), custom_call_target="tpu_custom_call" | custom-call | tf_op jit(solution)/shard_map/own/pallas_call | solution.py:272
  73.2 0.2 collective-permute-done.7.low_ref
  73.4 1.1 %low.1.part_ref = f32[128,256]{1,0:T(8,128)S(1)} custom-call(bf16[25,128,512]{2,1,0:T(8,128)(2,1)S(1)} %bitcast.19, bf16[32,16,128]{2,1,0:T(8,128)(2,1)S(1)} %collective-permute-done.7.low_ref, bf16[2,512,256]{2,1,0:T(8,128)(2,1)S(1)} %get-tuple-element.37.d_ref, f32[128,256]{1,0:T(8,128)S(1)} %own.1.part_ref), custom_call_target="tpu_custom_call" | custom-call | tf_op jit(solution)/shard_map/low/pallas_call | solution.py:272
  74.5 1.4 %incident_last.1 = bf16[32,16,128]{2,1,0:T(8,128)(2,1)S(1)} custom-call(bf16[25,128,512]{2,1,0:T(8,128)(2,1)S(1)} %bitcast.20, bf16[32,16,128]{2,1,0:T(8,128)(2,1)S(1)} %collective-permute-done.6.high_ref, bf16[2,512,256]{2,1,0:T(8,128)(2,1)S(1)} %get-tuple-element.37.d_ref, f32[128,256]{1,0:T(8,128)S(1)} %low.1.part_ref, f32[16,256]{1,0:T(8,128)S(1)} %get-tuple-element.30.a_ref), custom_call_target="tpu_custom_call" | custom-call | tf_op jit(solution)/shard_map/incident_last/pallas_call | solution.py:272
  76.0 12.6 %all_to_all.17.in_ref = bf16[32,16,128]{2,1,0:T(8,128)(2,1)S(1)} all-to-all(bf16[32,16,128]{2,1,0:T(8,128)(2,1)S(1)} %incident_last.1), channel_id=1, replica_groups=mesh['x'=4,'z'=8,'y'=4,'c'=2] {'z','y'}, dimensions={0} | all-to-all | bytes 262144 | tf_op jit(solution)/shard_map/all_to_all | solution.py:288
  88.6 4.5 %collective-permute-start.8 = (bf16[32,16,128]{2,1,0:T(8,128)(2,1)S(1)}, bf16[32,16,128]{2,1,0:T(8,128)(2,1)S(1)}, u32[]{:S(2)}, u32[]{:S(2)}) collective-permute-start(bf16[32,16,128]{2,1,0:T(8,128)(2,1)S(1)} %all_to_all.17.in_ref), channel_id=1, source_target_pairs={{0,1},{1,0},{2,3},{3,2},{4,5},{5,4},{6,7},{7,6},{8,9},{9,8},{10,11... | collective-permute-start | bytes 393224 | tf_op jit(solution)/shard_map/ppermute | solution.py:292
  93.1 1.2 %last_own.1 = (bf16[144,128]{1,0:T(8,128)(2,1)S(1)}, f32[7,1024]{1,0:T(8,128)S(1)}) custom-call(s32[2]{0:T(128)S(1)} %pad_add_fusion.where_am_i, bf16[32,16,128]{2,1,0:T(8,128)(2,1)S(1)} %all_to_all.17.in_ref, bf16[512,128]{1,0:T(8,128)(2,1)S(1)} %get-tuple-element.41.p_ref, bf16[7,512]{1,0:T(8,128)(2,1)S(1)} %get-tuple-element.42.d_ref, ...), custom_call_target="tpu_custom_call" | custom-call | tf_op jit(solution)/shard_map/last_own/pallas_call | solution.py:272
  94.3 1.8 %last.1 = (bf16[288,128]{1,0:T(8,128)(2,1)}, f32[7,8,36]{2,1,0:T(8,128)}) custom-call(s32[2]{0:T(128)S(1)} %pad_add_fusion.where_am_i, bf16[32,16,128]{2,1,0:T(8,128)(2,1)S(1)} %collective-permute-done.8.in_ref, bf16[512,128]{1,0:T(8,128)(2,1)S(1)} %get-tuple-element.41.p_ref, bf16[7,512]{1,0:T(8,128)(2,1)S(1)} %get-tuple-element.42.d_ref, ...), custom_call_target="tpu_custom_call" | custom-call | tf_op jit(solution)/shard_map/last/pallas_call | solution.py:272
  (16 shorter events, 0.1 us)
Async XLA Ops:
  0.6 3.5 %copy-start = (bf16[2,448,448]{2,1,0:T(8,128)(2,1)S(1)}, bf16[2,448,448]{2,1,0:T(8,128)(2,1)}, u32[]{:S(2)}) copy-start(bf16[2,448,448]{2,1,0:T(8,128)(2,1)} %param.10) | copy-start | bytes 2408452
  0.6 4.8 %copy-start.3 = (f32[8,36,7]{1,0,2:T(8,128)S(1)}, f32[8,36,7]{1,0,2:T(8,128)}, u32[]{:S(2)}) copy-start(f32[8,36,7]{1,0,2:T(8,128)} %param.9) | copy-start | bytes 24196
  0.7 4.4 %collective-permute-start.1 = (f32[7,8,36]{2,1,0:T(8,128)}, f32[7,8,36]{2,1,0:T(8,128)S(1)}, u32[]{:S(2)}, u32[]{:S(2)}) collective-permute-start(f32[7,8,36]{2,1,0:T(8,128)} %bitcast.24), channel_id=1, source_target_pairs={{0,1},{1,0},{2,3},{3,2},{4,5},{5,4},{6,7},{7,6},{8,9},{9,8},{10,11... | collective-permute-start | bytes 24200 | tf_op jit(solution)/shard_map/ppermute | solution.py:292
  4.0 1.4 %collective-permute-start = (f32[7,8,36]{2,1,0:T(8,128)}, f32[7,8,36]{2,1,0:T(8,128)S(1)}, u32[]{:S(2)}, u32[]{:S(2)}) collective-permute-start(f32[7,8,36]{2,1,0:T(8,128)} %bitcast.22), channel_id=1, source_target_pairs={{0,1},{1,0},{2,3},{3,2},{4,5},{5,4},{6,7},{7,6},{8,9},{9,8},{10,11... | collective-permute-start | bytes 24200 | tf_op jit(solution)/shard_map/ppermute | solution.py:292
  7.4 41.6 %copy-start.4 = (f32[8,36,7]{1,0,2:T(8,128)S(1)}, f32[8,36,7]{1,0,2:T(8,128)}, u32[]{:S(2)}) copy-start(f32[8,36,7]{1,0,2:T(8,128)} %param.8) | copy-start | bytes 24196
  42.9 6.0 %collective-permute-start.2 = (bf16[32,16,1024]{2,1,0:T(8,128)(2,1)S(1)}, bf16[32,16,1024]{2,1,0:T(8,128)(2,1)S(1)}, u32[]{:S(2)}, u32[]{:S(2)}) collective-permute-start(bf16[32,16,1024]{2,1,0:T(8,128)(2,1)S(1)} %all_to_all.15.in_ref), channel_id=1, source_target_pairs={{0,1},{1,0},{2,3},{3,2},{4,5},{5,4},{6,7},{7,6},{8,9},{9,8},{10,11... | collective-permute-start | bytes 3145736 | tf_op jit(solution)/shard_map/ppermute | solution.py:292
  46.1 6.4 %collective-permute-start.3 = (bf16[32,16,128]{2,1,0:T(8,128)(2,1)S(1)}, bf16[32,16,128]{2,1,0:T(8,128)(2,1)S(1)}, u32[]{:S(2)}, u32[]{:S(2)}) collective-permute-start(bf16[32,16,128]{2,1,0:T(8,128)(2,1)S(1)} %first.1.own_ref), channel_id=1, source_target_pairs={{0,64},{64,128},{128,192},{192,0},{1,65},{65,129},{129,193},{193,1... | collective-permute-start | bytes 393224 | tf_op jit(solution)/shard_map/ppermute | solution.py:297
  47.4 5.1 %collective-permute-start.4 = (bf16[32,16,128]{2,1,0:T(8,128)(2,1)S(1)}, bf16[32,16,128]{2,1,0:T(8,128)(2,1)S(1)}, u32[]{:S(2)}, u32[]{:S(2)}) collective-permute-start(bf16[32,16,128]{2,1,0:T(8,128)(2,1)S(1)} %first.1.own_ref), channel_id=1, source_target_pairs={{64,0},{128,64},{192,128},{0,192},{65,1},{129,65},{193,129},{1,193... | collective-permute-start | bytes 393224 | tf_op jit(solution)/shard_map/ppermute | solution.py:302
  50.9 17.5 %collective-permute-start.5 = (bf16[512,256]{1,0:T(8,128)(2,1)S(1)}, bf16[512,256]{1,0:T(8,128)(2,1)S(1)}, u32[]{:S(2)}, u32[]{:S(2)}) collective-permute-start(bf16[512,256]{1,0:T(8,128)(2,1)S(1)} %get-tuple-element.33.half_ref), channel_id=1, source_target_pairs={{0,64},{64,128},{128,192},{192,0},{1,65},{65,129},{129,193},{193,1... | collective-permute-start | bytes 786440 | tf_op jit(solution)/shard_map/ppermute | solution.py:297
  52.6 18.5 %copy-start.1 = (bf16[128,448]{0,1:T(8,128)(2,1)S(1)}, bf16[128,448]{0,1:T(8,128)(2,1)}, u32[]{:S(2)}) copy-start(bf16[128,448]{0,1:T(8,128)(2,1)} %param.15) | copy-start | bytes 344068
  52.6 18.5 %copy-start.2 = (bf16[7,448]{1,0:T(8,128)(2,1)S(1)}, bf16[7,448]{1,0:T(8,128)(2,1)}, u32[]{:S(2)}) copy-start(bf16[7,448]{1,0:T(8,128)(2,1)} %d_ref) | copy-start | bytes 18820
  68.4 5.0 %collective-permute-start.7 = (bf16[32,16,128]{2,1,0:T(8,128)(2,1)S(1)}, bf16[32,16,128]{2,1,0:T(8,128)(2,1)S(1)}, u32[]{:S(2)}, u32[]{:S(2)}) collective-permute-start(bf16[32,16,128]{2,1,0:T(8,128)(2,1)S(1)} %all_to_all.16.own_ref), channel_id=1, source_target_pairs={{0,64},{64,128},{128,192},{192,0},{1,65},{65,129},{129,193},{193,1... | collective-permute-start | bytes 393224 | tf_op jit(solution)/shard_map/ppermute | solution.py:297
  69.4 5.2 %collective-permute-start.6 = (bf16[32,16,128]{2,1,0:T(8,128)(2,1)S(1)}, bf16[32,16,128]{2,1,0:T(8,128)(2,1)S(1)}, u32[]{:S(2)}, u32[]{:S(2)}) collective-permute-start(bf16[32,16,128]{2,1,0:T(8,128)(2,1)S(1)} %all_to_all.16.own_ref), channel_id=1, source_target_pairs={{64,0},{128,64},{192,128},{0,192},{65,1},{129,65},{193,129},{1,193... | collective-permute-start | bytes 393224 | tf_op jit(solution)/shard_map/ppermute | solution.py:302
  88.6 5.7 %collective-permute-start.8 = (bf16[32,16,128]{2,1,0:T(8,128)(2,1)S(1)}, bf16[32,16,128]{2,1,0:T(8,128)(2,1)S(1)}, u32[]{:S(2)}, u32[]{:S(2)}) collective-permute-start(bf16[32,16,128]{2,1,0:T(8,128)(2,1)S(1)} %all_to_all.17.in_ref), channel_id=1, source_target_pairs={{0,1},{1,0},{2,3},{3,2},{4,5},{5,4},{6,7},{7,6},{8,9},{9,8},{10,11... | collective-permute-start | bytes 393224 | tf_op jit(solution)/shard_map/ppermute | solution.py:292

commit v9 on v8

--- a/solution.py
+++ b/solution.py
@@ -101,10 +101,10 @@
     return total
 
 
-def gaps(p, rows, dim):
-    dims = (rows, 128) if dim == 0 else (128, rows)
-    place, lane = iota(dims, dim), iota(dims, 1 - dim)
-    return ones((lane == 64 * p + 2 * (place >> 4) + (place & 15) - R) & ((place & 15) >= R))
+def gaps(p, dim):
+    place, lane = iota((128, 128), dim), iota((128, 128), 1 - dim)
+    start = jnp.where((place & 15) >= R, lane - 2 * (place >> 4) - (place & 15) + R, -1)
+    return jnp.concatenate([ones(start == 64 * p + 16 * t) for t in range(4)], axis=dim)
 
 
 def send_kernel(
@@ -117,7 +117,7 @@
         copy.start()
     field = chip_field(own_ref[...], other_ref[...], where_am_i[0], False)
     block = packed(field).reshape(BLK, 128)
-    fills = [dot(block, gaps(p, 2 * L, 1)) for p in range(2)]
+    fills = [dot(block, gaps(p, 1)) for p in range(2)]
     buoy = where_am_i[1]
     row, col = iota((M, L), 0), iota((M, L), 1)
     half = ones((row == HALF * (buoy & 1) + col - 2 * (col >> 4)) & ((col & 15) < R))
@@ -148,7 +148,7 @@
     block = 0.0
     for p in range(2):
         part = in_ref[:, :, 512 * p : 512 * (p + 1)].reshape(ROWS, 512)
-        block = block + dot(part, gaps(p, 512, 0))
+        block = block + dot(part, gaps(p, 0))
     out_ref[...] = block.reshape(CHIPS, BLK, 128).astype(BF16)
 
 
@@ -190,7 +190,7 @@
 
 
 def coeffs(field, d_ref):
-    return (dot(d_ref[0], field[:L]) + dot(d_ref[1], field[L:])).astype(BF16)
+    return dot(d_ref[...], field).astype(BF16)
 
 
 def own_kernel(w_ref, own_ref, d_ref, out_ref):
@@ -229,9 +229,10 @@
 
 
 def ready_kernel(where_am_i, half_ref, other_ref, p_ref, d_ref, full_out, p_out, d_out, lanes_out):
-    place = where_am_i[1] & 1
-    full_out[place] = half_ref[...]
-    full_out[1 - place] = other_ref[...]
+    even = (where_am_i[1] & 1) == 0
+    half, other = half_ref[...].astype(F32), other_ref[...].astype(F32)
+    full_out[:, :L] = jnp.where(even, half, other).astype(BF16)
+    full_out[:, L:] = jnp.where(even, other, half).astype(BF16)
     p_out[...] = dot(padding(), p_ref[...]).astype(BF16)
     d_out[...] = dot(d_ref[...], packing()).astype(BF16)
     row, col = iota((L, BD * 128), 0), iota((L, BD * 128), 1)
@@ -376,7 +377,7 @@
         (where_am_i,),
         (half, other_half, panel_rows.T, diffract),
         (
-            shape(2, ROWS, L),
+            shape(ROWS, 2 * L),
             shape(ROWS, panel_rows.shape[0]),
             shape(S, ROWS),
             shape(C, L, BD * 128),

time: 96.4 us -> 96.3 us (level)
  transfers between devices with their start and end apart: 9 -> 9, of which waited for: 4 -> 3; matrix products, arithmetic and copies ran while one was open for 1% -> 1% of each run, Pallas kernels for 9% -> 9%
where the time goes in v9:
time: 96.3 us; the launch traced here: 96 us
  blocking collectives  62.6 us (65%)
  starting transfers between devices  16.5 us (17%)
  Pallas kernels  14 us (15%)
  waiting for transfers between devices  1.29 us (1%)
    all_to_all x3, blocking collectives, exchange(): return lax.all_to_all(blocks, PLANE, 0, 0, tiled=True)  62.6 us
    pallas_call x10, Pallas kernels, call(): pl.pallas_call(kernel, out_shape=shapes, in_specs=[SM] * len(scalars) + [...  12 us
    ppermute x4, starting transfers between devices, swapped(): return lax.ppermute(value, 'c', [(0, 1), (1, 0)])  10.7 us
    ppermute x2, starting transfers between devices, from_next(): lax.ppermute(value, 'x', [((i + 1) % count, i) for i in range(count)])  3.17 us
    ppermute x3, starting transfers between devices, from_previous(): lax.ppermute(value, 'x', [(i, (i + 1) % count) for i in range(count)])  2.58 us
    pallas_call x1, Pallas kernels, shards(): pl.pallas_call(send_kernel, out_shape=shape(CHIPS, BLK, 1024), in_specs=[...  1.99 us
  transfers between devices with their start and end apart: 9, of which 3 were waited for; matrix products, arithmetic and copies ran while one was open for 1% of the time, Pallas kernels for 9%

profile of v9, /device:TPU:1, one launch (start us, length us, event | category | flops | bytes accessed | tf_op | source)
XLA Modules:
  0.0 96.0 jit_solution(10449643625793171459)
XLA Ops:
  0.6 0.0 copy-start
  0.7 3.3 %collective-permute-start.1 = (f32[7,8,36]{2,1,0:T(8,128)}, f32[7,8,36]{2,1,0:T(8,128)S(1)}, u32[]{:S(2)}, u32[]{:S(2)}) collective-permute-start(f32[7,8,36]{2,1,0:T(8,128)} %bitcast.24), channel_id=1, source_target_pairs={{0,1},{1,0},{2,3},{3,2},{4,5},{5,4},{6,7},{7,6},{8,9},{9,8},{10,11... | collective-permute-start | bytes 24200 | tf_op jit(solution)/shard_map/ppermute | solution.py:293
  4.0 0.1 collective-permute-start
  4.1 0.7 convolution_bitcast_fusion.wide_ref
  4.8 0.1 pad_add_fusion.where_am_i
  4.9 0.2 collective-permute-done.1.amb_other_ref
  5.0 0.3 collective-permute-done.other_ref
  5.4 2.0 %send.1 = bf16[32,16,1024]{2,1,0:T(8,128)(2,1)S(1)} custom-call(s32[2]{0:T(128)S(1)} %pad_add_fusion.where_am_i, s32[2]{0:T(128)} %source_hbm.1, s32[2]{0:T(128)} %target_hbm.1, s32[2]{0:T(128)} %live_hbm.1, bf16[7,448]{1,0:T(8,128)(2,1)} %d_ref, f32[7,8,36]{2,1,0:T(8,128)S(1)} %bitcast.23, f32[7,8,36]{2,1,0:T(8,128)S(1)} %collective-permute-done.other_ref, ...), custom_call_target="tpu_custom_call" | custom-call | tf_op jit(solution)/shard_map/send/pallas_call | solution.py:322
  7.4 0.0 copy-start.4
  7.4 35.5 %all_to_all.15.in_ref = bf16[32,16,1024]{2,1,0:T(8,128)(2,1)S(1)} all-to-all(bf16[32,16,1024]{2,1,0:T(8,128)(2,1)S(1)} %send.1), channel_id=1, replica_groups=mesh['x'=4,'z'=8,'y'=4,'c'=2] {'z','y'}, dimensions={0} | all-to-all | bytes 2097152 | tf_op jit(solution)/shard_map/all_to_all | solution.py:289
  42.9 2.8 %collective-permute-start.2 = (bf16[32,16,1024]{2,1,0:T(8,128)(2,1)S(1)}, bf16[32,16,1024]{2,1,0:T(8,128)(2,1)S(1)}, u32[]{:S(2)}, u32[]{:S(2)}) collective-permute-start(bf16[32,16,1024]{2,1,0:T(8,128)(2,1)S(1)} %all_to_all.15.in_ref), channel_id=1, source_target_pairs={{0,1},{1,0},{2,3},{3,2},{4,5},{5,4},{6,7},{7,6},{8,9},{9,8},{10,11... | collective-permute-start | bytes 3145736 | tf_op jit(solution)/shard_map/ppermute | solution.py:293
  45.7 0.4 first.1.own_ref
  46.1 1.3 %collective-permute-start.3 = (bf16[32,16,128]{2,1,0:T(8,128)(2,1)S(1)}, bf16[32,16,128]{2,1,0:T(8,128)(2,1)S(1)}, u32[]{:S(2)}, u32[]{:S(2)}) collective-permute-start(bf16[32,16,128]{2,1,0:T(8,128)(2,1)S(1)} %first.1.own_ref), channel_id=1, source_target_pairs={{0,64},{64,128},{128,192},{192,0},{1,65},{65,129},{129,193},{193,1... | collective-permute-start | bytes 393224 | tf_op jit(solution)/shard_map/ppermute | solution.py:298
  47.4 1.5 %collective-permute-start.4 = (bf16[32,16,128]{2,1,0:T(8,128)(2,1)S(1)}, bf16[32,16,128]{2,1,0:T(8,128)(2,1)S(1)}, u32[]{:S(2)}, u32[]{:S(2)}) collective-permute-start(bf16[32,16,128]{2,1,0:T(8,128)(2,1)S(1)} %first.1.own_ref), channel_id=1, source_target_pairs={{64,0},{128,64},{192,128},{0,192},{65,1},{129,65},{193,129},{1,193... | collective-permute-start | bytes 393224 | tf_op jit(solution)/shard_map/ppermute | solution.py:303
  48.9 0.0 collective-permute-done.2.other_ref
  49.0 1.9 %place.1 = (bf16[200,16,512]{2,1,0:T(8,128)(2,1)S(1)}, f32[16,256]{1,0:T(8,128)S(1)}, bf16[512,256]{1,0:T(8,128)(2,1)S(1)}) custom-call(s32[2]{0:T(128)S(1)} %pad_add_fusion.where_am_i, s32[32,1,2]{2,1,0:T(1,128)S(1)} %slice_convert_fusion.1.own_at, s32[32,1,2]{2,1,0:T(1,128)S(1)} %slice_convert_fusion.other_at, ...), custom_call_target="tpu_custom_call" | custom-call | tf_op jit(solution)/shard_map/place/pallas_call | solution.py:273
  50.9 0.3 collective-permute-start.5
  51.2 0.6 part.1.part_ref
  51.8 0.7 collective-permute-done.3.low_ref
  52.6 1.4 %incident_first.1 = bf16[32,16,128]{2,1,0:T(8,128)(2,1)S(1)} custom-call(bf16[25,128,512]{2,1,0:T(8,128)(2,1)S(1)} %bitcast.17, bf16[32,16,128]{2,1,0:T(8,128)(2,1)S(1)} %collective-permute-done.3.low_ref, bf16[32,16,128]{2,1,0:T(8,128)(2,1)S(1)} %collective-permute-done.4.high_ref, f32[128,256]{1,0:T(8,128)S(1)} %part.1.part_ref, ...), custom_call_target="tpu_custom_call" | custom-call | tf_op jit(solution)/shard_map/incident_first/pallas_call | solution.py:273
  53.9 14.5 %all_to_all.16.own_ref = bf16[32,16,128]{2,1,0:T(8,128)(2,1)S(1)} all-to-all(bf16[32,16,128]{2,1,0:T(8,128)(2,1)S(1)} %incident_first.1), channel_id=1, replica_groups=mesh['x'=4,'z'=8,'y'=4,'c'=2] {'z','y'}, dimensions={0} | all-to-all | bytes 262144 | tf_op jit(solution)/shard_map/all_to_all | solution.py:289
  68.4 1.0 %collective-permute-start.7 = (bf16[32,16,128]{2,1,0:T(8,128)(2,1)S(1)}, bf16[32,16,128]{2,1,0:T(8,128)(2,1)S(1)}, u32[]{:S(2)}, u32[]{:S(2)}) collective-permute-start(bf16[32,16,128]{2,1,0:T(8,128)(2,1)S(1)} %all_to_all.16.own_ref), channel_id=1, source_target_pairs={{0,64},{64,128},{128,192},{192,0},{1,65},{65,129},{129,193},{193,1... | collective-permute-start | bytes 393224 | tf_op jit(solution)/shard_map/ppermute | solution.py:298
  69.4 1.7 %collective-permute-start.6 = (bf16[32,16,128]{2,1,0:T(8,128)(2,1)S(1)}, bf16[32,16,128]{2,1,0:T(8,128)(2,1)S(1)}, u32[]{:S(2)}, u32[]{:S(2)}) collective-permute-start(bf16[32,16,128]{2,1,0:T(8,128)(2,1)S(1)} %all_to_all.16.own_ref), channel_id=1, source_target_pairs={{64,0},{128,64},{192,128},{0,192},{65,1},{129,65},{193,129},{1,193... | collective-permute-start | bytes 393224 | tf_op jit(solution)/shard_map/ppermute | solution.py:303
  71.1 1.2 %ready.1 = (bf16[512,512]{1,0:T(8,128)(2,1)S(1)}, bf16[512,128]{1,0:T(8,128)(2,1)S(1)}, bf16[7,512]{1,0:T(8,128)(2,1)S(1)}, bf16[2,256,1024]{2,1,0:T(8,128)(2,1)S(1)}) custom-call(s32[2]{0:T(128)S(1)} %pad_add_fusion.where_am_i, bf16[512,256]{1,0:T(8,128)(2,1)S(1)} %get-tuple-element.33.half_ref, bf16[512,256]{1,0:T(8,128)(2,1)S(1)} %collective-permute-done.5.other_ref, ...), custom_call_target="tpu_custom_call" | custom-call | tf_op jit(solution)/shard_map/ready/pallas_call | solution.py:273
  72.3 1.1 %own.1.part_ref = f32[128,256]{1,0:T(8,128)S(1)} custom-call(bf16[25,128,512]{2,1,0:T(8,128)(2,1)S(1)} %bitcast.18, bf16[32,16,128]{2,1,0:T(8,128)(2,1)S(1)} %all_to_all.16.own_ref, bf16[512,512]{1,0:T(8,128)(2,1)S(1)} %get-tuple-element.37.d_ref), custom_call_target="tpu_custom_call" | custom-call | tf_op jit(solution)/shard_map/own/pallas_call | solution.py:273
  73.4 0.0 collective-permute-done.7.low_ref
  73.4 1.1 %low.1.part_ref = f32[128,256]{1,0:T(8,128)S(1)} custom-call(bf16[25,128,512]{2,1,0:T(8,128)(2,1)S(1)} %bitcast.19, bf16[32,16,128]{2,1,0:T(8,128)(2,1)S(1)} %collective-permute-done.7.low_ref, bf16[512,512]{1,0:T(8,128)(2,1)S(1)} %get-tuple-element.37.d_ref, f32[128,256]{1,0:T(8,128)S(1)} %own.1.part_ref), custom_call_target="tpu_custom_call" | custom-call | tf_op jit(solution)/shard_map/low/pallas_call | solution.py:273
  74.5 1.4 %incident_last.1 = bf16[32,16,128]{2,1,0:T(8,128)(2,1)S(1)} custom-call(bf16[25,128,512]{2,1,0:T(8,128)(2,1)S(1)} %bitcast.20, bf16[32,16,128]{2,1,0:T(8,128)(2,1)S(1)} %collective-permute-done.6.high_ref, bf16[512,512]{1,0:T(8,128)(2,1)S(1)} %get-tuple-element.37.d_ref, f32[128,256]{1,0:T(8,128)S(1)} %low.1.part_ref, f32[16,256]{1,0:T(8,128)S(1)} %get-tuple-element.30.a_ref), custom_call_target="tpu_custom_call" | custom-call | tf_op jit(solution)/shard_map/incident_last/pallas_call | solution.py:273
  75.9 12.6 %all_to_all.17.in_ref = bf16[32,16,128]{2,1,0:T(8,128)(2,1)S(1)} all-to-all(bf16[32,16,128]{2,1,0:T(8,128)(2,1)S(1)} %incident_last.1), channel_id=1, replica_groups=mesh['x'=4,'z'=8,'y'=4,'c'=2] {'z','y'}, dimensions={0} | all-to-all | bytes 262144 | tf_op jit(solution)/shard_map/all_to_all | solution.py:289
  88.6 4.5 %collective-permute-start.8 = (bf16[32,16,128]{2,1,0:T(8,128)(2,1)S(1)}, bf16[32,16,128]{2,1,0:T(8,128)(2,1)S(1)}, u32[]{:S(2)}, u32[]{:S(2)}) collective-permute-start(bf16[32,16,128]{2,1,0:T(8,128)(2,1)S(1)} %all_to_all.17.in_ref), channel_id=1, source_target_pairs={{0,1},{1,0},{2,3},{3,2},{4,5},{5,4},{6,7},{7,6},{8,9},{9,8},{10,11... | collective-permute-start | bytes 393224 | tf_op jit(solution)/shard_map/ppermute | solution.py:293
  93.1 1.2 %last_own.1 = (bf16[144,128]{1,0:T(8,128)(2,1)S(1)}, f32[7,1024]{1,0:T(8,128)S(1)}) custom-call(s32[2]{0:T(128)S(1)} %pad_add_fusion.where_am_i, bf16[32,16,128]{2,1,0:T(8,128)(2,1)S(1)} %all_to_all.17.in_ref, bf16[512,128]{1,0:T(8,128)(2,1)S(1)} %get-tuple-element.41.p_ref, bf16[7,512]{1,0:T(8,128)(2,1)S(1)} %get-tuple-element.42.d_ref, ...), custom_call_target="tpu_custom_call" | custom-call | tf_op jit(solution)/shard_map/last_own/pallas_call | solution.py:273
  94.2 1.8 %last.1 = (bf16[288,128]{1,0:T(8,128)(2,1)}, f32[7,8,36]{2,1,0:T(8,128)}) custom-call(s32[2]{0:T(128)S(1)} %pad_add_fusion.where_am_i, bf16[32,16,128]{2,1,0:T(8,128)(2,1)S(1)} %collective-permute-done.8.in_ref, bf16[512,128]{1,0:T(8,128)(2,1)S(1)} %get-tuple-element.41.p_ref, bf16[7,512]{1,0:T(8,128)(2,1)S(1)} %get-tuple-element.42.d_ref, ...), custom_call_target="tpu_custom_call" | custom-call | tf_op jit(solution)/shard_map/last/pallas_call | solution.py:273
  (16 shorter events, 0.1 us)
Async XLA Ops:
  0.6 3.5 %copy-start = (bf16[2,448,448]{2,1,0:T(8,128)(2,1)S(1)}, bf16[2,448,448]{2,1,0:T(8,128)(2,1)}, u32[]{:S(2)}) copy-start(bf16[2,448,448]{2,1,0:T(8,128)(2,1)} %param.10) | copy-start | bytes 2408452
  0.6 4.8 %copy-start.3 = (f32[8,36,7]{1,0,2:T(8,128)S(1)}, f32[8,36,7]{1,0,2:T(8,128)}, u32[]{:S(2)}) copy-start(f32[8,36,7]{1,0,2:T(8,128)} %param.9) | copy-start | bytes 24196
  0.7 4.4 %collective-permute-start.1 = (f32[7,8,36]{2,1,0:T(8,128)}, f32[7,8,36]{2,1,0:T(8,128)S(1)}, u32[]{:S(2)}, u32[]{:S(2)}) collective-permute-start(f32[7,8,36]{2,1,0:T(8,128)} %bitcast.24), channel_id=1, source_target_pairs={{0,1},{1,0},{2,3},{3,2},{4,5},{5,4},{6,7},{7,6},{8,9},{9,8},{10,11... | collective-permute-start | bytes 24200 | tf_op jit(solution)/shard_map/ppermute | solution.py:293
  4.0 1.4 %collective-permute-start = (f32[7,8,36]{2,1,0:T(8,128)}, f32[7,8,36]{2,1,0:T(8,128)S(1)}, u32[]{:S(2)}, u32[]{:S(2)}) collective-permute-start(f32[7,8,36]{2,1,0:T(8,128)} %bitcast.22), channel_id=1, source_target_pairs={{0,1},{1,0},{2,3},{3,2},{4,5},{5,4},{6,7},{7,6},{8,9},{9,8},{10,11... | collective-permute-start | bytes 24200 | tf_op jit(solution)/shard_map/ppermute | solution.py:293
  7.4 41.6 %copy-start.4 = (f32[8,36,7]{1,0,2:T(8,128)S(1)}, f32[8,36,7]{1,0,2:T(8,128)}, u32[]{:S(2)}) copy-start(f32[8,36,7]{1,0,2:T(8,128)} %param.8) | copy-start | bytes 24196
  42.9 6.0 %collective-permute-start.2 = (bf16[32,16,1024]{2,1,0:T(8,128)(2,1)S(1)}, bf16[32,16,1024]{2,1,0:T(8,128)(2,1)S(1)}, u32[]{:S(2)}, u32[]{:S(2)}) collective-permute-start(bf16[32,16,1024]{2,1,0:T(8,128)(2,1)S(1)} %all_to_all.15.in_ref), channel_id=1, source_target_pairs={{0,1},{1,0},{2,3},{3,2},{4,5},{5,4},{6,7},{7,6},{8,9},{9,8},{10,11... | collective-permute-start | bytes 3145736 | tf_op jit(solution)/shard_map/ppermute | solution.py:293
  46.1 6.4 %collective-permute-start.3 = (bf16[32,16,128]{2,1,0:T(8,128)(2,1)S(1)}, bf16[32,16,128]{2,1,0:T(8,128)(2,1)S(1)}, u32[]{:S(2)}, u32[]{:S(2)}) collective-permute-start(bf16[32,16,128]{2,1,0:T(8,128)(2,1)S(1)} %first.1.own_ref), channel_id=1, source_target_pairs={{0,64},{64,128},{128,192},{192,0},{1,65},{65,129},{129,193},{193,1... | collective-permute-start | bytes 393224 | tf_op jit(solution)/shard_map/ppermute | solution.py:298
  47.4 5.1 %collective-permute-start.4 = (bf16[32,16,128]{2,1,0:T(8,128)(2,1)S(1)}, bf16[32,16,128]{2,1,0:T(8,128)(2,1)S(1)}, u32[]{:S(2)}, u32[]{:S(2)}) collective-permute-start(bf16[32,16,128]{2,1,0:T(8,128)(2,1)S(1)} %first.1.own_ref), channel_id=1, source_target_pairs={{64,0},{128,64},{192,128},{0,192},{65,1},{129,65},{193,129},{1,193... | collective-permute-start | bytes 393224 | tf_op jit(solution)/shard_map/ppermute | solution.py:303
  50.9 17.5 %collective-permute-start.5 = (bf16[512,256]{1,0:T(8,128)(2,1)S(1)}, bf16[512,256]{1,0:T(8,128)(2,1)S(1)}, u32[]{:S(2)}, u32[]{:S(2)}) collective-permute-start(bf16[512,256]{1,0:T(8,128)(2,1)S(1)} %get-tuple-element.33.half_ref), channel_id=1, source_target_pairs={{0,64},{64,128},{128,192},{192,0},{1,65},{65,129},{129,193},{193,1... | collective-permute-start | bytes 786440 | tf_op jit(solution)/shard_map/ppermute | solution.py:298
  52.5 18.5 %copy-start.1 = (bf16[128,448]{0,1:T(8,128)(2,1)S(1)}, bf16[128,448]{0,1:T(8,128)(2,1)}, u32[]{:S(2)}) copy-start(bf16[128,448]{0,1:T(8,128)(2,1)} %param.15) | copy-start | bytes 344068
  52.6 18.5 %copy-start.2 = (bf16[7,448]{1,0:T(8,128)(2,1)S(1)}, bf16[7,448]{1,0:T(8,128)(2,1)}, u32[]{:S(2)}) copy-start(bf16[7,448]{1,0:T(8,128)(2,1)} %d_ref) | copy-start | bytes 18820
  68.4 5.0 %collective-permute-start.7 = (bf16[32,16,128]{2,1,0:T(8,128)(2,1)S(1)}, bf16[32,16,128]{2,1,0:T(8,128)(2,1)S(1)}, u32[]{:S(2)}, u32[]{:S(2)}) collective-permute-start(bf16[32,16,128]{2,1,0:T(8,128)(2,1)S(1)} %all_to_all.16.own_ref), channel_id=1, source_target_pairs={{0,64},{64,128},{128,192},{192,0},{1,65},{65,129},{129,193},{193,1... | collective-permute-start | bytes 393224 | tf_op jit(solution)/shard_map/ppermute | solution.py:298
  69.4 5.2 %collective-permute-start.6 = (bf16[32,16,128]{2,1,0:T(8,128)(2,1)S(1)}, bf16[32,16,128]{2,1,0:T(8,128)(2,1)S(1)}, u32[]{:S(2)}, u32[]{:S(2)}) collective-permute-start(bf16[32,16,128]{2,1,0:T(8,128)(2,1)S(1)} %all_to_all.16.own_ref), channel_id=1, source_target_pairs={{64,0},{128,64},{192,128},{0,192},{65,1},{129,65},{193,129},{1,193... | collective-permute-start | bytes 393224 | tf_op jit(solution)/shard_map/ppermute | solution.py:303
  88.6 5.7 %collective-permute-start.8 = (bf16[32,16,128]{2,1,0:T(8,128)(2,1)S(1)}, bf16[32,16,128]{2,1,0:T(8,128)(2,1)S(1)}, u32[]{:S(2)}, u32[]{:S(2)}) collective-permute-start(bf16[32,16,128]{2,1,0:T(8,128)(2,1)S(1)} %all_to_all.17.in_ref), channel_id=1, source_target_pairs={{0,1},{1,0},{2,3},{3,2},{4,5},{5,4},{6,7},{7,6},{8,9},{9,8},{10,11... | collective-permute-start | bytes 393224 | tf_op jit(solution)/shard_map/ppermute | solution.py:293

commit v10 on v9

--- a/solution.py
+++ b/solution.py
@@ -219,7 +219,8 @@
     row, col = iota((L, L), 0), iota((L, L), 1)
     same = ones(((row >> 3) == (col >> 3)) & (row < LAN))
     high, rest = two_terms(total)
-    total = dot(high, same) + dot(rest, same)
+    total = dot(jnp.concatenate([high, rest], axis=0), same)
+    total = total[: BD * BLK] + total[BD * BLK :]
     row, lane = iota((BLK, L), 0), iota((BLK, L), 1)
     mine = a_ref[...]
     for t in range(BD):

time: 96.3 us -> 96.3 us (level)
  no operation moved by 1% of the time
where the time goes in v10:
time: 96.3 us; the launch traced here: 96 us
  blocking collectives  62.6 us (65%)
  starting transfers between devices  16.5 us (17%)
  Pallas kernels  14 us (15%)
  waiting for transfers between devices  1.29 us (1%)
    all_to_all x3, blocking collectives, exchange(): return lax.all_to_all(blocks, PLANE, 0, 0, tiled=True)  62.6 us
    pallas_call x10, Pallas kernels, call(): pl.pallas_call(kernel, out_shape=shapes, in_specs=[SM] * len(scalars) + [...  12 us
    ppermute x4, starting transfers between devices, swapped(): return lax.ppermute(value, 'c', [(0, 1), (1, 0)])  10.7 us
    ppermute x2, starting transfers between devices, from_next(): lax.ppermute(value, 'x', [((i + 1) % count, i) for i in range(count)])  3.17 us
    ppermute x3, starting transfers between devices, from_previous(): lax.ppermute(value, 'x', [(i, (i + 1) % count) for i in range(count)])  2.58 us
    pallas_call x1, Pallas kernels, shards(): pl.pallas_call(send_kernel, out_shape=shape(CHIPS, BLK, 1024), in_specs=[...  1.99 us
  transfers between devices with their start and end apart: 9, of which 3 were waited for; matrix products, arithmetic and copies ran while one was open for 1% of the time, Pallas kernels for 9%

profile of v10, /device:TPU:1, one launch (start us, length us, event | category | flops | bytes accessed | tf_op | source)
XLA Modules:
  0.0 96.0 jit_solution(12595862463619874017)
XLA Ops:
  0.6 0.0 copy-start
  0.7 3.3 %collective-permute-start.1 = (f32[7,8,36]{2,1,0:T(8,128)}, f32[7,8,36]{2,1,0:T(8,128)S(1)}, u32[]{:S(2)}, u32[]{:S(2)}) collective-permute-start(f32[7,8,36]{2,1,0:T(8,128)} %bitcast.24), channel_id=1, source_target_pairs={{0,1},{1,0},{2,3},{3,2},{4,5},{5,4},{6,7},{7,6},{8,9},{9,8},{10,11... | collective-permute-start | bytes 24200 | tf_op jit(solution)/shard_map/ppermute | solution.py:294
  4.0 0.1 collective-permute-start
  4.1 0.7 convolution_bitcast_fusion.wide_ref
  4.8 0.1 pad_add_fusion.where_am_i
  4.9 0.2 collective-permute-done.1.amb_other_ref
  5.0 0.3 collective-permute-done.other_ref
  5.4 2.0 %send.1 = bf16[32,16,1024]{2,1,0:T(8,128)(2,1)S(1)} custom-call(s32[2]{0:T(128)S(1)} %pad_add_fusion.where_am_i, s32[2]{0:T(128)} %source_hbm.1, s32[2]{0:T(128)} %target_hbm.1, s32[2]{0:T(128)} %live_hbm.1, bf16[7,448]{1,0:T(8,128)(2,1)} %d_ref, f32[7,8,36]{2,1,0:T(8,128)S(1)} %bitcast.23, f32[7,8,36]{2,1,0:T(8,128)S(1)} %collective-permute-done.other_ref, ...), custom_call_target="tpu_custom_call" | custom-call | tf_op jit(solution)/shard_map/send/pallas_call | solution.py:323
  7.4 0.0 copy-start.4
  7.4 35.5 %all_to_all.15.in_ref = bf16[32,16,1024]{2,1,0:T(8,128)(2,1)S(1)} all-to-all(bf16[32,16,1024]{2,1,0:T(8,128)(2,1)S(1)} %send.1), channel_id=1, replica_groups=mesh['x'=4,'z'=8,'y'=4,'c'=2] {'z','y'}, dimensions={0} | all-to-all | bytes 2097152 | tf_op jit(solution)/shard_map/all_to_all | solution.py:290
  42.9 2.8 %collective-permute-start.2 = (bf16[32,16,1024]{2,1,0:T(8,128)(2,1)S(1)}, bf16[32,16,1024]{2,1,0:T(8,128)(2,1)S(1)}, u32[]{:S(2)}, u32[]{:S(2)}) collective-permute-start(bf16[32,16,1024]{2,1,0:T(8,128)(2,1)S(1)} %all_to_all.15.in_ref), channel_id=1, source_target_pairs={{0,1},{1,0},{2,3},{3,2},{4,5},{5,4},{6,7},{7,6},{8,9},{9,8},{10,11... | collective-permute-start | bytes 3145736 | tf_op jit(solution)/shard_map/ppermute | solution.py:294
  45.7 0.4 first.1.own_ref
  46.1 1.3 %collective-permute-start.3 = (bf16[32,16,128]{2,1,0:T(8,128)(2,1)S(1)}, bf16[32,16,128]{2,1,0:T(8,128)(2,1)S(1)}, u32[]{:S(2)}, u32[]{:S(2)}) collective-permute-start(bf16[32,16,128]{2,1,0:T(8,128)(2,1)S(1)} %first.1.own_ref), channel_id=1, source_target_pairs={{0,64},{64,128},{128,192},{192,0},{1,65},{65,129},{129,193},{193,1... | collective-permute-start | bytes 393224 | tf_op jit(solution)/shard_map/ppermute | solution.py:299
  47.4 1.5 %collective-permute-start.4 = (bf16[32,16,128]{2,1,0:T(8,128)(2,1)S(1)}, bf16[32,16,128]{2,1,0:T(8,128)(2,1)S(1)}, u32[]{:S(2)}, u32[]{:S(2)}) collective-permute-start(bf16[32,16,128]{2,1,0:T(8,128)(2,1)S(1)} %first.1.own_ref), channel_id=1, source_target_pairs={{64,0},{128,64},{192,128},{0,192},{65,1},{129,65},{193,129},{1,193... | collective-permute-start | bytes 393224 | tf_op jit(solution)/shard_map/ppermute | solution.py:304
  48.9 0.0 collective-permute-done.2.other_ref
  49.0 1.9 %place.1 = (bf16[200,16,512]{2,1,0:T(8,128)(2,1)S(1)}, f32[16,256]{1,0:T(8,128)S(1)}, bf16[512,256]{1,0:T(8,128)(2,1)S(1)}) custom-call(s32[2]{0:T(128)S(1)} %pad_add_fusion.where_am_i, s32[32,1,2]{2,1,0:T(1,128)S(1)} %slice_convert_fusion.1.own_at, s32[32,1,2]{2,1,0:T(1,128)S(1)} %slice_convert_fusion.other_at, ...), custom_call_target="tpu_custom_call" | custom-call | tf_op jit(solution)/shard_map/place/pallas_call | solution.py:274
  50.9 0.3 collective-permute-start.5
  51.2 0.6 part.1.part_ref
  51.8 0.7 collective-permute-done.3.low_ref
  52.6 1.3 %incident_first.1 = bf16[32,16,128]{2,1,0:T(8,128)(2,1)S(1)} custom-call(bf16[25,128,512]{2,1,0:T(8,128)(2,1)S(1)} %bitcast.17, bf16[32,16,128]{2,1,0:T(8,128)(2,1)S(1)} %collective-permute-done.3.low_ref, bf16[32,16,128]{2,1,0:T(8,128)(2,1)S(1)} %collective-permute-done.4.high_ref, f32[128,256]{1,0:T(8,128)S(1)} %part.1.part_ref, ...), custom_call_target="tpu_custom_call" | custom-call | tf_op jit(solution)/shard_map/incident_first/pallas_call | solution.py:274
  53.9 14.5 %all_to_all.16.own_ref = bf16[32,16,128]{2,1,0:T(8,128)(2,1)S(1)} all-to-all(bf16[32,16,128]{2,1,0:T(8,128)(2,1)S(1)} %incident_first.1), channel_id=1, replica_groups=mesh['x'=4,'z'=8,'y'=4,'c'=2] {'z','y'}, dimensions={0} | all-to-all | bytes 262144 | tf_op jit(solution)/shard_map/all_to_all | solution.py:290
  68.4 1.0 %collective-permute-start.7 = (bf16[32,16,128]{2,1,0:T(8,128)(2,1)S(1)}, bf16[32,16,128]{2,1,0:T(8,128)(2,1)S(1)}, u32[]{:S(2)}, u32[]{:S(2)}) collective-permute-start(bf16[32,16,128]{2,1,0:T(8,128)(2,1)S(1)} %all_to_all.16.own_ref), channel_id=1, source_target_pairs={{0,64},{64,128},{128,192},{192,0},{1,65},{65,129},{129,193},{193,1... | collective-permute-start | bytes 393224 | tf_op jit(solution)/shard_map/ppermute | solution.py:299
  69.4 1.7 %collective-permute-start.6 = (bf16[32,16,128]{2,1,0:T(8,128)(2,1)S(1)}, bf16[32,16,128]{2,1,0:T(8,128)(2,1)S(1)}, u32[]{:S(2)}, u32[]{:S(2)}) collective-permute-start(bf16[32,16,128]{2,1,0:T(8,128)(2,1)S(1)} %all_to_all.16.own_ref), channel_id=1, source_target_pairs={{64,0},{128,64},{192,128},{0,192},{65,1},{129,65},{193,129},{1,193... | collective-permute-start | bytes 393224 | tf_op jit(solution)/shard_map/ppermute | solution.py:304
  71.1 1.2 %ready.1 = (bf16[512,512]{1,0:T(8,128)(2,1)S(1)}, bf16[512,128]{1,0:T(8,128)(2,1)S(1)}, bf16[7,512]{1,0:T(8,128)(2,1)S(1)}, bf16[2,256,1024]{2,1,0:T(8,128)(2,1)S(1)}) custom-call(s32[2]{0:T(128)S(1)} %pad_add_fusion.where_am_i, bf16[512,256]{1,0:T(8,128)(2,1)S(1)} %get-tuple-element.33.half_ref, bf16[512,256]{1,0:T(8,128)(2,1)S(1)} %collective-permute-done.5.other_ref, ...), custom_call_target="tpu_custom_call" | custom-call | tf_op jit(solution)/shard_map/ready/pallas_call | solution.py:274
  72.3 1.1 %own.1.part_ref = f32[128,256]{1,0:T(8,128)S(1)} custom-call(bf16[25,128,512]{2,1,0:T(8,128)(2,1)S(1)} %bitcast.18, bf16[32,16,128]{2,1,0:T(8,128)(2,1)S(1)} %all_to_all.16.own_ref, bf16[512,512]{1,0:T(8,128)(2,1)S(1)} %get-tuple-element.37.d_ref), custom_call_target="tpu_custom_call" | custom-call | tf_op jit(solution)/shard_map/own/pallas_call | solution.py:274
  73.4 0.0 collective-permute-done.7.low_ref
  73.4 1.1 %low.1.part_ref = f32[128,256]{1,0:T(8,128)S(1)} custom-call(bf16[25,128,512]{2,1,0:T(8,128)(2,1)S(1)} %bitcast.19, bf16[32,16,128]{2,1,0:T(8,128)(2,1)S(1)} %collective-permute-done.7.low_ref, bf16[512,512]{1,0:T(8,128)(2,1)S(1)} %get-tuple-element.37.d_ref, f32[128,256]{1,0:T(8,128)S(1)} %own.1.part_ref), custom_call_target="tpu_custom_call" | custom-call | tf_op jit(solution)/shard_map/low/pallas_call | solution.py:274
  74.5 1.4 %incident_last.1 = bf16[32,16,128]{2,1,0:T(8,128)(2,1)S(1)} custom-call(bf16[25,128,512]{2,1,0:T(8,128)(2,1)S(1)} %bitcast.20, bf16[32,16,128]{2,1,0:T(8,128)(2,1)S(1)} %collective-permute-done.6.high_ref, bf16[512,512]{1,0:T(8,128)(2,1)S(1)} %get-tuple-element.37.d_ref, f32[128,256]{1,0:T(8,128)S(1)} %low.1.part_ref, f32[16,256]{1,0:T(8,128)S(1)} %get-tuple-element.30.a_ref), custom_call_target="tpu_custom_call" | custom-call | tf_op jit(solution)/shard_map/incident_last/pallas_call | solution.py:274
  75.9 12.6 %all_to_all.17.in_ref = bf16[32,16,128]{2,1,0:T(8,128)(2,1)S(1)} all-to-all(bf16[32,16,128]{2,1,0:T(8,128)(2,1)S(1)} %incident_last.1), channel_id=1, replica_groups=mesh['x'=4,'z'=8,'y'=4,'c'=2] {'z','y'}, dimensions={0} | all-to-all | bytes 262144 | tf_op jit(solution)/shard_map/all_to_all | solution.py:290
  88.5 4.5 %collective-permute-start.8 = (bf16[32,16,128]{2,1,0:T(8,128)(2,1)S(1)}, bf16[32,16,128]{2,1,0:T(8,128)(2,1)S(1)}, u32[]{:S(2)}, u32[]{:S(2)}) collective-permute-start(bf16[32,16,128]{2,1,0:T(8,128)(2,1)S(1)} %all_to_all.17.in_ref), channel_id=1, source_target_pairs={{0,1},{1,0},{2,3},{3,2},{4,5},{5,4},{6,7},{7,6},{8,9},{9,8},{10,11... | collective-permute-start | bytes 393224 | tf_op jit(solution)/shard_map/ppermute | solution.py:294
  93.0 1.2 %last_own.1 = (bf16[144,128]{1,0:T(8,128)(2,1)S(1)}, f32[7,1024]{1,0:T(8,128)S(1)}) custom-call(s32[2]{0:T(128)S(1)} %pad_add_fusion.where_am_i, bf16[32,16,128]{2,1,0:T(8,128)(2,1)S(1)} %all_to_all.17.in_ref, bf16[512,128]{1,0:T(8,128)(2,1)S(1)} %get-tuple-element.41.p_ref, bf16[7,512]{1,0:T(8,128)(2,1)S(1)} %get-tuple-element.42.d_ref, ...), custom_call_target="tpu_custom_call" | custom-call | tf_op jit(solution)/shard_map/last_own/pallas_call | solution.py:274
  94.2 1.8 %last.1 = (bf16[288,128]{1,0:T(8,128)(2,1)}, f32[7,8,36]{2,1,0:T(8,128)}) custom-call(s32[2]{0:T(128)S(1)} %pad_add_fusion.where_am_i, bf16[32,16,128]{2,1,0:T(8,128)(2,1)S(1)} %collective-permute-done.8.in_ref, bf16[512,128]{1,0:T(8,128)(2,1)S(1)} %get-tuple-element.41.p_ref, bf16[7,512]{1,0:T(8,128)(2,1)S(1)} %get-tuple-element.42.d_ref, ...), custom_call_target="tpu_custom_call" | custom-call | tf_op jit(solution)/shard_map/last/pallas_call | solution.py:274
  (16 shorter events, 0.1 us)
Async XLA Ops:
  0.6 3.5 %copy-start = (bf16[2,448,448]{2,1,0:T(8,128)(2,1)S(1)}, bf16[2,448,448]{2,1,0:T(8,128)(2,1)}, u32[]{:S(2)}) copy-start(bf16[2,448,448]{2,1,0:T(8,128)(2,1)} %param.10) | copy-start | bytes 2408452
  0.6 4.8 %copy-start.3 = (f32[8,36,7]{1,0,2:T(8,128)S(1)}, f32[8,36,7]{1,0,2:T(8,128)}, u32[]{:S(2)}) copy-start(f32[8,36,7]{1,0,2:T(8,128)} %param.9) | copy-start | bytes 24196
  0.7 4.4 %collective-permute-start.1 = (f32[7,8,36]{2,1,0:T(8,128)}, f32[7,8,36]{2,1,0:T(8,128)S(1)}, u32[]{:S(2)}, u32[]{:S(2)}) collective-permute-start(f32[7,8,36]{2,1,0:T(8,128)} %bitcast.24), channel_id=1, source_target_pairs={{0,1},{1,0},{2,3},{3,2},{4,5},{5,4},{6,7},{7,6},{8,9},{9,8},{10,11... | collective-permute-start | bytes 24200 | tf_op jit(solution)/shard_map/ppermute | solution.py:294
  4.0 1.4 %collective-permute-start = (f32[7,8,36]{2,1,0:T(8,128)}, f32[7,8,36]{2,1,0:T(8,128)S(1)}, u32[]{:S(2)}, u32[]{:S(2)}) collective-permute-start(f32[7,8,36]{2,1,0:T(8,128)} %bitcast.22), channel_id=1, source_target_pairs={{0,1},{1,0},{2,3},{3,2},{4,5},{5,4},{6,7},{7,6},{8,9},{9,8},{10,11... | collective-permute-start | bytes 24200 | tf_op jit(solution)/shard_map/ppermute | solution.py:294
  7.4 41.6 %copy-start.4 = (f32[8,36,7]{1,0,2:T(8,128)S(1)}, f32[8,36,7]{1,0,2:T(8,128)}, u32[]{:S(2)}) copy-start(f32[8,36,7]{1,0,2:T(8,128)} %param.8) | copy-start | bytes 24196
  42.9 6.0 %collective-permute-start.2 = (bf16[32,16,1024]{2,1,0:T(8,128)(2,1)S(1)}, bf16[32,16,1024]{2,1,0:T(8,128)(2,1)S(1)}, u32[]{:S(2)}, u32[]{:S(2)}) collective-permute-start(bf16[32,16,1024]{2,1,0:T(8,128)(2,1)S(1)} %all_to_all.15.in_ref), channel_id=1, source_target_pairs={{0,1},{1,0},{2,3},{3,2},{4,5},{5,4},{6,7},{7,6},{8,9},{9,8},{10,11... | collective-permute-start | bytes 3145736 | tf_op jit(solution)/shard_map/ppermute | solution.py:294
  46.1 6.4 %collective-permute-start.3 = (bf16[32,16,128]{2,1,0:T(8,128)(2,1)S(1)}, bf16[32,16,128]{2,1,0:T(8,128)(2,1)S(1)}, u32[]{:S(2)}, u32[]{:S(2)}) collective-permute-start(bf16[32,16,128]{2,1,0:T(8,128)(2,1)S(1)} %first.1.own_ref), channel_id=1, source_target_pairs={{0,64},{64,128},{128,192},{192,0},{1,65},{65,129},{129,193},{193,1... | collective-permute-start | bytes 393224 | tf_op jit(solution)/shard_map/ppermute | solution.py:299
  47.4 5.1 %collective-permute-start.4 = (bf16[32,16,128]{2,1,0:T(8,128)(2,1)S(1)}, bf16[32,16,128]{2,1,0:T(8,128)(2,1)S(1)}, u32[]{:S(2)}, u32[]{:S(2)}) collective-permute-start(bf16[32,16,128]{2,1,0:T(8,128)(2,1)S(1)} %first.1.own_ref), channel_id=1, source_target_pairs={{64,0},{128,64},{192,128},{0,192},{65,1},{129,65},{193,129},{1,193... | collective-permute-start | bytes 393224 | tf_op jit(solution)/shard_map/ppermute | solution.py:304
  50.9 17.5 %collective-permute-start.5 = (bf16[512,256]{1,0:T(8,128)(2,1)S(1)}, bf16[512,256]{1,0:T(8,128)(2,1)S(1)}, u32[]{:S(2)}, u32[]{:S(2)}) collective-permute-start(bf16[512,256]{1,0:T(8,128)(2,1)S(1)} %get-tuple-element.33.half_ref), channel_id=1, source_target_pairs={{0,64},{64,128},{128,192},{192,0},{1,65},{65,129},{129,193},{193,1... | collective-permute-start | bytes 786440 | tf_op jit(solution)/shard_map/ppermute | solution.py:299
  52.5 18.5 %copy-start.1 = (bf16[128,448]{0,1:T(8,128)(2,1)S(1)}, bf16[128,448]{0,1:T(8,128)(2,1)}, u32[]{:S(2)}) copy-start(bf16[128,448]{0,1:T(8,128)(2,1)} %param.15) | copy-start | bytes 344068
  52.6 18.5 %copy-start.2 = (bf16[7,448]{1,0:T(8,128)(2,1)S(1)}, bf16[7,448]{1,0:T(8,128)(2,1)}, u32[]{:S(2)}) copy-start(bf16[7,448]{1,0:T(8,128)(2,1)} %d_ref) | copy-start | bytes 18820
  68.4 5.0 %collective-permute-start.7 = (bf16[32,16,128]{2,1,0:T(8,128)(2,1)S(1)}, bf16[32,16,128]{2,1,0:T(8,128)(2,1)S(1)}, u32[]{:S(2)}, u32[]{:S(2)}) collective-permute-start(bf16[32,16,128]{2,1,0:T(8,128)(2,1)S(1)} %all_to_all.16.own_ref), channel_id=1, source_target_pairs={{0,64},{64,128},{128,192},{192,0},{1,65},{65,129},{129,193},{193,1... | collective-permute-start | bytes 393224 | tf_op jit(solution)/shard_map/ppermute | solution.py:299
  69.4 5.2 %collective-permute-start.6 = (bf16[32,16,128]{2,1,0:T(8,128)(2,1)S(1)}, bf16[32,16,128]{2,1,0:T(8,128)(2,1)S(1)}, u32[]{:S(2)}, u32[]{:S(2)}) collective-permute-start(bf16[32,16,128]{2,1,0:T(8,128)(2,1)S(1)} %all_to_all.16.own_ref), channel_id=1, source_target_pairs={{64,0},{128,64},{192,128},{0,192},{65,1},{129,65},{193,129},{1,193... | collective-permute-start | bytes 393224 | tf_op jit(solution)/shard_map/ppermute | solution.py:304
  88.5 5.7 %collective-permute-start.8 = (bf16[32,16,128]{2,1,0:T(8,128)(2,1)S(1)}, bf16[32,16,128]{2,1,0:T(8,128)(2,1)S(1)}, u32[]{:S(2)}, u32[]{:S(2)}) collective-permute-start(bf16[32,16,128]{2,1,0:T(8,128)(2,1)S(1)} %all_to_all.17.in_ref), channel_id=1, source_target_pairs={{0,1},{1,0},{2,3},{3,2},{4,5},{5,4},{6,7},{7,6},{8,9},{9,8},{10,11... | collective-permute-start | bytes 393224 | tf_op jit(solution)/shard_map/ppermute | solution.py:294
